TPU v7x, 32 devices: a whole 2x2x4 slice. The times are simulated.
32 devices in a mesh: grp: 2 (over x), px: 4 (over y, core), pz: 4 (over z).
Axes of the slice: x: 2, y: 2, z: 4, core: 2. Of those that a mesh axis runs over, the one named last changes fastest.
Arguments:
- cell_index: int32 [1024, 512], P(('px', 'pz')), may hold values from 0 to 255
- block_index: int32 [1024], P(('px', 'pz')), may hold values from 0 to 255
- volume: float32 [1024, 512], P(('px', 'pz')), may hold values from 0.2 to 2
- response_rate: float32 [1024, 512], P(('px', 'pz')), may hold values from 0.2 to 2
- spanwise_position: float32 [1024, 512], P(('px', 'pz')), may hold values from -3.140625 to 3.140625
- particle_velocity: float32 [3, 1024, 512], P(None, ('px', 'pz')), may hold values from -6 to 6
- seen_velocity: float32 [3, 1024, 512], P(None, ('px', 'pz')), may hold values from -6 to 6
- fluid_velocity: float32 [512, 3, 8, 2, 1024], P(None, None, ('grp', 'pz'), None, 'px'), may hold values from -6 to 6
- eigen_basis: float32 [512, 512], replicated, may hold values from -1 to 2, as said below
- eigen_inverse: float32 [512, 512], replicated, may hold values from -8 to 8, as said below
- eigenvalues: float32 [512], replicated, may hold values from 1 to 100000
Outputs:
- velocity_planes: bfloat16 [512, 3, 8, 2, 2048], P(('px', 'pz'), None, 'grp')
- updated_velocity: float32 [3, 1024, 512], P(None, ('px', 'pz'))
Inputs may be any that keep to these rules, and one draw needn't show every extreme that they name: eigen_inverse is the inverse of eigen_basis. eigen_basis has a dominant unit diagonal.
All inputs are finite; a program needn't handle non-finite values.
Results may differ from a plain program's by a relative error of at most 0.007.
Values may be sent and summed in bfloat16 or wider, within the bound.
No kernel may reach another device: no remote copies, remote signals or barrier semaphores. Data moves between devices by JAX's collectives and lax.ppermute only.
A program may use at most 128 MiB of HBM per device.

v0:
```python
import functools
import math

import jax
import jax.numpy as jnp
import numpy as np
from jax import lax
from jax.experimental import pallas as pl
from jax.experimental.pallas import tpu as pltpu
from jax.sharding import PartitionSpec as P

NX = 2048
KX = 1024
CB = 256
HALF = NX // 2
PAIR = KX // 2

time_step = 0.5
gravity = 0.8
viscosity = 0.0001


def turns(rows, columns):
    phase = np.mod(np.asarray(rows)[:, None] * np.asarray(columns)[None, :], NX)
    angles = phase.astype(np.float64) * (2.0 * math.pi / NX)
    return np.cos(angles).astype(np.float32), np.sin(angles).astype(np.float32)


def forward_seeds():
    waves = np.concatenate([2 * np.arange(PAIR) - KX // 2, 2 * np.arange(PAIR) + 1 - KX // 2])
    base = turns(np.arange(8), waves)
    steps = turns(8 * 2 ** np.arange(8), waves)
    scale = np.float32(1.0 / math.sqrt(NX))
    return [base[0] * scale, base[1] * scale, steps[0], steps[1]]


def inverse_seeds():
    points = np.arange(HALF)
    bases = [turns(2 * np.arange(8) + parity - KX // 2, points) for parity in range(2)]
    steps = turns(16 * 2 ** np.arange(8), points)
    scale = np.float32(1.0 / math.sqrt(NX))
    cosines = np.stack([b[0] for b in bases]) * scale
    sines = np.stack([b[1] for b in bases]) * scale
    return [cosines, sines, steps[0], steps[1]]


def order_matrix():
    matrix = np.zeros((256, 256), np.float32)
    natural = np.arange(256)
    matrix[(natural % 2) * 128 + natural // 2, natural] = 1.0
    return matrix


def grow(cos_ref, sin_ref, base, steps, rows):
    cos_ref[0:8, :] = base[0]
    sin_ref[0:8, :] = base[1]
    done = 8
    level = 0
    while done < rows:
        turn_cos = steps[0][level : level + 1, :]
        turn_sin = steps[1][level : level + 1, :]

        def block(index, carry, done=done, turn_cos=turn_cos, turn_sin=turn_sin):
            start = pl.multiple_of(index * 8, 8)
            old_cos = cos_ref[pl.ds(start, 8), :]
            old_sin = sin_ref[pl.ds(start, 8), :]
            cos_ref[pl.ds(done + start, 8), :] = old_cos * turn_cos - old_sin * turn_sin
            sin_ref[pl.ds(done + start, 8), :] = old_sin * turn_cos + old_cos * turn_sin
            return carry

        lax.fori_loop(0, done // 8, block, 0)
        done *= 2
        level += 1


def spread_kernel(
    block_ref,
    group_ref,
    cell_ref,
    volume_ref,
    rate_ref,
    place_ref,
    motion_ref,
    seen_ref,
    base_cos_ref,
    base_sin_ref,
    step_cos_ref,
    step_sin_ref,
    order_ref,
    out_ref,
    phase_ref,
    field,
    table_cos,
    table_sin,
    table,
    left,
    *,
    half_modes,
    pencil_modes,
    pencil_waves,
):
    tiles, size = cell_ref.shape
    strips = NX // CB
    group_rows = 2 * half_modes
    width = 3 * group_rows
    slab_rows = field.shape[1] // width

    place = place_ref[...]
    first = (group_ref[0] * half_modes + 1).astype(jnp.float32)
    cos_one = jnp.cos(place)
    sin_one = jnp.sin(place)
    cos_now = jnp.cos(place * first)
    sin_now = jnp.sin(place * first)
    for mode in range(half_modes):
        for piece in range(size // 128):
            lanes = slice(piece * 128, (piece + 1) * 128)
            spot = pl.ds(mode, tiles, stride=group_rows)
            phase_ref[piece, spot, :] = cos_now[:, lanes]
            spot = pl.ds(half_modes + mode, tiles, stride=group_rows)
            phase_ref[piece, spot, :] = -sin_now[:, lanes]
        if mode + 1 < half_modes:
            cos_now, sin_now = (
                cos_now * cos_one - sin_now * sin_one,
                sin_now * cos_one + cos_now * sin_one,
            )

    grow(
        table_cos,
        table_sin,
        (base_cos_ref[...], base_sin_ref[...]),
        (step_cos_ref, step_sin_ref),
        HALF,
    )
    for parity in range(2):
        lanes = slice(parity * PAIR, (parity + 1) * PAIR)
        table[parity, 0:HALF, :] = table_cos[:, lanes].astype(jnp.bfloat16)
        table[parity, HALF:NX, :] = table_sin[:, lanes].astype(jnp.bfloat16)

    def clear(index, carry):
        field[index] = jnp.zeros(field.shape[1:], jnp.float32)
        return carry

    lax.fori_loop(0, field.shape[0], clear, 0)

    cells = lax.broadcasted_iota(jnp.int32, (CB, size), 0)

    def tile_step(tile, carry):
        row = pl.ds(tile, 1)
        volume = volume_ref[row, :]
        pull = volume * rate_ref[row, :]
        first_row = pl.ds(pl.multiple_of(tile * group_rows, 8), group_rows)
        phases = jnp.concatenate(
            [phase_ref[piece, first_row, :] for piece in range(size // 128)], axis=1
        )
        rows = []
        for component in range(3):
            amount = pull * (seen_ref[component, row, :] - motion_ref[component, row, :])
            if component == 1:
                amount = amount - gravity * volume
            rows.append(amount * phases)
        payload = jnp.concatenate(rows, axis=0).astype(jnp.bfloat16)
        one_hot = (cell_ref[row, :] == cells).astype(jnp.float32).astype(jnp.bfloat16)
        shares = lax.dot_general(
            payload, one_hot, (((1,), (1,)), ((), ())), preferred_element_type=jnp.float32
        )
        block = block_ref[tile]
        strip = block % strips
        start = pl.multiple_of((block // strips) * width, 8)
        for half in range(2):
            field[strip * 2 + half, pl.ds(start, width), :] += shares[
                :, half * 128 : (half + 1) * 128
            ]
        return carry

    lax.fori_loop(0, tiles, tile_step, 0, unroll=2)

    order = order_ref[...]
    for component in range(3):
        products = []
        for parity in range(2):
            sign = 1.0 - 2.0 * parity
            for part in range(2):
                for mode in range(half_modes):
                    column = (component * 2 + part) * half_modes + mode
                    other = (component * 2 + 1 - part) * half_modes + mode
                    rows = pl.ds(column, slab_rows, stride=width)
                    other_row = ((1 - part) * half_modes + mode) * slab_rows
                    own_row = (part * half_modes + mode) * slab_rows
                    for strip in range(HALF // 128):
                        low = field[strip, rows, :]
                        high = field[strip + HALF // 128, rows, :]
                        value = low + high if parity == 0 else low - high
                        lanes = slice(strip * 128, (strip + 1) * 128)
                        left[own_row : own_row + slab_rows, lanes] = value.astype(jnp.bfloat16)
                        turned = value if part == 1 else -value
                        lanes = slice(HALF + strip * 128, HALF + (strip + 1) * 128)
                        left[other_row : other_row + slab_rows, lanes] = turned.astype(jnp.bfloat16)
            products.append(
                jnp.dot(left[...], table[parity], preferred_element_type=jnp.float32).astype(
                    jnp.bfloat16
                )
            )
        for block in range(PAIR // 128):
            lanes = slice(block * 128, (block + 1) * 128)
            mixed = jnp.concatenate([products[0][:, lanes], products[1][:, lanes]], axis=1)
            natural = jnp.dot(mixed, order, preferred_element_type=jnp.float32).astype(jnp.bfloat16)
            for piece in range(256 // min(256, pencil_waves)):
                span = min(256, pencil_waves)
                wave = block * 256 + piece * span
                owner_px = wave // pencil_waves
                inside = wave % pencil_waves
                for part in range(2):
                    for mode in range(half_modes):
                        owner_pz = mode // pencil_modes
                        column = (
                            (component * pencil_modes + mode % pencil_modes) * 2 + part
                        ) * pencil_waves + inside
                        row = (part * half_modes + mode) * slab_rows
                        out_ref[
                            owner_px * (half_modes // pencil_modes) + owner_pz,
                            :,
                            column : column + span,
                        ] = natural[row : row + slab_rows, piece * span : (piece + 1) * span]


def table_kernel(base_cos_ref, base_sin_ref, step_cos_ref, step_sin_ref, out_ref, work_cos, work_sin):
    for parity in range(2):
        grow(
            work_cos,
            work_sin,
            (base_cos_ref[parity], base_sin_ref[parity]),
            (step_cos_ref, step_sin_ref),
            PAIR,
        )
        out_ref[parity, 0:PAIR, :] = work_cos[...].astype(jnp.bfloat16)
        out_ref[parity, PAIR:KX, :] = work_sin[...].astype(jnp.bfloat16)


def split(value):
    high = value.astype(jnp.bfloat16)
    return high, (value - high.astype(jnp.float32)).astype(jnp.bfloat16)


def dot32(a, b):
    return jnp.dot(a, b, preferred_element_type=jnp.float32)


def project_kernel(high_ref, low_ref, state_ref, out_ref):
    state_high, state_low = split(state_ref[...])
    out_ref[...] = (
        dot32(high_ref[...], state_high)
        + dot32(high_ref[...], state_low)
        + dot32(low_ref[...], state_high)
    )


def solve_kernel(
    inverse_high, inverse_low, basis_high, basis_low, damping_ref, state_ref, force_ref, out_ref
):
    force = force_ref[...]
    modal = state_ref[...] + time_step * (
        dot32(inverse_high[...], force) + dot32(inverse_low[...], force)
    )
    modal_high, modal_low = split(modal * damping_ref[...])
    solved = (
        dot32(basis_high[...], modal_high)
        + dot32(basis_high[...], modal_low)
        + dot32(basis_low[...], modal_high)
    )
    out_ref[...] = solved.astype(jnp.bfloat16)


def gather_kernel(
    block_ref,
    cell_ref,
    phase_ref,
    table_ref,
    order_ref,
    back_ref,
    planes_ref,
    part_ref,
    left,
    values,
    sampled,
    *,
    half_modes,
    pencil_modes,
    pencil_waves,
):
    tiles, size = cell_ref.shape
    strips = NX // CB
    group_rows = 2 * half_modes
    slab_rows = back_ref.shape[1]
    pz_count = half_modes // pencil_modes
    order = order_ref[...]
    component_rows = group_rows * slab_rows
    for component in range(3):
        for block in range(KX // 256):
            rows = []
            for part in range(2):
                for mode in range(half_modes):
                    pieces = []
                    span = min(256, pencil_waves)
                    for piece in range(256 // span):
                        wave = block * 256 + piece * span
                        column = (
                            (component * pencil_modes + mode % pencil_modes) * 2 + part
                        ) * pencil_waves + wave % pencil_waves
                        source = (wave // pencil_waves) * pz_count + mode // pencil_modes
                        pieces.append(back_ref[source, :, column : column + span])
                    rows.append(pieces[0] if len(pieces) == 1 else jnp.concatenate(pieces, axis=1))
            natural = jnp.concatenate(rows, axis=0)
            mixed = lax.dot_general(
                natural, order, (((1,), (1,)), ((), ())), preferred_element_type=jnp.float32
            )
            half_rows = half_modes * slab_rows
            real = mixed[:half_rows]
            imag = mixed[half_rows:]
            for parity in range(2):
                lanes = slice(parity * 128, (parity + 1) * 128)
                first = slice(block * 128, (block + 1) * 128)
                second = slice(PAIR + block * 128, PAIR + (block + 1) * 128)
                left[parity, 0:half_rows, first] = real[:, lanes].astype(jnp.bfloat16)
                left[parity, 0:half_rows, second] = (-imag[:, lanes]).astype(jnp.bfloat16)
                left[parity, half_rows:, first] = imag[:, lanes].astype(jnp.bfloat16)
                left[parity, half_rows:, second] = real[:, lanes].astype(jnp.bfloat16)
        even = dot32(left[0], table_ref[0])
        odd = dot32(left[1], table_ref[1])
        for side in range(2):
            plane = (even + odd if side == 0 else even - odd).astype(jnp.bfloat16)
            whole = plane.astype(jnp.float32)
            for mode in range(half_modes):
                for part in range(2):
                    row = (part * half_modes + mode) * slab_rows
                    planes_ref[component, mode, part, :, side * HALF : (side + 1) * HALF] = plane[
                        row : row + slab_rows
                    ]
            for strip in range(HALF // 128):
                values[
                    side * (HALF // 128) + strip,
                    component * component_rows : (component + 1) * component_rows,
                    :,
                ] = whole[:, strip * 128 : (strip + 1) * 128]

    def tile_step(tile, carry):
        block = block_ref[tile]
        strip = block % strips
        y = block // strips
        cell = jnp.broadcast_to(cell_ref[pl.ds(tile, 1), :], (group_rows, size))
        spot = cell % 128
        upper = cell >= 128
        first_row = pl.ds(pl.multiple_of(tile * group_rows, 8), group_rows)
        for component in range(3):
            rows = pl.ds(component * component_rows + y, group_rows, stride=slab_rows)
            left_half = values[strip * 2, rows, :]
            right_half = values[strip * 2 + 1, rows, :]
            pieces = []
            for piece in range(size // 128):
                lanes = slice(piece * 128, (piece + 1) * 128)
                low = jnp.take_along_axis(left_half, spot[:, lanes], axis=1)
                high = jnp.take_along_axis(right_half, spot[:, lanes], axis=1)
                picked = jnp.where(upper[:, lanes], high, low)
                pieces.append(
                    jnp.sum(picked * phase_ref[piece, first_row, :], axis=0, keepdims=True)
                )
            sampled[component, pl.ds(tile, 1), :] = jnp.concatenate(pieces, axis=1)
        return carry

    lax.fori_loop(0, tiles, tile_step, 0, unroll=2)
    part_ref[...] = sampled[...].astype(jnp.bfloat16)


def on_device(
    cell_index,
    block_index,
    volume,
    response_rate,
    spanwise_position,
    particle_velocity,
    seen_velocity,
    fluid_velocity,
    eigen_basis,
    eigen_inverse,
    eigenvalues,
):
    group_index = lax.axis_index("grp")
    px_count = lax.axis_size("px")
    pz_count = lax.axis_size("pz")
    rows = fluid_velocity.shape[0]
    pencil_modes = fluid_velocity.shape[2]
    pencil_waves = fluid_velocity.shape[4]
    half_modes = pencil_modes * pz_count
    slabs = px_count * pz_count
    slab_rows = rows // slabs
    strips = NX // CB
    tiles, size = cell_index.shape
    width = 6 * half_modes
    columns = 6 * pencil_modes * pencil_waves
    sizes = dict(half_modes=half_modes, pencil_modes=pencil_modes, pencil_waves=pencil_waves)

    vmem = pl.BlockSpec(memory_space=pltpu.VMEM)
    smem = pl.BlockSpec(memory_space=pltpu.SMEM)
    order = jnp.asarray(order_matrix(), jnp.bfloat16)

    outgoing, phases = pl.pallas_call(
        functools.partial(spread_kernel, **sizes),
        out_shape=(
            jax.ShapeDtypeStruct((slabs, slab_rows, columns), jnp.bfloat16),
            jax.ShapeDtypeStruct((size // 128, tiles * 2 * half_modes, 128), jnp.float32),
        ),
        in_specs=[smem, smem] + [vmem] * 11,
        out_specs=(vmem, vmem),
        scratch_shapes=[
            pltpu.VMEM((NX // 128, slab_rows * width, 128), jnp.float32),
            pltpu.VMEM((HALF, KX), jnp.float32),
            pltpu.VMEM((HALF, KX), jnp.float32),
            pltpu.VMEM((2, NX, PAIR), jnp.bfloat16),
            pltpu.VMEM((2 * half_modes * slab_rows, NX), jnp.bfloat16),
        ],
        name="spread",
    )(
        block_index,
        group_index.reshape(1).astype(jnp.int32),
        cell_index,
        volume,
        response_rate,
        spanwise_position,
        particle_velocity,
        seen_velocity,
        *[jnp.asarray(seed) for seed in forward_seeds()],
        order,
    )
    force = lax.all_to_all(outgoing, ("px", "pz"), split_axis=0, concat_axis=0, tiled=True)
    force = force.reshape(rows, columns)

    def halves(matrix):
        high = lax.reduce_precision(matrix, 8, 7)
        return high.astype(jnp.bfloat16), (matrix - high).astype(jnp.bfloat16)

    inverse_high, inverse_low = halves(eigen_inverse)
    basis_high, basis_low = halves(eigen_basis)
    state = jnp.transpose(fluid_velocity, (0, 1, 2, 3, 4)).reshape(rows, columns)
    square = pl.BlockSpec((rows, rows), lambda i: (0, 0))
    strip_spec = pl.BlockSpec((rows, pencil_waves), lambda i: (0, i))
    steps = columns // pencil_waves
    projected = pl.pallas_call(
        project_kernel,
        grid=(steps,),
        out_shape=jax.ShapeDtypeStruct((rows, columns), jnp.float32),
        in_specs=[square, square, strip_spec],
        out_specs=strip_spec,
        name="project",
    )(inverse_high, inverse_low, state)
    stream_wave = (lax.axis_index("px") * pencil_waves + jnp.arange(pencil_waves) - KX // 2).astype(
        jnp.float32
    ) * 0.5
    span_wave = (
        group_index * half_modes
        + lax.axis_index("pz") * pencil_modes
        + jnp.arange(pencil_modes)
        + 1
    ).astype(jnp.float32)
    wave_square = (
        stream_wave[None, :] * stream_wave[None, :] + span_wave[:, None] * span_wave[:, None]
    ).reshape(1, pencil_modes * pencil_waves)
    damping = 1.0 / (1.0 + viscosity * (eigenvalues[:, None] + wave_square))
    table = pl.pallas_call(
        table_kernel,
        out_shape=jax.ShapeDtypeStruct((2, KX, HALF), jnp.bfloat16),
        in_specs=[vmem] * 4,
        out_specs=vmem,
        scratch_shapes=[pltpu.VMEM((PAIR, HALF), jnp.float32)] * 2,
        name="waves",
    )(*[jnp.asarray(seed) for seed in inverse_seeds()])

    solved = pl.pallas_call(
        solve_kernel,
        grid=(steps,),
        out_shape=jax.ShapeDtypeStruct((rows, columns), jnp.bfloat16),
        in_specs=[
            square,
            square,
            square,
            square,
            pl.BlockSpec((rows, pencil_waves), lambda i: (0, (i // 2) % pencil_modes)),
            strip_spec,
            strip_spec,
        ],
        out_specs=strip_spec,
        name="solve",
    )(inverse_high, inverse_low, basis_high, basis_low, damping, projected, force)
    returned = lax.all_to_all(
        solved.reshape(slabs, slab_rows, columns),
        ("px", "pz"),
        split_axis=0,
        concat_axis=0,
        tiled=True,
    )
    planes, mode_part = pl.pallas_call(
        functools.partial(gather_kernel, **sizes),
        out_shape=(
            jax.ShapeDtypeStruct((3, half_modes, 2, slab_rows, NX), jnp.bfloat16),
            jax.ShapeDtypeStruct((3, tiles, size), jnp.bfloat16),
        ),
        in_specs=[smem] + [vmem] * 5,
        out_specs=(vmem, vmem),
        scratch_shapes=[
            pltpu.VMEM((2, 2 * half_modes * slab_rows, KX), jnp.bfloat16),
            pltpu.VMEM((NX // 128, slab_rows * width, 128), jnp.float32),
            pltpu.VMEM((3, tiles, size), jnp.float32),
        ],
        name="gather",
    )(block_index, cell_index, phases, table, order, returned)
    velocity_planes = jnp.transpose(planes, (3, 0, 1, 2, 4))
    other_part = lax.ppermute(mode_part, "grp", [(0, 1), (1, 0)])
    fluid_at = mode_part.astype(jnp.float32) + other_part.astype(jnp.float32)
    upward = (jnp.arange(3) == 1).astype(jnp.float32)[:, None, None]
    updated_velocity = (
        particle_velocity
        + time_step * response_rate * (fluid_at - particle_velocity)
        - time_step * gravity * upward
    )
    return (velocity_planes, updated_velocity)


def solution(mesh):
    in_specs = (
        P(("px", "pz"), None),
        P(("px", "pz")),
        P(("px", "pz"), None),
        P(("px", "pz"), None),
        P(("px", "pz"), None),
        P(None, ("px", "pz"), None),
        P(None, ("px", "pz"), None),
        P(None, None, ("grp", "pz"), None, "px"),
        P(),
        P(),
        P(),
    )
    out_specs = (P(("px", "pz"), None, "grp", None, None), P(None, ("px", "pz"), None))
    return jax.shard_map(
        on_device, mesh=mesh, in_specs=in_specs, out_specs=out_specs, check_vma=False
    )
```

profile of v0, /device:TPU:0, one launch (start us, length us, event | category | flops | bytes accessed | tf_op | source)
XLA Modules:
  0.0 148.1 jit_solution(279493269634622261)
XLA Ops:
  0.6 21.0 %spread.1 = (bf16[16,32,1536]{2,1,0:T(8,128)(2,1)}, f32[4,512,128]{2,1,0:T(8,128)}) custom-call(s32[64]{0:T(128)} %block_ref.3, s32[1]{0:T(128)} %bitcast.group_ref, s32[64,512]{1,0:T(8,128)} %cell_ref.3, f32[64,512]{1,0:T(8,128)} %volume_ref.1, f32[64,512]{1,0:T(8,128)} %rate_ref.1, f32[64,512]{1,0:T(8,128)} %place_ref.1, f32[3,64,512]{2,1,0:T(8,128)} %motion_ref.1, ...), custom_call_target="tpu_custom_call" | custom-call | tf_op jit(solution)/shard_map/spread/pallas_call | solution.py:405
  21.6 7.4 %all-to-all-start = ((bf16[16,32,1536]{2,1,0:T(8,128)(2,1)}), bf16[16,32,1536]{2,1,0:T(8,128)(2,1)S(1)}, u32[]{:S(2)}, u32[]{:S(2)}) async-start(bf16[16,32,1536]{2,1,0:T(8,128)(2,1)} %get-tuple-element.7), calls=%async_computation | async-start | bytes 3145728 | tf_op jit(solution)/shard_map/all_to_all | solution.py:433
  29.0 0.0 copy-start.3
  29.1 5.6 %reshape.45.state_ref = f32[512,1536]{1,0:T(8,128)} reshape(f32[512,3,1,2,256]{4,3,2,1,0:T(2,128)} %param.27) | data formatting | bytes 6291456 | tf_op jit(solution)/shard_map/reshape | solution.py:442
  34.6 0.0 copy-done.3
  34.6 2.8 %fusion = (bf16[512,512]{1,0:T(8,128)(2,1)}, bf16[512,512]{1,0:T(8,128)(2,1)}, bf16[512,512]{1,0:T(8,128)(2,1)}, bf16[512,512]{1,0:T(8,128)(2,1)}) fusion(f32[512,512]{1,0:T(8,128)S(1)} %copy-done.3, f32[512,512]{1,0:T(8,128)} %param.28), kind=kLoop, calls=%fused_computation.4 | loop fusion | flops 2097152 | bytes 4194304 | tf_op jit(solution)/shard_map/convert_element_type | solution.py:438
  37.4 0.0 copy-start.6
  37.4 7.2 %project.1.state_ref = f32[512,1536]{1,0:T(8,128)} custom-call(bf16[512,512]{1,0:T(8,128)(2,1)} %get-tuple-element.15.high_ref.inverse_high, bf16[512,512]{1,0:T(8,128)(2,1)} %get-tuple-element.14.low_ref.inverse_low, f32[512,1536]{1,0:T(8,128)} %reshape.45.state_ref), custom_call_target="tpu_custom_call" | custom-call | tf_op jit(solution)/shard_map/project/pallas_call | solution.py:446
  44.6 0.0 copy-done.6
  44.6 1.0 add_divide_fusion.damping_ref
  45.6 21.5 %all-to-all-done = bf16[16,32,1536]{2,1,0:T(8,128)(2,1)S(1)} async-done(((bf16[16,32,1536]{2,1,0:T(8,128)(2,1)}), bf16[16,32,1536]{2,1,0:T(8,128)(2,1)S(1)}, u32[]{:S(2)}, u32[]{:S(2)}) %all-to-all-start) | async-done | bytes 1572896 | tf_op jit(solution)/shard_map/all_to_all | solution.py:433
  67.1 0.0 copy-start.1
  67.1 1.1 copy-done.1
  68.3 11.8 %solve.1 = bf16[512,1536]{1,0:T(8,128)(2,1)} custom-call(bf16[512,512]{1,0:T(8,128)(2,1)} %get-tuple-element.15.high_ref.inverse_high, bf16[512,512]{1,0:T(8,128)(2,1)} %get-tuple-element.14.low_ref.inverse_low, bf16[512,512]{1,0:T(8,128)(2,1)} %get-tuple-element.16.basis_high, bf16[512,512]{1,0:T(8,128)(2,1)} %get-tuple-element.17.basis_low, ...), custom_call_target="tpu_custom_call" | custom-call | tf_op jit(solution)/shard_map/solve/pallas_call | solution.py:476
  80.1 3.9 %all-to-all-start.1 = ((bf16[16,32,1536]{2,1,0:T(8,128)(2,1)}), bf16[16,32,1536]{2,1,0:T(8,128)(2,1)S(1)}, u32[]{:S(2)}, u32[]{:S(2)}) async-start(bf16[16,32,1536]{2,1,0:T(8,128)(2,1)} %bitcast.5), calls=%async_computation.1 | async-start | bytes 3145728 | tf_op jit(solution)/shard_map/all_to_all | solution.py:492
  84.0 4.8 %waves.1.table_ref = bf16[2,1024,1024]{2,1,0:T(8,128)(2,1)} custom-call(f32[2,8,1024]{2,1,0:T(8,128)} %constant.58.clone.base_cos_ref, f32[2,8,1024]{2,1,0:T(8,128)} %constant.59.clone.base_sin_ref, f32[8,1024]{1,0:T(8,128)} %constant.60.clone.step_cos_ref, f32[8,1024]{1,0:T(8,128)} %constant.61.clone.step_sin_ref), custom_call_target="tpu_custom_call" | custom-call | tf_op jit(solution)/shard_map/waves/pallas_call | solution.py:467
  88.8 33.0 %all-to-all-done.1.back_ref = bf16[16,32,1536]{2,1,0:T(8,128)(2,1)S(1)} async-done(((bf16[16,32,1536]{2,1,0:T(8,128)(2,1)}), bf16[16,32,1536]{2,1,0:T(8,128)(2,1)S(1)}, u32[]{:S(2)}, u32[]{:S(2)}) %all-to-all-start.1) | async-done | bytes 1572896 | tf_op jit(solution)/shard_map/all_to_all | solution.py:492
  121.9 0.0 copy-start
  121.9 1.1 copy-done
  123.0 0.0 copy-start.4
  123.0 15.8 %gather.1 = (bf16[3,4,2,32,2048]{4,3,2,1,0:T(8,128)(2,1)}, bf16[3,64,512]{2,1,0:T(8,128)(2,1)}) custom-call(s32[64]{0:T(128)} %block_ref.3, s32[64,512]{1,0:T(8,128)} %cell_ref.3, f32[4,512,128]{2,1,0:T(8,128)} %get-tuple-element.6.phase_ref, bf16[2,1024,1024]{2,1,0:T(8,128)(2,1)} %waves.1.table_ref, bf16[256,256]{1,0:T(8,128)(2,1)} %constant.53.clone.order_ref, ...), custom_call_target="tpu_custom_call" | custom-call | tf_op jit(solution)/shard_map/gather/pallas_call | solution.py:499
  138.8 1.5 %collective-permute-start = (bf16[3,64,512]{2,1,0:T(8,128)(2,1)}, bf16[3,64,512]{2,1,0:T(8,128)(2,1)S(1)}, u32[]{:S(2)}, u32[]{:S(2)}) collective-permute-start(bf16[3,64,512]{2,1,0:T(8,128)(2,1)} %get-tuple-element.9), channel_id=1, source_target_pairs={{0,16},{16,0},{1,17},{17,1},{2,18},{18,2},{3,19},{19,3},{4,20},{20... | collective-permute-start | bytes 589832 | tf_op jit(solution)/shard_map/ppermute | solution.py:515
  140.3 0.0 copy-done.4
  140.3 0.0 copy-start.2
  140.3 0.0 copy-start.5
  140.3 6.9 %copy.22 = bf16[32,3,4,2,2048]{4,3,2,1,0:T(2,128)(2,1)} copy(bf16[32,3,4,2,2048]{4,0,3,2,1:T(8,128)(2,1)} %bitcast.6) | data formatting | bytes 6291456
  147.2 0.0 collective-permute-done
  147.2 0.0 copy-done.2
  147.2 0.0 copy-done.5
  147.2 0.9 add_subtract_fusion
  (3 shorter events, 0.0 us)
Async XLA Ops:
  21.6 45.5 %all-to-all-start = ((bf16[16,32,1536]{2,1,0:T(8,128)(2,1)}), bf16[16,32,1536]{2,1,0:T(8,128)(2,1)S(1)}, u32[]{:S(2)}, u32[]{:S(2)}) async-start(bf16[16,32,1536]{2,1,0:T(8,128)(2,1)} %get-tuple-element.7), calls=%async_computation | async-start | bytes 3145728 | tf_op jit(solution)/shard_map/all_to_all | solution.py:433
  29.0 5.6 %copy-start.3 = (f32[512,512]{1,0:T(8,128)S(1)}, f32[512,512]{1,0:T(8,128)}, u32[]{:S(2)}) copy-start(f32[512,512]{1,0:T(8,128)} %param.29) | copy-start | bytes 3145732
  37.4 7.2 %copy-start.6 = (f32[512]{0:T(512)S(1)}, f32[512]{0:T(512)}, u32[]{:S(2)}) copy-start(f32[512]{0:T(512)} %param.30) | copy-start | bytes 6148
  67.1 1.1 copy-start.1
  80.1 41.8 %all-to-all-start.1 = ((bf16[16,32,1536]{2,1,0:T(8,128)(2,1)}), bf16[16,32,1536]{2,1,0:T(8,128)(2,1)S(1)}, u32[]{:S(2)}, u32[]{:S(2)}) async-start(bf16[16,32,1536]{2,1,0:T(8,128)(2,1)} %bitcast.5), calls=%async_computation.1 | async-start | bytes 3145728 | tf_op jit(solution)/shard_map/all_to_all | solution.py:492
  121.9 1.1 copy-start
  123.0 17.3 %copy-start.4 = (f32[64,512]{1,0:T(8,128)S(1)}, f32[64,512]{1,0:T(8,128)}, u32[]{:S(2)}) copy-start(f32[64,512]{1,0:T(8,128)} %rate_ref.1) | copy-start | bytes 393220
  138.8 8.4 %collective-permute-start = (bf16[3,64,512]{2,1,0:T(8,128)(2,1)}, bf16[3,64,512]{2,1,0:T(8,128)(2,1)S(1)}, u32[]{:S(2)}, u32[]{:S(2)}) collective-permute-start(bf16[3,64,512]{2,1,0:T(8,128)(2,1)} %get-tuple-element.9), channel_id=1, source_target_pairs={{0,16},{16,0},{1,17},{17,1},{2,18},{18,2},{3,19},{19,3},{4,20},{20... | collective-permute-start | bytes 589832 | tf_op jit(solution)/shard_map/ppermute | solution.py:515
  140.3 6.9 %copy-start.2 = (f32[3,64,512]{2,1,0:T(8,128)S(1)}, f32[3,64,512]{2,1,0:T(8,128)}, u32[]{:S(2)}) copy-start(f32[3,64,512]{2,1,0:T(8,128)} %motion_ref.1) | copy-start | bytes 1179652
  140.3 6.9 %copy-start.5 = (bf16[3,64,512]{2,1,0:T(8,128)(2,1)S(1)}, bf16[3,64,512]{2,1,0:T(8,128)(2,1)}, u32[]{:S(2)}) copy-start(bf16[3,64,512]{2,1,0:T(8,128)(2,1)} %get-tuple-element.9) | copy-start | bytes 589828
where the time goes:
time: 149 us; the launch traced here: 148 us
  Pallas kernels  60.6 us (41%)
  waiting for transfers between devices  54.6 us (37%)
  local copies, waits for them, and re-layouts  14.7 us (10%)
  starting transfers between devices  12.8 us (9%)
  other arithmetic  4.68 us (3%)
    all_to_all x1, waiting for transfers between devices, on_device(): lax.all_to_all(solved.reshape(slabs, slab_rows, columns), ('px', 'pz'), s...  33 us
    all_to_all x1, waiting for transfers between devices, on_device(): lax.all_to_all(outgoing, ('px', 'pz'), split_axis=0, concat_axis=0, tiled...  21.5 us
    pallas_call x1, Pallas kernels, on_device(): pl.pallas_call(functools.partial(spread_kernel, **sizes), out_shape=(jax....  21 us
    pallas_call x1, Pallas kernels, on_device(): pl.pallas_call(functools.partial(gather_kernel, **sizes), out_shape=(jax....  15.8 us
    pallas_call x1, Pallas kernels, on_device(): pl.pallas_call(solve_kernel, grid=(steps,), out_shape=jax.ShapeDtypeStruc...  11.8 us
    unnamed x15, local copies, waits for them, and re-layouts  9.2 us
    all_to_all x1, starting transfers between devices, on_device(): lax.all_to_all(outgoing, ('px', 'pz'), split_axis=0, concat_axis=0, tiled...  7.41 us
    pallas_call x1, Pallas kernels, on_device(): pl.pallas_call(project_kernel, grid=(steps,), out_shape=jax.ShapeDtypeStr...  7.19 us
  transfers between devices with their start and end apart: 3, of which 2 were waited for; matrix products, arithmetic and copies ran while one was open for 11% of the time, Pallas kernels for 8%

commit v1 on v0

v1 whole, which is shorter than its diff:
```python
import functools
import math

import jax
import jax.numpy as jnp
import numpy as np
from jax import lax
from jax.experimental import pallas as pl
from jax.experimental.pallas import tpu as pltpu
from jax.sharding import PartitionSpec as P

NX = 2048
KX = 1024
CB = 256
HALF = NX // 2
PAIR = KX // 2
TILE_GROUP = 8

time_step = 0.5
gravity = 0.8
viscosity = 0.0001


def turns(rows, columns):
    phase = np.mod(np.asarray(rows)[:, None] * np.asarray(columns)[None, :], NX)
    angles = phase.astype(np.float64) * (2.0 * math.pi / NX)
    return np.cos(angles).astype(np.float32), np.sin(angles).astype(np.float32)


def forward_seeds():
    waves = np.concatenate([2 * np.arange(PAIR) - KX // 2, 2 * np.arange(PAIR) + 1 - KX // 2])
    base = turns(np.arange(8), waves)
    steps = turns(8 * 2 ** np.arange(8), waves)
    scale = np.float32(1.0 / math.sqrt(NX))
    return [base[0] * scale, base[1] * scale, steps[0], steps[1]]


def inverse_seeds():
    points = np.arange(HALF)
    bases = [turns(2 * np.arange(8) + parity - KX // 2, points) for parity in range(2)]
    steps = turns(16 * 2 ** np.arange(8), points)
    scale = np.float32(1.0 / math.sqrt(NX))
    cosines = np.stack([b[0] for b in bases]) * scale
    sines = np.stack([b[1] for b in bases]) * scale
    return [cosines, sines, steps[0], steps[1]]


def order_matrix(waves):
    matrix = np.zeros((waves, waves), np.float32)
    lanes = np.arange(waves)
    half = waves // 2
    matrix[2 * (lanes % half) + lanes // half, lanes] = 1.0
    return matrix


def spread_rows(half_modes, slab_rows):
    part, mode, y = np.meshgrid(
        np.arange(2), np.arange(half_modes), np.arange(slab_rows), indexing="ij"
    )
    count = part.size
    matrix = np.zeros((count, count), np.float32)
    source = (y * 2 + part) * half_modes + mode
    matrix[np.arange(count), source.ravel()] = 1.0
    return matrix


def gather_rows(half_modes, slab_rows):
    y, mode, part = np.meshgrid(
        np.arange(slab_rows), np.arange(half_modes), np.arange(2), indexing="ij"
    )
    count = part.size
    matrix = np.zeros((2 * count, count), np.float32)
    source = (part * half_modes + mode) * slab_rows + y
    other = ((1 - part) * half_modes + mode) * slab_rows + y
    matrix[np.arange(count), source.ravel()] = 1.0
    matrix[count + np.arange(count), other.ravel()] = np.where(part.ravel() == 0, -1.0, 1.0)
    return matrix


def grow(cos_ref, sin_ref, base, steps, rows):
    cos_ref[0:8, :] = base[0]
    sin_ref[0:8, :] = base[1]
    done = 8
    level = 0
    while done < rows:
        turn_cos = steps[0][level : level + 1, :]
        turn_sin = steps[1][level : level + 1, :]

        def block(index, carry, done=done, turn_cos=turn_cos, turn_sin=turn_sin):
            start = pl.multiple_of(index * 8, 8)
            old_cos = cos_ref[pl.ds(start, 8), :]
            old_sin = sin_ref[pl.ds(start, 8), :]
            cos_ref[pl.ds(done + start, 8), :] = old_cos * turn_cos - old_sin * turn_sin
            sin_ref[pl.ds(done + start, 8), :] = old_sin * turn_cos + old_cos * turn_sin
            return carry

        lax.fori_loop(0, done // 8, block, 0)
        done *= 2
        level += 1


def dot32(a, b):
    return jnp.dot(a, b, preferred_element_type=jnp.float32)


def spread_kernel(
    block_ref,
    group_ref,
    cell_ref,
    volume_ref,
    rate_ref,
    place_ref,
    motion_ref,
    seen_ref,
    base_cos_ref,
    base_sin_ref,
    step_cos_ref,
    step_sin_ref,
    order_ref,
    out_ref,
    phase_out_ref,
    field,
    table_cos,
    table_sin,
    table,
    left,
    amounts,
    phases,
    phases_out,
    packed,
    phase_sem,
    out_sem,
    *,
    half_modes,
    pencil_modes,
    pencil_waves,
):
    tiles, size = cell_ref.shape
    strips = NX // CB
    group_rows = 2 * half_modes
    slab_rows = field.shape[1] // (3 * group_rows)
    component_rows = slab_rows * group_rows
    pz_count = half_modes // pencil_modes

    place = place_ref[...]
    first = (group_ref[0] * half_modes + 1).astype(jnp.float32)
    cos_one = jnp.cos(place)
    sin_one = jnp.sin(place)
    cos_now = jnp.cos(place * first)
    sin_now = jnp.sin(place * first)
    for mode in range(half_modes):
        for piece in range(size // 128):
            lanes = slice(piece * 128, (piece + 1) * 128)
            for part, value in ((0, cos_now[:, lanes]), (1, -sin_now[:, lanes])):
                phases[piece, pl.ds(part * half_modes + mode, tiles, stride=group_rows), :] = value
                phases_out[piece, pl.ds(2 * mode + part, tiles, stride=group_rows), :] = value
        if mode + 1 < half_modes:
            cos_now, sin_now = (
                cos_now * cos_one - sin_now * sin_one,
                sin_now * cos_one + cos_now * sin_one,
            )
    phase_copy = pltpu.make_async_copy(phases_out, phase_out_ref, phase_sem)
    phase_copy.start()

    upper = cell_ref[...] >= 128
    volume = volume_ref[...]
    pull = volume * rate_ref[...]
    for component in range(3):
        amount = pull * (seen_ref[component] - motion_ref[component])
        if component == 1:
            amount = amount - gravity * volume
        amounts[component] = jnp.where(upper, 0.0, amount)
        amounts[3 + component] = jnp.where(upper, amount, 0.0)

    grow(
        table_cos,
        table_sin,
        (base_cos_ref[...], base_sin_ref[...]),
        (step_cos_ref, step_sin_ref),
        HALF,
    )
    for parity in range(2):
        lanes = slice(parity * PAIR, (parity + 1) * PAIR)
        table[parity, :, 0:PAIR] = table_cos[:, lanes].astype(jnp.bfloat16)
        table[parity, :, PAIR:KX] = table_sin[:, lanes].astype(jnp.bfloat16)

    def clear(index, carry):
        field[index] = jnp.zeros(field.shape[1:], jnp.float32)
        return carry

    lax.fori_loop(0, field.shape[0], clear, 0)

    cells = lax.broadcasted_iota(jnp.int32, (128, size), 0)

    def tile_group(group, carry):
        shares = []
        for offset in range(TILE_GROUP):
            tile = group * TILE_GROUP + offset
            row = pl.ds(tile, 1)
            rows_of_tile = pl.ds(pl.multiple_of(tile * group_rows, 8), group_rows)
            phase = jnp.concatenate(
                [phases[piece, rows_of_tile, :] for piece in range(size // 128)], axis=1
            )
            payload = jnp.concatenate([amounts[k, row, :] * phase for k in range(6)], axis=0)
            spot = cell_ref[row, :] % 128
            one_hot = (spot == cells).astype(jnp.float32).astype(jnp.bfloat16)
            shares.append(
                lax.dot_general(
                    payload.astype(jnp.bfloat16),
                    one_hot,
                    (((1,), (1,)), ((), ())),
                    preferred_element_type=jnp.float32,
                )
            )
        for offset in range(TILE_GROUP):
            block = block_ref[group * TILE_GROUP + offset]
            strip = block % strips
            y = block // strips
            for half in range(2):
                for component in range(3):
                    start = pl.multiple_of(component * component_rows + y * group_rows, 8)
                    own = (half * 3 + component) * group_rows
                    field[strip * 2 + half, pl.ds(start, group_rows), :] += shares[offset][
                        own : own + group_rows
                    ]
        return carry

    lax.fori_loop(0, tiles // TILE_GROUP, tile_group, 0)

    order = order_ref[...]
    part_sign = jnp.where(
        lax.broadcasted_iota(jnp.int32, (slab_rows, group_rows, PAIR), 1) < half_modes, 1.0, -1.0
    )
    half_waves = pencil_waves // 2
    copies = []
    for component in range(3):
        rows = slice(component * component_rows, (component + 1) * component_rows)
        for strip in range(HALF // 128):
            low = field[strip, rows, :]
            high = field[strip + HALF // 128, rows, :]
            lanes = slice(strip * 128, (strip + 1) * 128)
            left[0, :, lanes] = (low + high).astype(jnp.bfloat16)
            left[1, :, lanes] = (low - high).astype(jnp.bfloat16)
        for parity in range(2):
            product = dot32(left[parity], table[parity])
            turned = product[:, PAIR:].reshape(slab_rows, group_rows, PAIR)
            turned = pltpu.roll(turned, half_modes, 1) * part_sign
            spectrum = (product[:, :PAIR] + turned.reshape(component_rows, PAIR)).astype(
                jnp.bfloat16
            )
            spectrum = dot32(order, spectrum).astype(jnp.bfloat16)
            for owner_px in range(KX // pencil_waves):
                for part in range(2):
                    for mode in range(half_modes):
                        column = (
                            (component * pencil_modes + mode % pencil_modes) * 2 + part
                        ) * pencil_waves + parity * half_waves
                        row = (part * half_modes + mode) * slab_rows
                        packed[
                            owner_px * pz_count + mode // pencil_modes,
                            :,
                            column : column + half_waves,
                        ] = spectrum[
                            row : row + slab_rows,
                            owner_px * half_waves : (owner_px + 1) * half_waves,
                        ]
        span = 2 * pencil_modes * pencil_waves
        lanes = pl.ds(component * span, span)
        copy = pltpu.make_async_copy(
            packed.at[:, :, lanes], out_ref.at[:, :, lanes], out_sem.at[component]
        )
        copy.start()
        copies.append(copy)
    for copy in copies:
        copy.wait()
    phase_copy.wait()


def table_kernel(base_cos_ref, base_sin_ref, step_cos_ref, step_sin_ref, out_ref, work_cos, work_sin):
    for parity in range(2):
        grow(
            work_cos,
            work_sin,
            (base_cos_ref[parity], base_sin_ref[parity]),
            (step_cos_ref, step_sin_ref),
            PAIR,
        )
        out_ref[parity, 0:PAIR, :] = work_cos[...].astype(jnp.bfloat16)
        out_ref[parity, PAIR:KX, :] = work_sin[...].astype(jnp.bfloat16)


def split(value):
    high = value.astype(jnp.bfloat16)
    return high, (value - high.astype(jnp.float32)).astype(jnp.bfloat16)


def project_kernel(high_ref, low_ref, order_ref, state_ref, out_ref):
    order = order_ref[...]
    state_high, state_low = [
        dot32(value, order).astype(jnp.bfloat16) for value in split(state_ref[...])
    ]
    out_ref[...] = (
        dot32(high_ref[...], state_high)
        + dot32(high_ref[...], state_low)
        + dot32(low_ref[...], state_high)
    )


def solve_kernel(
    inverse_high_ref,
    inverse_low_ref,
    basis_high_ref,
    basis_low_ref,
    damping_ref,
    state_ref,
    force_ref,
    out_ref,
    matrices,
    damping,
    state,
    sems,
):
    rows, step = damping_ref.shape
    columns = force_ref.shape[-1]
    force_rows = force_ref[...].reshape(rows, columns)
    slab_shape = out_ref.shape[:2]
    spans = [pl.ds(start, step) for start in range(0, columns, step)]
    loads = [
        (inverse_high_ref, matrices.at[0]),
        (inverse_low_ref, matrices.at[1]),
        (state_ref.at[:, spans[0]], state.at[:, spans[0]]),
        (damping_ref, damping),
        (basis_high_ref, matrices.at[2]),
        (basis_low_ref, matrices.at[3]),
    ] + [(state_ref.at[:, span], state.at[:, span]) for span in spans[1:]]
    copies = [
        pltpu.make_async_copy(source, target, sems.at[index])
        for index, (source, target) in enumerate(loads)
    ]
    for copy in copies:
        copy.start()
    for index, start in enumerate(range(0, columns, step)):
        lanes = slice(start, start + step)
        force = force_rows[:, lanes]
        if index == 0:
            copies[0].wait()
            copies[1].wait()
        pushed = dot32(matrices[0], force) + dot32(matrices[1], force)
        copies[2 if index == 0 else 5 + index].wait()
        if index == 0:
            copies[3].wait()
        modal = (state[:, lanes] + time_step * pushed) * damping[...]
        modal_high, modal_low = split(modal)
        if index == 0:
            copies[4].wait()
            copies[5].wait()
        solved = (
            dot32(matrices[2], modal_high)
            + dot32(matrices[2], modal_low)
            + dot32(matrices[3], modal_high)
        )
        out_ref[:, :, lanes] = solved.astype(jnp.bfloat16).reshape(slab_shape + (step,))


def merge_rows(values):
    sublane = lax.broadcasted_iota(jnp.int32, (8, 128), 0)
    for bit in (4, 2, 1):
        keep = (sublane & bit) == 0
        half = len(values) // 2
        merged = []
        for index in range(half):
            a, b = values[index], values[index + half]
            own = jnp.where(keep, a, b)
            other = jnp.where(keep, b, a)
            if bit == 4:
                moved = pltpu.roll(other, 4, 0)
            else:
                moved = jnp.where(
                    keep, pltpu.roll(other, 8 - bit, 0), pltpu.roll(other, bit, 0)
                )
            merged.append(own + moved)
        values = merged
    return values[0]


def gather_kernel(
    block_ref,
    cell_ref,
    order_ref,
    table_ref,
    back_ref,
    phase_ref,
    planes_ref,
    part_ref,
    left,
    values,
    planes,
    sampled,
    phases,
    table,
    table_sem,
    phase_sem,
    plane_sem,
    *,
    half_modes,
    pencil_modes,
    pencil_waves,
):
    tiles, size = cell_ref.shape
    strips = NX // CB
    group_rows = 2 * half_modes
    slab_rows = back_ref.shape[1]
    pz_count = half_modes // pencil_modes
    half_waves = pencil_waves // 2
    component_rows = group_rows * slab_rows
    table_copies = [
        pltpu.make_async_copy(table_ref.at[parity], table.at[parity], table_sem.at[parity])
        for parity in range(2)
    ]
    for copy in table_copies:
        copy.start()
    phase_copy = pltpu.make_async_copy(phase_ref, phases, phase_sem)
    phase_copy.start()
    copies = []
    for component in range(3):
        rows = []
        for part in range(2):
            for mode in range(half_modes):
                column = (
                    (component * pencil_modes + mode % pencil_modes) * 2 + part
                ) * pencil_waves
                pieces = []
                for parity in range(2):
                    for px in range(KX // pencil_waves):
                        first = column + parity * half_waves
                        pieces.append(
                            back_ref[
                                px * pz_count + mode // pencil_modes,
                                :,
                                first : first + half_waves,
                            ]
                        )
                rows.append(jnp.concatenate(pieces, axis=1))
        turned = dot32(order_ref[...], jnp.concatenate(rows, axis=0)).astype(jnp.bfloat16)
        for parity in range(2):
            lanes = slice(parity * PAIR, (parity + 1) * PAIR)
            left[parity, :, 0:PAIR] = turned[0:component_rows, lanes]
            left[parity, :, PAIR:KX] = turned[component_rows:, lanes]
        if component == 0:
            table_copies[0].wait()
        even = dot32(left[0], table[0])
        if component == 0:
            table_copies[1].wait()
        odd = dot32(left[1], table[1])
        for side in range(2):
            plane = (even + odd if side == 0 else even - odd).astype(jnp.bfloat16)
            whole = plane.astype(jnp.float32)
            planes[:, component, :, :, side * HALF : (side + 1) * HALF] = plane.reshape(
                slab_rows, half_modes, 2, HALF
            )
            for strip in range(HALF // 128):
                values[
                    side * (HALF // 128) + strip,
                    component * component_rows : (component + 1) * component_rows,
                    :,
                ] = whole[:, strip * 128 : (strip + 1) * 128]
        copy = pltpu.make_async_copy(
            planes.at[:, component], planes_ref.at[:, component], plane_sem.at[component]
        )
        copy.start()
        copies.append(copy)
    phase_copy.wait()

    def tile_group(group, carry):
        first_tile = pl.multiple_of(group * 8, 8)
        places = []
        for offset in range(8):
            block = block_ref[first_tile + offset]
            places.append((block % strips, block // strips))
        cells = cell_ref[pl.ds(first_tile, 8), :]
        for piece in range(size // 128):
            lanes = slice(piece * 128, (piece + 1) * 128)
            weighted = [[], [], []]
            for offset in range(8):
                strip, y = places[offset]
                cell = jnp.broadcast_to(cells[offset : offset + 1, lanes], (group_rows, 128))
                spot = cell % 128
                upper = cell >= 128
                rows_of_tile = pl.multiple_of((first_tile + offset) * group_rows, 8)
                phase = phases[piece, pl.ds(rows_of_tile, group_rows), :]
                for component in range(3):
                    start = pl.multiple_of(component * component_rows + y * group_rows, 8)
                    rows = pl.ds(start, group_rows)
                    low = jnp.take_along_axis(values[strip * 2, rows, :], spot, axis=1)
                    high = jnp.take_along_axis(values[strip * 2 + 1, rows, :], spot, axis=1)
                    product = jnp.where(upper, high, low) * phase
                    total = product[0:8]
                    for more in range(8, group_rows, 8):
                        total = total + product[more : more + 8]
                    weighted[component].append(total)
            for component in range(3):
                sampled[component, pl.ds(first_tile, 8), lanes] = merge_rows(weighted[component])
        return carry

    lax.fori_loop(0, tiles // 8, tile_group, 0)
    part_ref[...] = sampled[...].astype(jnp.bfloat16)
    for copy in copies:
        copy.wait()


def on_device(
    cell_index,
    block_index,
    volume,
    response_rate,
    spanwise_position,
    particle_velocity,
    seen_velocity,
    fluid_velocity,
    eigen_basis,
    eigen_inverse,
    eigenvalues,
):
    group_index = lax.axis_index("grp")
    px_count = lax.axis_size("px")
    pz_count = lax.axis_size("pz")
    rows = fluid_velocity.shape[0]
    pencil_modes = fluid_velocity.shape[2]
    pencil_waves = fluid_velocity.shape[4]
    half_modes = pencil_modes * pz_count
    slabs = px_count * pz_count
    slab_rows = rows // slabs
    strips = NX // CB
    tiles, size = cell_index.shape
    width = 6 * half_modes
    component_rows = 2 * half_modes * slab_rows
    columns = 6 * pencil_modes * pencil_waves
    pencil = pencil_modes * pencil_waves
    sizes = dict(half_modes=half_modes, pencil_modes=pencil_modes, pencil_waves=pencil_waves)

    vmem = pl.BlockSpec(memory_space=pltpu.VMEM)
    smem = pl.BlockSpec(memory_space=pltpu.SMEM)
    hbm = pl.BlockSpec(memory_space=pltpu.HBM)
    in_hbm = functools.partial(pltpu.with_memory_space_constraint, memory_space=pltpu.HBM)
    phase_shape = (size // 128, tiles * 2 * half_modes, 128)

    outgoing, phases = pl.pallas_call(
        functools.partial(spread_kernel, **sizes),
        out_shape=(
            jax.ShapeDtypeStruct((slabs, slab_rows, columns), jnp.bfloat16),
            jax.ShapeDtypeStruct(phase_shape, jnp.float32),
        ),
        in_specs=[smem, smem] + [vmem] * 11,
        out_specs=(hbm, hbm),
        scratch_shapes=[
            pltpu.VMEM((NX // 128, slab_rows * width, 128), jnp.float32),
            pltpu.VMEM((HALF, KX), jnp.float32),
            pltpu.VMEM((HALF, KX), jnp.float32),
            pltpu.VMEM((2, HALF, KX), jnp.bfloat16),
            pltpu.VMEM((2, component_rows, HALF), jnp.bfloat16),
            pltpu.VMEM((6, tiles, size), jnp.float32),
            pltpu.VMEM(phase_shape, jnp.float32),
            pltpu.VMEM(phase_shape, jnp.float32),
            pltpu.VMEM((slabs, slab_rows, columns), jnp.bfloat16),
            pltpu.SemaphoreType.DMA,
            pltpu.SemaphoreType.DMA((3,)),
        ],
        name="spread",
    )(
        block_index,
        group_index.reshape(1).astype(jnp.int32),
        cell_index,
        volume,
        response_rate,
        spanwise_position,
        particle_velocity,
        seen_velocity,
        *[jnp.asarray(seed) for seed in forward_seeds()],
        jnp.asarray(spread_rows(half_modes, slab_rows), jnp.bfloat16),
    )
    force = lax.all_to_all(outgoing, ("px", "pz"), split_axis=0, concat_axis=0, tiled=True)

    def halves(matrix):
        high = lax.reduce_precision(matrix, 8, 7)
        return high.astype(jnp.bfloat16), (matrix - high).astype(jnp.bfloat16)

    inverse_high, inverse_low = halves(eigen_inverse)
    basis_high, basis_low = halves(eigen_basis)
    state = fluid_velocity.transpose(0, 1, 2, 3, 4).reshape(rows, columns)
    square = pl.BlockSpec((rows, rows), lambda i: (0, 0))
    strip_spec = pl.BlockSpec((rows, pencil_waves), lambda i: (0, i))
    projected = pl.pallas_call(
        project_kernel,
        grid=(columns // pencil_waves,),
        out_shape=jax.ShapeDtypeStruct((rows, columns), jnp.float32),
        in_specs=[
            square,
            square,
            pl.BlockSpec((pencil_waves, pencil_waves), lambda i: (0, 0)),
            strip_spec,
        ],
        out_specs=strip_spec,
        compiler_params=pltpu.CompilerParams(vmem_limit_bytes=24 << 20),
        name="project",
    )(inverse_high, inverse_low, jnp.asarray(order_matrix(pencil_waves), jnp.bfloat16), state)
    lane = jnp.arange(pencil_waves)
    half_waves = pencil_waves // 2
    wave = 2 * (lane % half_waves) + lane // half_waves
    stream_wave = (lax.axis_index("px") * pencil_waves + wave - KX // 2).astype(jnp.float32) * 0.5
    span_wave = (
        group_index * half_modes
        + lax.axis_index("pz") * pencil_modes
        + jnp.arange(pencil_modes)
        + 1
    ).astype(jnp.float32)
    wave_square = (
        stream_wave[None, :] * stream_wave[None, :] + span_wave[:, None] * span_wave[:, None]
    )
    wave_square = jnp.broadcast_to(wave_square[:, None, :], (pencil_modes, 2, pencil_waves))
    damping = 1.0 / (
        1.0 + viscosity * (eigenvalues[:, None] + wave_square.reshape(1, 2 * pencil))
    )
    table = pl.pallas_call(
        table_kernel,
        out_shape=jax.ShapeDtypeStruct((2, KX, HALF), jnp.bfloat16),
        in_specs=[vmem] * 4,
        out_specs=vmem,
        scratch_shapes=[pltpu.VMEM((PAIR, HALF), jnp.float32)] * 2,
        compiler_params=pltpu.CompilerParams(vmem_limit_bytes=24 << 20),
        name="waves",
    )(*[jnp.asarray(seed) for seed in inverse_seeds()])

    solved = pl.pallas_call(
        solve_kernel,
        out_shape=jax.ShapeDtypeStruct((slabs, slab_rows, columns), jnp.bfloat16),
        in_specs=[hbm] * 6 + [vmem],
        out_specs=vmem,
        scratch_shapes=[
            pltpu.VMEM((4, rows, rows), jnp.bfloat16),
            pltpu.VMEM((rows, 2 * pencil), jnp.float32),
            pltpu.VMEM((rows, columns), jnp.float32),
            pltpu.SemaphoreType.DMA((8,)),
        ],
        compiler_params=pltpu.CompilerParams(vmem_limit_bytes=32 << 20),
        name="solve",
    )(
        in_hbm(inverse_high),
        in_hbm(inverse_low),
        in_hbm(basis_high),
        in_hbm(basis_low),
        in_hbm(damping),
        in_hbm(projected),
        force,
    )
    returned = lax.all_to_all(solved, ("px", "pz"), split_axis=0, concat_axis=0, tiled=True)
    velocity_planes, mode_part = pl.pallas_call(
        functools.partial(gather_kernel, **sizes),
        out_shape=(
            jax.ShapeDtypeStruct((slab_rows, 3, half_modes, 2, NX), jnp.bfloat16),
            jax.ShapeDtypeStruct((3, tiles, size), jnp.bfloat16),
        ),
        in_specs=[smem, vmem, vmem, hbm, vmem, hbm],
        out_specs=(hbm, vmem),
        scratch_shapes=[
            pltpu.VMEM((2, component_rows, KX), jnp.bfloat16),
            pltpu.VMEM((NX // 128, slab_rows * width, 128), jnp.float32),
            pltpu.VMEM((slab_rows, 3, half_modes, 2, NX), jnp.bfloat16),
            pltpu.VMEM((3, tiles, size), jnp.float32),
            pltpu.VMEM(phase_shape, jnp.float32),
            pltpu.VMEM((2, KX, HALF), jnp.bfloat16),
            pltpu.SemaphoreType.DMA((2,)),
            pltpu.SemaphoreType.DMA,
            pltpu.SemaphoreType.DMA((3,)),
        ],
        compiler_params=pltpu.CompilerParams(vmem_limit_bytes=40 << 20),
        name="gather",
    )(
        block_index,
        cell_index,
        jnp.asarray(gather_rows(half_modes, slab_rows), jnp.bfloat16),
        in_hbm(table),
        returned,
        in_hbm(phases),
    )
    other_part = lax.ppermute(mode_part, "grp", [(0, 1), (1, 0)])
    fluid_at = mode_part.astype(jnp.float32) + other_part.astype(jnp.float32)
    upward = (jnp.arange(3) == 1).astype(jnp.float32)[:, None, None]
    updated_velocity = (
        particle_velocity
        + time_step * response_rate * (fluid_at - particle_velocity)
        - time_step * gravity * upward
    )
    return (velocity_planes, updated_velocity)


def solution(mesh):
    in_specs = (
        P(("px", "pz"), None),
        P(("px", "pz")),
        P(("px", "pz"), None),
        P(("px", "pz"), None),
        P(("px", "pz"), None),
        P(None, ("px", "pz"), None),
        P(None, ("px", "pz"), None),
        P(None, None, ("grp", "pz"), None, "px"),
        P(),
        P(),
        P(),
    )
    out_specs = (P(("px", "pz"), None, "grp", None, None), P(None, ("px", "pz"), None))
    return jax.shard_map(
        on_device, mesh=mesh, in_specs=in_specs, out_specs=out_specs, check_vma=False
    )
```

time: 149 us -> 131 us (0.88)
  Pallas kernels: 60.6 us -> 42.2 us
  local copies, waits for them, and re-layouts: 14.7 us -> 7.88 us
  waiting for transfers between devices: 54.6 us -> 61.2 us
    pallas_call x1, Pallas kernels: 21 us -> 15.2 us  [on_device(): pl.pallas_call(functools.partial(spread_kernel, **sizes), out_shape=(jax....]
    unnamed x15 -> x32, local copies, waits for them, and re-layouts: 9.2 us -> 3.74 us
    pallas_call x1, Pallas kernels: 15.8 us -> 10.3 us  [on_device(): pl.pallas_call(functools.partial(gather_kernel, **sizes), out_shape=(jax....]
    ppermute x1, waiting for transfers between devices: 0.01 us -> 5 us  [on_device(): other_part = lax.ppermute(mode_part, 'grp', [(0, 1), (1, 0)])]
    pallas_call x2, Pallas kernels: 19 us -> 14.8 us  [the longest x1 9.07 us: on_device(): pl.pallas_call(solve_kernel, out_shape=jax.ShapeDtypeStruct((slabs, slab_...]
    pallas_call x1, Pallas kernels: 4.83 us -> 1.98 us  [on_device(): pl.pallas_call(table_kernel, out_shape=jax.ShapeDtypeStruct((2, KX, HALF)...]
  transfers between devices with their start and end apart: 3 -> 3, of which waited for: 2 -> 3; matrix products, arithmetic and copies ran while one was open for 11% -> 6% of each run, Pallas kernels for 8% -> 6%
where the time goes in v1:
time: 131 us; the launch traced here: 130 us
  waiting for transfers between devices  61.2 us (47%)
  Pallas kernels  42.2 us (32%)
  starting transfers between devices  13.1 us (10%)
  local copies, waits for them, and re-layouts  7.88 us (6%)
  other arithmetic  5.02 us (4%)
    all_to_all x1, waiting for transfers between devices, on_device(): lax.all_to_all(solved, ('px', 'pz'), split_axis=0, concat_axis=0, tiled=T...  33.8 us
    all_to_all x1, waiting for transfers between devices, on_device(): lax.all_to_all(outgoing, ('px', 'pz'), split_axis=0, concat_axis=0, tiled...  22.4 us
    pallas_call x1, Pallas kernels, on_device(): pl.pallas_call(functools.partial(spread_kernel, **sizes), out_shape=(jax....  15.2 us
    pallas_call x1, Pallas kernels, on_device(): pl.pallas_call(functools.partial(gather_kernel, **sizes), out_shape=(jax....  10.3 us
    pallas_call x1, Pallas kernels, on_device(): pl.pallas_call(solve_kernel, out_shape=jax.ShapeDtypeStruct((slabs, slab_...  9.07 us
    all_to_all x1, starting transfers between devices, on_device(): lax.all_to_all(outgoing, ('px', 'pz'), split_axis=0, concat_axis=0, tiled...  7.47 us
    pallas_call x1, Pallas kernels, on_device(): pl.pallas_call(project_kernel, grid=(columns // pencil_waves,), out_shape...  5.7 us
    ppermute x1, waiting for transfers between devices, on_device(): other_part = lax.ppermute(mode_part, 'grp', [(0, 1), (1, 0)])  5 us
  transfers between devices with their start and end apart: 3, of which 3 were waited for; matrix products, arithmetic and copies ran while one was open for 6% of the time, Pallas kernels for 6%

profile of v1, /device:TPU:0, one launch (start us, length us, event | category | flops | bytes accessed | tf_op | source)
XLA Modules:
  0.0 130.3 jit_solution(1195913916855101331)
XLA Ops:
  0.6 15.2 %spread.1 = (bf16[16,32,1536]{2,1,0:T(8,128)(2,1)}, f32[4,512,128]{2,1,0:T(8,128)}) custom-call(s32[64]{0:T(128)} %block_ref.3, s32[1]{0:T(128)} %bitcast.group_ref, s32[64,512]{1,0:T(8,128)} %cell_ref.3, f32[64,512]{1,0:T(8,128)} %volume_ref.1, f32[64,512]{1,0:T(8,128)} %rate_ref.1, f32[64,512]{1,0:T(8,128)} %place_ref.1, f32[3,64,512]{2,1,0:T(8,128)} %motion_ref.1, ...), custom_call_target="tpu_custom_call" | custom-call | tf_op jit(solution)/shard_map/spread/pallas_call | solution.py:547
  15.8 7.5 %all-to-all-start = ((bf16[16,32,1536]{2,1,0:T(8,128)(2,1)}), bf16[16,32,1536]{2,1,0:T(8,128)(2,1)}, u32[]{:S(2)}, u32[]{:S(2)}) async-start(bf16[16,32,1536]{2,1,0:T(8,128)(2,1)} %get-tuple-element.6), calls=%async_computation | async-start | bytes 3145728 | tf_op jit(solution)/shard_map/all_to_all | solution.py:581
  23.3 4.1 %reshape.64.state_ref = f32[512,1536]{1,0:T(8,128)S(1)} reshape(f32[512,3,1,2,256]{4,3,2,1,0:T(2,128)} %param.29) | data formatting | bytes 6291456 | tf_op jit(solution)/shard_map/reshape | solution.py:589
  27.4 0.0 copy-start.6
  27.5 2.9 %fusion = (bf16[512,512]{1,0:T(8,128)(2,1)S(1)}, bf16[512,512]{1,0:T(8,128)(2,1)S(1)}, bf16[512,512]{1,0:T(8,128)(2,1)}, bf16[512,512]{1,0:T(8,128)(2,1)}) fusion(f32[512,512]{1,0:T(8,128)} %param.31, f32[512,512]{1,0:T(8,128)} %param.30), kind=kLoop, calls=%fused_computation.4 | loop fusion | flops 2097152 | bytes 4194304 | tf_op jit(solution)/shard_map/convert_element_type | solution.py:585
  30.4 0.0 copy-start.2
  30.4 0.0 copy-start.3
  30.4 0.0 copy-done.6
  30.4 0.0 copy-start.14
  30.4 5.7 %project.1.state_ref = f32[512,1536]{1,0:T(8,128)S(1)} custom-call(bf16[512,512]{1,0:T(8,128)(2,1)S(1)} %get-tuple-element.13.high_ref.inverse_high_ref, bf16[512,512]{1,0:T(8,128)(2,1)S(1)} %get-tuple-element.12.low_ref.inverse_low_ref, bf16[256,256]{1,0:T(8,128)(2,1)S(1)} %copy-done.6, f32[512,1536]{1,0:T(8,128)S(1)} %reshape.64.state_ref), custom_call_target="tpu_custom_call" | custom-call | tf_op jit(solution)/shard_map/project/pallas_call | solution.py:592
  36.1 0.0 copy-done.2
  36.1 0.0 copy-done.3
  36.2 0.0 copy-start.1
  36.2 1.7 %copy-done.1 = f32[512,1536]{1,0:T(8,128)} copy-done((f32[512,1536]{1,0:T(8,128)}, f32[512,1536]{1,0:T(8,128)S(1)}, u32[]{:S(2)}) %copy-start.1) | copy-done | bytes 3145752
  37.8 0.0 copy-done.14
  37.8 1.2 add_divide_fusion.damping_ref
  39.0 22.4 %all-to-all-done.force_ref = bf16[16,32,1536]{2,1,0:T(8,128)(2,1)} async-done(((bf16[16,32,1536]{2,1,0:T(8,128)(2,1)}), bf16[16,32,1536]{2,1,0:T(8,128)(2,1)}, u32[]{:S(2)}, u32[]{:S(2)}) %all-to-all-start) | async-done | bytes 1572896 | tf_op jit(solution)/shard_map/all_to_all | solution.py:581
  61.4 9.1 %solve.1 = bf16[16,32,1536]{2,1,0:T(8,128)(2,1)} custom-call(bf16[512,512]{1,0:T(8,128)(2,1)} %copy-done.3, bf16[512,512]{1,0:T(8,128)(2,1)} %copy-done.2, bf16[512,512]{1,0:T(8,128)(2,1)} %get-tuple-element.14.basis_high_ref, bf16[512,512]{1,0:T(8,128)(2,1)} %get-tuple-element.15.basis_low_ref, f32[512,512]{1,0:T(8,128)} %add_divide_fusion.damping_ref, ...), custom_call_target="tpu_custom_call" | custom-call | tf_op jit(solution)/shard_map/solve/pallas_call | solution.py:633
  70.5 0.0 copy-start.7
  70.5 0.0 copy-start.8
  70.5 0.0 copy-start.9
  70.5 0.0 copy-start.10
  70.6 0.0 copy-start.4
  70.6 0.0 copy-start.5
  70.6 0.0 copy-start.11
  70.6 4.1 %all-to-all-start.1 = ((bf16[16,32,1536]{2,1,0:T(8,128)(2,1)}), bf16[16,32,1536]{2,1,0:T(8,128)(2,1)S(1)}, u32[]{:S(2)}, u32[]{:S(2)}) async-start(bf16[16,32,1536]{2,1,0:T(8,128)(2,1)} %solve.1), calls=%async_computation.1 | async-start | bytes 3145728 | tf_op jit(solution)/shard_map/all_to_all | solution.py:655
  74.7 0.0 copy-done.7
  74.7 0.0 copy-done.8
  74.7 0.0 copy-done.9
  74.7 0.0 copy-done.10
  74.7 2.0 %waves.1.table_ref = bf16[2,1024,1024]{2,1,0:T(8,128)(2,1)S(1)} custom-call(f32[2,8,1024]{2,1,0:T(8,128)S(1)} %copy-done.7, f32[2,8,1024]{2,1,0:T(8,128)S(1)} %copy-done.8, f32[8,1024]{1,0:T(8,128)S(1)} %copy-done.9, f32[8,1024]{1,0:T(8,128)S(1)} %copy-done.10), custom_call_target="tpu_custom_call" | custom-call | tf_op jit(solution)/shard_map/waves/pallas_call | solution.py:623
  76.7 0.0 copy-start
  76.7 2.0 %copy-done = bf16[2,1024,1024]{2,1,0:T(8,128)(2,1)} copy-done((bf16[2,1024,1024]{2,1,0:T(8,128)(2,1)}, bf16[2,1024,1024]{2,1,0:T(8,128)(2,1)S(1)}, u32[]{:S(2)}) %copy-start) | copy-done | bytes 4194328
  78.7 33.8 %all-to-all-done.1.back_ref = bf16[16,32,1536]{2,1,0:T(8,128)(2,1)S(1)} async-done(((bf16[16,32,1536]{2,1,0:T(8,128)(2,1)}), bf16[16,32,1536]{2,1,0:T(8,128)(2,1)S(1)}, u32[]{:S(2)}, u32[]{:S(2)}) %all-to-all-start.1) | async-done | bytes 1572896 | tf_op jit(solution)/shard_map/all_to_all | solution.py:655
  112.5 0.0 copy-done.4
  112.5 0.0 copy-done.5
  112.5 0.0 copy-done.11
  112.5 0.0 copy-start.13
  112.5 0.0 copy-start.12
  112.5 10.3 %gather.1 = (bf16[32,3,4,2,2048]{4,3,2,1,0:T(2,128)(2,1)}, bf16[3,64,512]{2,1,0:T(8,128)(2,1)S(1)}) custom-call(s32[64]{0:T(128)S(1)} %copy-done.11, s32[64,512]{1,0:T(8,128)S(1)} %copy-done.4, bf16[512,256]{1,0:T(8,128)(2,1)S(1)} %copy-done.5, bf16[2,1024,1024]{2,1,0:T(8,128)(2,1)} %copy-done, bf16[16,32,1536]{2,1,0:T(8,128)(2,1)S(1)} %all-to-all-done.1.back_ref, ...), custom_call_target="tpu_custom_call" | custom-call | tf_op jit(solution)/shard_map/gather/pallas_call | solution.py:656
  122.9 1.6 %collective-permute-start = (bf16[3,64,512]{2,1,0:T(8,128)(2,1)S(1)}, bf16[3,64,512]{2,1,0:T(8,128)(2,1)S(1)}, u32[]{:S(2)}, u32[]{:S(2)}) collective-permute-start(bf16[3,64,512]{2,1,0:T(8,128)(2,1)S(1)} %get-tuple-element.9), channel_id=1, source_target_pairs={{0,16},{16,0},{1,17},{17,1},{2,18},{18,2},{3,19},{19,3},{4,20},{20... | collective-permute-start | bytes 589832 | tf_op jit(solution)/shard_map/ppermute | solution.py:685
  124.4 0.0 copy-done.13
  124.4 5.0 %collective-permute-done = bf16[3,64,512]{2,1,0:T(8,128)(2,1)S(1)} collective-permute-done((bf16[3,64,512]{2,1,0:T(8,128)(2,1)S(1)}, bf16[3,64,512]{2,1,0:T(8,128)(2,1)S(1)}, u32[]{:S(2)}, u32[]{:S(2)}) %collective-permute-start) | collective-permute-done | bytes 196640 | tf_op jit(solution)/shard_map/ppermute | solution.py:685
  129.5 0.0 copy-done.12
  129.5 0.9 add_subtract_fusion
  (5 shorter events, 0.0 us)
Async XLA Ops:
  15.8 45.6 %all-to-all-start = ((bf16[16,32,1536]{2,1,0:T(8,128)(2,1)}), bf16[16,32,1536]{2,1,0:T(8,128)(2,1)}, u32[]{:S(2)}, u32[]{:S(2)}) async-start(bf16[16,32,1536]{2,1,0:T(8,128)(2,1)} %get-tuple-element.6), calls=%async_computation | async-start | bytes 3145728 | tf_op jit(solution)/shard_map/all_to_all | solution.py:581
  27.4 3.0 %copy-start.6 = (bf16[256,256]{1,0:T(8,128)(2,1)S(1)}, bf16[256,256]{1,0:T(8,128)(2,1)}, u32[]{:S(2)}) copy-start(bf16[256,256]{1,0:T(8,128)(2,1)} %constant.94.clone.order_ref) | copy-start | bytes 393220
  30.4 5.7 %copy-start.2 = (bf16[512,512]{1,0:T(8,128)(2,1)}, bf16[512,512]{1,0:T(8,128)(2,1)S(1)}, u32[]{:S(2)}) copy-start(bf16[512,512]{1,0:T(8,128)(2,1)S(1)} %get-tuple-element.12.low_ref.inverse_low_ref) | copy-start | bytes 1572868
  30.4 5.7 %copy-start.3 = (bf16[512,512]{1,0:T(8,128)(2,1)}, bf16[512,512]{1,0:T(8,128)(2,1)S(1)}, u32[]{:S(2)}) copy-start(bf16[512,512]{1,0:T(8,128)(2,1)S(1)} %get-tuple-element.13.high_ref.inverse_high_ref) | copy-start | bytes 1572868
  30.4 7.4 %copy-start.14 = (f32[512]{0:T(512)S(1)}, f32[512]{0:T(512)}, u32[]{:S(2)}) copy-start(f32[512]{0:T(512)} %param.32) | copy-start | bytes 6148
  36.2 1.7 %copy-start.1 = (f32[512,1536]{1,0:T(8,128)}, f32[512,1536]{1,0:T(8,128)S(1)}, u32[]{:S(2)}) copy-start(f32[512,1536]{1,0:T(8,128)S(1)} %project.1.state_ref) | copy-start | bytes 9437188
  70.5 4.2 %copy-start.7 = (f32[2,8,1024]{2,1,0:T(8,128)S(1)}, f32[2,8,1024]{2,1,0:T(8,128)}, u32[]{:S(2)}) copy-start(f32[2,8,1024]{2,1,0:T(8,128)} %constant.95.clone.base_cos_ref) | copy-start | bytes 196612
  70.5 4.2 %copy-start.8 = (f32[2,8,1024]{2,1,0:T(8,128)S(1)}, f32[2,8,1024]{2,1,0:T(8,128)}, u32[]{:S(2)}) copy-start(f32[2,8,1024]{2,1,0:T(8,128)} %constant.96.clone.base_sin_ref) | copy-start | bytes 196612
  70.5 4.2 %copy-start.9 = (f32[8,1024]{1,0:T(8,128)S(1)}, f32[8,1024]{1,0:T(8,128)}, u32[]{:S(2)}) copy-start(f32[8,1024]{1,0:T(8,128)} %constant.97.clone.step_cos_ref) | copy-start | bytes 98308
  70.5 4.2 %copy-start.10 = (f32[8,1024]{1,0:T(8,128)S(1)}, f32[8,1024]{1,0:T(8,128)}, u32[]{:S(2)}) copy-start(f32[8,1024]{1,0:T(8,128)} %constant.98.clone.step_sin_ref) | copy-start | bytes 98308
  70.6 42.0 %copy-start.4 = (s32[64,512]{1,0:T(8,128)S(1)}, s32[64,512]{1,0:T(8,128)}, u32[]{:S(2)}) copy-start(s32[64,512]{1,0:T(8,128)} %cell_ref.3) | copy-start | bytes 393220
  70.6 42.0 %copy-start.5 = (bf16[512,256]{1,0:T(8,128)(2,1)S(1)}, bf16[512,256]{1,0:T(8,128)(2,1)}, u32[]{:S(2)}) copy-start(bf16[512,256]{1,0:T(8,128)(2,1)} %constant.99.clone.order_ref) | copy-start | bytes 786436
  70.6 41.9 %copy-start.11 = (s32[64]{0:T(128)S(1)}, s32[64]{0:T(128)}, u32[]{:S(2)}) copy-start(s32[64]{0:T(128)} %block_ref.3) | copy-start | bytes 772
  70.6 41.9 %all-to-all-start.1 = ((bf16[16,32,1536]{2,1,0:T(8,128)(2,1)}), bf16[16,32,1536]{2,1,0:T(8,128)(2,1)S(1)}, u32[]{:S(2)}, u32[]{:S(2)}) async-start(bf16[16,32,1536]{2,1,0:T(8,128)(2,1)} %solve.1), calls=%async_computation.1 | async-start | bytes 3145728 | tf_op jit(solution)/shard_map/all_to_all | solution.py:655
  76.7 2.0 %copy-start = (bf16[2,1024,1024]{2,1,0:T(8,128)(2,1)}, bf16[2,1024,1024]{2,1,0:T(8,128)(2,1)S(1)}, u32[]{:S(2)}) copy-start(bf16[2,1024,1024]{2,1,0:T(8,128)(2,1)S(1)} %waves.1.table_ref) | copy-start | bytes 12582916
  112.5 11.9 %copy-start.13 = (f32[64,512]{1,0:T(8,128)S(1)}, f32[64,512]{1,0:T(8,128)}, u32[]{:S(2)}) copy-start(f32[64,512]{1,0:T(8,128)} %rate_ref.1) | copy-start | bytes 393220
  112.5 16.9 %copy-start.12 = (f32[3,64,512]{2,1,0:T(8,128)S(1)}, f32[3,64,512]{2,1,0:T(8,128)}, u32[]{:S(2)}) copy-start(f32[3,64,512]{2,1,0:T(8,128)} %motion_ref.1) | copy-start | bytes 1179652
  122.9 6.6 %collective-permute-start = (bf16[3,64,512]{2,1,0:T(8,128)(2,1)S(1)}, bf16[3,64,512]{2,1,0:T(8,128)(2,1)S(1)}, u32[]{:S(2)}, u32[]{:S(2)}) collective-permute-start(bf16[3,64,512]{2,1,0:T(8,128)(2,1)S(1)} %get-tuple-element.9), channel_id=1, source_target_pairs={{0,16},{16,0},{1,17},{17,1},{2,18},{18,2},{3,19},{19,3},{4,20},{20... | collective-permute-start | bytes 589832 | tf_op jit(solution)/shard_map/ppermute | solution.py:685

commit v2 on v1

--- a/solution.py
+++ b/solution.py
@@ -8,6 +8,7 @@
 from jax.experimental import pallas as pl
 from jax.experimental.pallas import tpu as pltpu
 from jax.sharding import PartitionSpec as P
+
 
 NX = 2048
 KX = 1024
@@ -53,14 +54,13 @@
     return matrix
 
 
-def spread_rows(half_modes, slab_rows):
-    part, mode, y = np.meshgrid(
-        np.arange(2), np.arange(half_modes), np.arange(slab_rows), indexing="ij"
-    )
-    count = part.size
-    matrix = np.zeros((count, count), np.float32)
-    source = (y * 2 + part) * half_modes + mode
-    matrix[np.arange(count), source.ravel()] = 1.0
+def spread_rows(modes, slab_rows, width):
+    component, part, mode, y = np.meshgrid(
+        np.arange(3), np.arange(2), np.arange(modes), np.arange(slab_rows), indexing="ij"
+    )
+    matrix = np.zeros((part.size, slab_rows * width), np.float32)
+    source = y * width + (component * 2 + part) * modes + mode
+    matrix[np.arange(part.size), source.ravel()] = 1.0
     return matrix
 
 
@@ -103,86 +103,74 @@
     return jnp.dot(a, b, preferred_element_type=jnp.float32)
 
 
-def spread_kernel(
-    block_ref,
-    group_ref,
-    cell_ref,
-    volume_ref,
-    rate_ref,
-    place_ref,
-    motion_ref,
-    seen_ref,
-    base_cos_ref,
-    base_sin_ref,
-    step_cos_ref,
-    step_sin_ref,
-    order_ref,
-    out_ref,
-    phase_out_ref,
-    field,
-    table_cos,
-    table_sin,
-    table,
-    left,
-    amounts,
-    phases,
-    phases_out,
-    packed,
-    phase_sem,
-    out_sem,
-    *,
-    half_modes,
-    pencil_modes,
-    pencil_waves,
-):
-    tiles, size = cell_ref.shape
-    strips = NX // CB
-    group_rows = 2 * half_modes
-    slab_rows = field.shape[1] // (3 * group_rows)
-    component_rows = slab_rows * group_rows
-    pz_count = half_modes // pencil_modes
-
-    place = place_ref[...]
-    first = (group_ref[0] * half_modes + 1).astype(jnp.float32)
-    cos_one = jnp.cos(place)
-    sin_one = jnp.sin(place)
-    cos_now = jnp.cos(place * first)
-    sin_now = jnp.sin(place * first)
-    for mode in range(half_modes):
-        for piece in range(size // 128):
-            lanes = slice(piece * 128, (piece + 1) * 128)
-            for part, value in ((0, cos_now[:, lanes]), (1, -sin_now[:, lanes])):
-                phases[piece, pl.ds(part * half_modes + mode, tiles, stride=group_rows), :] = value
-                phases_out[piece, pl.ds(2 * mode + part, tiles, stride=group_rows), :] = value
-        if mode + 1 < half_modes:
-            cos_now, sin_now = (
-                cos_now * cos_one - sin_now * sin_one,
-                sin_now * cos_one + cos_now * sin_one,
-            )
-    phase_copy = pltpu.make_async_copy(phases_out, phase_out_ref, phase_sem)
-    phase_copy.start()
-
-    upper = cell_ref[...] >= 128
+def pack_kernel(cell_ref, volume_ref, rate_ref, place_ref, motion_ref, seen_ref, out_ref):
+    out_ref[0] = cell_ref[...].astype(jnp.float32).astype(jnp.bfloat16)
     volume = volume_ref[...]
     pull = volume * rate_ref[...]
     for component in range(3):
         amount = pull * (seen_ref[component] - motion_ref[component])
         if component == 1:
             amount = amount - gravity * volume
-        amounts[component] = jnp.where(upper, 0.0, amount)
-        amounts[3 + component] = jnp.where(upper, amount, 0.0)
-
-    grow(
-        table_cos,
-        table_sin,
-        (base_cos_ref[...], base_sin_ref[...]),
-        (step_cos_ref, step_sin_ref),
-        HALF,
-    )
-    for parity in range(2):
-        lanes = slice(parity * PAIR, (parity + 1) * PAIR)
-        table[parity, :, 0:PAIR] = table_cos[:, lanes].astype(jnp.bfloat16)
-        table[parity, :, PAIR:KX] = table_sin[:, lanes].astype(jnp.bfloat16)
+        out_ref[1 + component] = amount.astype(jnp.bfloat16)
+    out_ref[4], out_ref[5] = split(place_ref[...])
+
+
+def turn_modes(place, first, modes):
+    cos_one = jnp.cos(place)
+    sin_one = jnp.sin(place)
+    cos_now = jnp.cos(place * first)
+    sin_now = jnp.sin(place * first)
+    turned = [(cos_now, sin_now)]
+    for _ in range(modes - 1):
+        cos_now, sin_now = (
+            cos_now * cos_one - sin_now * sin_one,
+            sin_now * cos_one + cos_now * sin_one,
+        )
+        turned.append((cos_now, sin_now))
+    return turned
+
+
+def phase_kernel(first_ref, place_ref, out_ref, *, half_modes):
+    tiles, size = place_ref.shape
+    first = first_ref[0].astype(jnp.float32)
+    for mode, (cosine, sine) in enumerate(turn_modes(place_ref[...], first, half_modes)):
+        for piece in range(size // 128):
+            lanes = slice(piece * 128, (piece + 1) * 128)
+            for part, value in ((0, cosine), (1, -sine)):
+                rows = pl.ds(2 * mode + part, tiles, stride=2 * half_modes)
+                out_ref[piece, rows, :] = value[:, lanes]
+
+
+def spread_kernel(*refs, modes, pencil_modes, pencil_waves, slab_rows, width, makes_table):
+    if makes_table:
+        block_ref, first_ref, pack_ref, order_ref = refs[:4]
+        base_cos_ref, base_sin_ref, step_cos_ref, step_sin_ref, out_ref, table_out_ref = refs[4:10]
+        field, left, amounts, spots, phases, table, table_sem, table_cos, table_sin = refs[10:]
+    else:
+        block_ref, first_ref, pack_ref, order_ref, table_in_ref, out_ref = refs[:6]
+        field, left, amounts, spots, phases, table, table_sem = refs[6:]
+    _, tiles, size = pack_ref.shape
+    strips = NX // CB
+    count = 2 * modes
+    zl_count = modes // pencil_modes
+    half_waves = pencil_waves // 2
+
+    if makes_table:
+        grow(
+            table_cos,
+            table_sin,
+            (base_cos_ref[...], base_sin_ref[...]),
+            (step_cos_ref, step_sin_ref),
+            HALF,
+        )
+        for parity in range(2):
+            lanes = slice(parity * PAIR, (parity + 1) * PAIR)
+            table[parity, :, 0:PAIR] = table_cos[:, lanes].astype(jnp.bfloat16)
+            table[parity, :, PAIR:KX] = table_sin[:, lanes].astype(jnp.bfloat16)
+        table_copy = pltpu.make_async_copy(table, table_out_ref, table_sem)
+    else:
+        table_copy = pltpu.make_async_copy(table_in_ref, table, table_sem)
+    table_copy.start()
 
     def clear(index, carry):
         field[index] = jnp.zeros(field.shape[1:], jnp.float32)
@@ -190,23 +178,52 @@
 
     lax.fori_loop(0, field.shape[0], clear, 0)
 
+    place = pack_ref[4].astype(jnp.float32) + pack_ref[5].astype(jnp.float32)
+    first = first_ref[0].astype(jnp.float32)
+    for mode, (cosine, sine) in enumerate(turn_modes(place, first, modes)):
+        for piece in range(size // 128):
+            lanes = slice(piece * 128, (piece + 1) * 128)
+            for part, value in ((0, cosine), (1, -sine)):
+                for component in range(width // count):
+                    row = component * count + part * modes + mode
+                    phases[piece, pl.ds(row, tiles, stride=width), :] = value[:, lanes]
+    cell = pack_ref[0].astype(jnp.float32).astype(jnp.int32)
+    spots[...] = cell % 128
+    upper = cell >= 128
+    for component in range(3):
+        amount = pack_ref[1 + component].astype(jnp.float32)
+        amounts[component] = jnp.where(upper, 0.0, amount)
+        amounts[3 + component] = jnp.where(upper, amount, 0.0)
+
     cells = lax.broadcasted_iota(jnp.int32, (128, size), 0)
+    row_component = lax.broadcasted_iota(jnp.int32, (width, size), 0) // count
 
     def tile_group(group, carry):
         shares = []
         for offset in range(TILE_GROUP):
             tile = group * TILE_GROUP + offset
             row = pl.ds(tile, 1)
-            rows_of_tile = pl.ds(pl.multiple_of(tile * group_rows, 8), group_rows)
+            rows_of_tile = pl.ds(pl.multiple_of(tile * width, 8), width)
             phase = jnp.concatenate(
                 [phases[piece, rows_of_tile, :] for piece in range(size // 128)], axis=1
             )
-            payload = jnp.concatenate([amounts[k, row, :] * phase for k in range(6)], axis=0)
-            spot = cell_ref[row, :] % 128
-            one_hot = (spot == cells).astype(jnp.float32).astype(jnp.bfloat16)
+            payload = []
+            for half in range(2):
+                spread = jnp.where(
+                    row_component == 0,
+                    amounts[3 * half, row, :],
+                    jnp.where(
+                        row_component == 1,
+                        amounts[3 * half + 1, row, :],
+                        jnp.where(row_component == 2, amounts[3 * half + 2, row, :], 0.0),
+                    ),
+                )
+                payload.append(spread * phase)
+            payload = jnp.concatenate(payload, axis=0).astype(jnp.bfloat16)
+            one_hot = (spots[row, :] == cells).astype(jnp.float32).astype(jnp.bfloat16)
             shares.append(
                 lax.dot_general(
-                    payload.astype(jnp.bfloat16),
+                    payload,
                     one_hot,
                     (((1,), (1,)), ((), ())),
                     preferred_element_type=jnp.float32,
@@ -215,65 +232,50 @@
         for offset in range(TILE_GROUP):
             block = block_ref[group * TILE_GROUP + offset]
             strip = block % strips
-            y = block // strips
+            start = pl.multiple_of((block // strips) * width, 8)
             for half in range(2):
-                for component in range(3):
-                    start = pl.multiple_of(component * component_rows + y * group_rows, 8)
-                    own = (half * 3 + component) * group_rows
-                    field[strip * 2 + half, pl.ds(start, group_rows), :] += shares[offset][
-                        own : own + group_rows
-                    ]
+                field[strip * 2 + half, pl.ds(start, width), :] += shares[offset][
+                    half * width : (half + 1) * width
+                ]
         return carry
 
     lax.fori_loop(0, tiles // TILE_GROUP, tile_group, 0)
 
+    for strip in range(HALF // 128):
+        low = field[strip]
+        high = field[strip + HALF // 128]
+        lanes = slice(strip * 128, (strip + 1) * 128)
+        left[0, :, lanes] = (low + high).astype(jnp.bfloat16)
+        left[1, :, lanes] = (low - high).astype(jnp.bfloat16)
     order = order_ref[...]
-    part_sign = jnp.where(
-        lax.broadcasted_iota(jnp.int32, (slab_rows, group_rows, PAIR), 1) < half_modes, 1.0, -1.0
-    )
-    half_waves = pencil_waves // 2
-    copies = []
-    for component in range(3):
-        rows = slice(component * component_rows, (component + 1) * component_rows)
-        for strip in range(HALF // 128):
-            low = field[strip, rows, :]
-            high = field[strip + HALF // 128, rows, :]
-            lanes = slice(strip * 128, (strip + 1) * 128)
-            left[0, :, lanes] = (low + high).astype(jnp.bfloat16)
-            left[1, :, lanes] = (low - high).astype(jnp.bfloat16)
-        for parity in range(2):
-            product = dot32(left[parity], table[parity])
-            turned = product[:, PAIR:].reshape(slab_rows, group_rows, PAIR)
-            turned = pltpu.roll(turned, half_modes, 1) * part_sign
-            spectrum = (product[:, :PAIR] + turned.reshape(component_rows, PAIR)).astype(
-                jnp.bfloat16
-            )
-            spectrum = dot32(order, spectrum).astype(jnp.bfloat16)
-            for owner_px in range(KX // pencil_waves):
+    sublane = lax.broadcasted_iota(jnp.int32, (slab_rows * width // 8, 8, PAIR), 1)
+    is_real = sublane % count < modes
+    if not makes_table:
+        table_copy.wait()
+    for parity in range(2):
+        product = dot32(left[parity], table[parity])
+        sines = product[:, PAIR:].reshape(slab_rows * width // 8, 8, PAIR)
+        turned = jnp.where(is_real, pltpu.roll(sines, 8 - modes, 1), -pltpu.roll(sines, modes, 1))
+        spectrum = product[:, :PAIR] + turned.reshape(slab_rows * width, PAIR)
+        spectrum = dot32(order, spectrum.astype(jnp.bfloat16)).astype(jnp.bfloat16)
+        for owner_px in range(KX // pencil_waves):
+            for component in range(3):
                 for part in range(2):
-                    for mode in range(half_modes):
+                    for mode in range(modes):
                         column = (
                             (component * pencil_modes + mode % pencil_modes) * 2 + part
                         ) * pencil_waves + parity * half_waves
-                        row = (part * half_modes + mode) * slab_rows
-                        packed[
-                            owner_px * pz_count + mode // pencil_modes,
+                        row = ((component * 2 + part) * modes + mode) * slab_rows
+                        out_ref[
+                            owner_px * zl_count + mode // pencil_modes,
                             :,
                             column : column + half_waves,
                         ] = spectrum[
                             row : row + slab_rows,
                             owner_px * half_waves : (owner_px + 1) * half_waves,
                         ]
-        span = 2 * pencil_modes * pencil_waves
-        lanes = pl.ds(component * span, span)
-        copy = pltpu.make_async_copy(
-            packed.at[:, :, lanes], out_ref.at[:, :, lanes], out_sem.at[component]
-        )
-        copy.start()
-        copies.append(copy)
-    for copy in copies:
-        copy.wait()
-    phase_copy.wait()
+    if makes_table:
+        table_copy.wait()
 
 
 def table_kernel(base_cos_ref, base_sin_ref, step_cos_ref, step_sin_ref, out_ref, work_cos, work_sin):
@@ -313,7 +315,8 @@
     basis_low_ref,
     damping_ref,
     state_ref,
-    force_ref,
+    own_force_ref,
+    other_force_ref,
     out_ref,
     matrices,
     damping,
@@ -321,8 +324,7 @@
     sems,
 ):
     rows, step = damping_ref.shape
-    columns = force_ref.shape[-1]
-    force_rows = force_ref[...].reshape(rows, columns)
+    columns = own_force_ref.shape[-1]
     slab_shape = out_ref.shape[:2]
     spans = [pl.ds(start, step) for start in range(0, columns, step)]
     loads = [
@@ -341,7 +343,13 @@
         copy.start()
     for index, start in enumerate(range(0, columns, step)):
         lanes = slice(start, start + step)
-        force = force_rows[:, lanes]
+        force = jnp.concatenate(
+            [
+                own_force_ref[:, :, lanes].reshape(rows // 2, step),
+                other_force_ref[:, :, lanes].reshape(rows // 2, step),
+            ],
+            axis=0,
+        )
         if index == 0:
             copies[0].wait()
             copies[1].wait()
@@ -523,14 +531,17 @@
 ):
     group_index = lax.axis_index("grp")
     px_count = lax.axis_size("px")
-    pz_count = lax.axis_size("pz")
+    zh_count = lax.axis_size("zh")
+    zl_count = lax.axis_size("zl")
+    pz_count = zh_count * zl_count
+    half_index = lax.axis_index("zh")
+    pz_index = half_index * zl_count + lax.axis_index("zl")
     rows = fluid_velocity.shape[0]
     pencil_modes = fluid_velocity.shape[2]
     pencil_waves = fluid_velocity.shape[4]
     half_modes = pencil_modes * pz_count
     slabs = px_count * pz_count
     slab_rows = rows // slabs
-    strips = NX // CB
     tiles, size = cell_index.shape
     width = 6 * half_modes
     component_rows = 2 * half_modes * slab_rows
@@ -544,41 +555,78 @@
     in_hbm = functools.partial(pltpu.with_memory_space_constraint, memory_space=pltpu.HBM)
     phase_shape = (size // 128, tiles * 2 * half_modes, 128)
 
-    outgoing, phases = pl.pallas_call(
-        functools.partial(spread_kernel, **sizes),
-        out_shape=(
-            jax.ShapeDtypeStruct((slabs, slab_rows, columns), jnp.bfloat16),
-            jax.ShapeDtypeStruct(phase_shape, jnp.float32),
-        ),
-        in_specs=[smem, smem] + [vmem] * 11,
-        out_specs=(hbm, hbm),
-        scratch_shapes=[
-            pltpu.VMEM((NX // 128, slab_rows * width, 128), jnp.float32),
-            pltpu.VMEM((HALF, KX), jnp.float32),
-            pltpu.VMEM((HALF, KX), jnp.float32),
-            pltpu.VMEM((2, HALF, KX), jnp.bfloat16),
-            pltpu.VMEM((2, component_rows, HALF), jnp.bfloat16),
-            pltpu.VMEM((6, tiles, size), jnp.float32),
-            pltpu.VMEM(phase_shape, jnp.float32),
-            pltpu.VMEM(phase_shape, jnp.float32),
-            pltpu.VMEM((slabs, slab_rows, columns), jnp.bfloat16),
-            pltpu.SemaphoreType.DMA,
-            pltpu.SemaphoreType.DMA((3,)),
-        ],
-        name="spread",
+    modes = half_modes // zh_count
+    row_width = -(-6 * modes // 8) * 8
+    spread_shape = (px_count * zl_count, slab_rows, columns)
+    table_shape = (2, HALF, KX)
+    pack = pl.pallas_call(
+        pack_kernel,
+        out_shape=jax.ShapeDtypeStruct((6, tiles, size), jnp.bfloat16),
+        in_specs=[vmem] * 6,
+        out_specs=vmem,
+        name="pack",
     )(
-        block_index,
-        group_index.reshape(1).astype(jnp.int32),
         cell_index,
         volume,
         response_rate,
         spanwise_position,
         particle_velocity,
         seen_velocity,
-        *[jnp.asarray(seed) for seed in forward_seeds()],
-        jnp.asarray(spread_rows(half_modes, slab_rows), jnp.bfloat16),
-    )
-    force = lax.all_to_all(outgoing, ("px", "pz"), split_axis=0, concat_axis=0, tiled=True)
+    )
+    swap = [(0, 1), (1, 0)]
+    other_pack = lax.ppermute(pack, "zh", swap)
+    other_block = lax.ppermute(block_index, "zh", swap)
+    first_wave = (group_index * half_modes + half_index * modes + 1).reshape(1).astype(jnp.int32)
+    spread_order = jnp.asarray(spread_rows(modes, slab_rows, row_width), jnp.bfloat16)
+    spread_scratch = [
+        pltpu.VMEM((NX // 128, slab_rows * row_width, 128), jnp.float32),
+        pltpu.VMEM((2, slab_rows * row_width, HALF), jnp.bfloat16),
+        pltpu.VMEM((6, tiles, size), jnp.float32),
+        pltpu.VMEM((tiles, size), jnp.int32),
+        pltpu.VMEM((size // 128, tiles * row_width, 128), jnp.float32),
+        pltpu.VMEM(table_shape, jnp.bfloat16),
+        pltpu.SemaphoreType.DMA,
+    ]
+    spread_sizes = dict(
+        modes=modes,
+        pencil_modes=pencil_modes,
+        pencil_waves=pencil_waves,
+        slab_rows=slab_rows,
+        width=row_width,
+    )
+    spread_own = pl.pallas_call(
+        functools.partial(spread_kernel, makes_table=True, **spread_sizes),
+        out_shape=(
+            jax.ShapeDtypeStruct(spread_shape, jnp.bfloat16),
+            jax.ShapeDtypeStruct(table_shape, jnp.bfloat16),
+        ),
+        in_specs=[smem, smem] + [vmem] * 6,
+        out_specs=(vmem, hbm),
+        scratch_shapes=spread_scratch + [pltpu.VMEM((HALF, KX), jnp.float32)] * 2,
+        name="spread",
+    )
+    seeds = [jnp.asarray(seed) for seed in forward_seeds()]
+    outgoing, wave_table = spread_own(block_index, first_wave, pack, spread_order, *seeds)
+    own_force = lax.all_to_all(outgoing, ("px", "zl"), split_axis=0, concat_axis=0, tiled=True)
+    other_outgoing = pl.pallas_call(
+        functools.partial(spread_kernel, makes_table=False, **spread_sizes),
+        out_shape=jax.ShapeDtypeStruct(spread_shape, jnp.bfloat16),
+        in_specs=[smem, smem, vmem, vmem, hbm],
+        out_specs=vmem,
+        scratch_shapes=spread_scratch,
+        name="spread_other",
+    )(other_block, first_wave, other_pack, spread_order, in_hbm(wave_table))
+    other_force = lax.all_to_all(
+        other_outgoing, ("px", "zl"), split_axis=0, concat_axis=0, tiled=True
+    )
+    phases = pl.pallas_call(
+        functools.partial(phase_kernel, half_modes=half_modes),
+        out_shape=jax.ShapeDtypeStruct(phase_shape, jnp.float32),
+        in_specs=[smem, vmem],
+        out_specs=vmem,
+        compiler_params=pltpu.CompilerParams(vmem_limit_bytes=24 << 20),
+        name="phases",
+    )((group_index * half_modes + 1).reshape(1).astype(jnp.int32), spanwise_position)
 
     def halves(matrix):
         high = lax.reduce_precision(matrix, 8, 7)
@@ -586,6 +634,12 @@
 
     inverse_high, inverse_low = halves(eigen_inverse)
     basis_high, basis_low = halves(eigen_basis)
+    by_half = eigen_inverse.reshape(rows, px_count, zh_count, zl_count * slab_rows)
+    own_columns = lax.dynamic_slice_in_dim(by_half, half_index, 1, 2).reshape(rows, rows // 2)
+    other_columns = lax.dynamic_slice_in_dim(by_half, 1 - half_index, 1, 2).reshape(
+        rows, rows // 2
+    )
+    turned_high, turned_low = halves(jnp.concatenate([own_columns, other_columns], axis=1))
     state = fluid_velocity.transpose(0, 1, 2, 3, 4).reshape(rows, columns)
     square = pl.BlockSpec((rows, rows), lambda i: (0, 0))
     strip_spec = pl.BlockSpec((rows, pencil_waves), lambda i: (0, i))
@@ -609,7 +663,7 @@
     stream_wave = (lax.axis_index("px") * pencil_waves + wave - KX // 2).astype(jnp.float32) * 0.5
     span_wave = (
         group_index * half_modes
-        + lax.axis_index("pz") * pencil_modes
+        + pz_index * pencil_modes
         + jnp.arange(pencil_modes)
         + 1
     ).astype(jnp.float32)
@@ -633,7 +687,7 @@
     solved = pl.pallas_call(
         solve_kernel,
         out_shape=jax.ShapeDtypeStruct((slabs, slab_rows, columns), jnp.bfloat16),
-        in_specs=[hbm] * 6 + [vmem],
+        in_specs=[hbm] * 6 + [vmem] * 2,
         out_specs=vmem,
         scratch_shapes=[
             pltpu.VMEM((4, rows, rows), jnp.bfloat16),
@@ -644,15 +698,16 @@
         compiler_params=pltpu.CompilerParams(vmem_limit_bytes=32 << 20),
         name="solve",
     )(
-        in_hbm(inverse_high),
-        in_hbm(inverse_low),
+        in_hbm(turned_high),
+        in_hbm(turned_low),
         in_hbm(basis_high),
         in_hbm(basis_low),
         in_hbm(damping),
         in_hbm(projected),
-        force,
-    )
-    returned = lax.all_to_all(solved, ("px", "pz"), split_axis=0, concat_axis=0, tiled=True)
+        own_force,
+        other_force,
+    )
+    returned = lax.all_to_all(solved, ("px", "zh", "zl"), split_axis=0, concat_axis=0, tiled=True)
     velocity_planes, mode_part = pl.pallas_call(
         functools.partial(gather_kernel, **sizes),
         out_shape=(
@@ -694,20 +749,25 @@
 
 
 def solution(mesh):
+    groups, px_count, pz_count = mesh.devices.shape
+    halves = jax.sharding.Mesh(
+        mesh.devices.reshape(groups, px_count, 2, pz_count // 2), ("grp", "px", "zh", "zl")
+    )
+    slab = ("px", "zh", "zl")
     in_specs = (
-        P(("px", "pz"), None),
-        P(("px", "pz")),
-        P(("px", "pz"), None),
-        P(("px", "pz"), None),
-        P(("px", "pz"), None),
-        P(None, ("px", "pz"), None),
-        P(None, ("px", "pz"), None),
-        P(None, None, ("grp", "pz"), None, "px"),
+        P(slab, None),
+        P(slab),
+        P(slab, None),
+        P(slab, None),
+        P(slab, None),
+        P(None, slab, None),
+        P(None, slab, None),
+        P(None, None, ("grp", "zh", "zl"), None, "px"),
         P(),
         P(),
         P(),
     )
-    out_specs = (P(("px", "pz"), None, "grp", None, None), P(None, ("px", "pz"), None))
+    out_specs = (P(slab, None, "grp", None, None), P(None, slab, None))
     return jax.shard_map(
-        on_device, mesh=mesh, in_specs=in_specs, out_specs=out_specs, check_vma=False
-    )
+        on_device, mesh=halves, in_specs=in_specs, out_specs=out_specs, check_vma=False
+    )

time: 131 us -> 148 us (1.13)
  Pallas kernels: 42.2 us -> 54.1 us
  starting transfers between devices: 13.1 us -> 23.3 us
  waiting for transfers between devices: 61.2 us -> 52.2 us
  local copies, waits for them, and re-layouts: 7.88 us -> 12 us
    all_to_all x2 -> x3, waiting for transfers between devices: 56.2 us -> 31.9 us  [the longest x1 31.9 us: on_device(): lax.all_to_all(solved, ('px', 'zh', 'zl'), split_axis=0, concat_axis=0, t...]
    ppermute x0 -> x2, waiting for transfers between devices: none -> 15.2 us  [the longest x1 15.2 us: on_device(): other_block = lax.ppermute(block_index, 'zh', swap)]
    pallas_call x1 -> x4, Pallas kernels: 15.2 us -> 27.2 us  [the longest x1 12.6 us: on_device(): spread_own(block_index, first_wave, pack, spread_order, *seeds)]
    all_to_all x2 -> x3, starting transfers between devices: 11.5 us -> 18.9 us  [the longest x1 6.85 us: on_device(): lax.all_to_all(other_outgoing, ('px', 'zl'), split_axis=0, concat_axis=0,...]
    ppermute x0 -> x2, starting transfers between devices: none -> 2.92 us  [the longest x1 2.6 us: on_device(): other_pack = lax.ppermute(pack, 'zh', swap)]
    unnamed x32 -> x49, local copies, waits for them, and re-layouts: 3.74 us -> 5.79 us
    reshape x0 -> x2, local copies, waits for them, and re-layouts: none -> 1.98 us  [the longest x1 0.99 us: on_device(): lax.dynamic_slice_in_dim(by_half, half_index, 1, 2).reshape(rows, rows // 2)]
  transfers between devices with their start and end apart: 3 -> 6, of which waited for: 3 -> 3; matrix products, arithmetic and copies ran while one was open for 6% -> 7% of each run, Pallas kernels for 6% -> 14%
where the time goes in v2:
time: 148 us
  Pallas kernels  54.1 us (37%)
  waiting for transfers between devices  52.2 us (35%)
  starting transfers between devices  23.3 us (16%)
  local copies, waits for them, and re-layouts  12 us (8%)
  other arithmetic  5.03 us (3%)
    all_to_all x1, waiting for transfers between devices, on_device(): lax.all_to_all(solved, ('px', 'zh', 'zl'), split_axis=0, concat_axis=0, t...  31.9 us
    ppermute x1, waiting for transfers between devices, on_device(): other_block = lax.ppermute(block_index, 'zh', swap)  15.2 us
    pallas_call x1, Pallas kernels, on_device(): spread_own(block_index, first_wave, pack, spread_order, *seeds)  12.6 us
    pallas_call x1, Pallas kernels, on_device(): pl.pallas_call(functools.partial(spread_kernel, makes_table=False, **spre...  11.3 us
    pallas_call x1, Pallas kernels, on_device(): pl.pallas_call(functools.partial(gather_kernel, **sizes), out_shape=(jax....  10.3 us
    pallas_call x1, Pallas kernels, on_device(): pl.pallas_call(solve_kernel, out_shape=jax.ShapeDtypeStruct((slabs, slab_...  8.82 us
    all_to_all x1, starting transfers between devices, on_device(): lax.all_to_all(other_outgoing, ('px', 'zl'), split_axis=0, concat_axis=0,...  6.85 us
    all_to_all x1, starting transfers between devices, on_device(): lax.all_to_all(solved, ('px', 'zh', 'zl'), split_axis=0, concat_axis=0, t...  6.72 us
  transfers between devices with their start and end apart: 6, of which 3 were waited for; matrix products, arithmetic and copies ran while one was open for 7% of the time, Pallas kernels for 14%

profile of v2, /device:TPU:0, one launch (start us, length us, event | category | flops | bytes accessed | tf_op | source)
XLA Modules:
  0.0 147.6 jit_solution(10408761718740268910)
XLA Ops:
  0.6 0.0 copy-start.13
  0.7 2.2 %pack.1.refs_2_ = bf16[6,64,512]{2,1,0:T(8,128)(2,1)} custom-call(s32[64,512]{1,0:T(8,128)} %cell_ref.3, f32[64,512]{1,0:T(8,128)} %volume_ref.1, f32[64,512]{1,0:T(8,128)} %rate_ref.1, f32[64,512]{1,0:T(8,128)} %place_ref.3, f32[3,64,512]{2,1,0:T(8,128)} %motion_ref.1, f32[3,64,512]{2,1,0:T(8,128)} %seen_ref.1), custom_call_target="tpu_custom_call" | custom-call | tf_op jit(solution)/shard_map/pack/pallas_call | solution.py:562
  2.9 12.6 %spread.1 = (bf16[8,32,1536]{2,1,0:T(8,128)(2,1)}, bf16[2,1024,1024]{2,1,0:T(8,128)(2,1)}) custom-call(s32[64]{0:T(128)} %block_ref.1, s32[1]{0:T(128)} %bitcast.3.refs_1_, bf16[6,64,512]{2,1,0:T(8,128)(2,1)} %pack.1.refs_2_, bf16[384,512]{1,0:T(8,128)(2,1)} %constant.96.clone.refs_3_, f32[8,1024]{1,0:T(8,128)} %constant.97.clone.refs_4_, ...), custom_call_target="tpu_custom_call" | custom-call | tf_op jit(solution)/shard_map/spread/pallas_call | solution.py:609
  15.4 5.3 %all-to-all-start = ((bf16[8,32,1536]{2,1,0:T(8,128)(2,1)}), bf16[8,32,1536]{2,1,0:T(8,128)(2,1)S(1)}, u32[]{:S(2)}, u32[]{:S(2)}) async-start(bf16[8,32,1536]{2,1,0:T(8,128)(2,1)} %get-tuple-element.6), calls=%async_computation | async-start | bytes 1572864 | tf_op jit(solution)/shard_map/all_to_all | solution.py:610
  20.7 2.6 %collective-permute-start.1 = (bf16[6,64,512]{2,1,0:T(8,128)(2,1)}, bf16[6,64,512]{2,1,0:T(8,128)(2,1)S(1)}, u32[]{:S(2)}, u32[]{:S(2)}) collective-permute-start(bf16[6,64,512]{2,1,0:T(8,128)(2,1)} %pack.1.refs_2_), channel_id=1, source_target_pairs={{0,2},{2,0},{1,3},{3,1},{4,6},{6,4},{5,7},{7,5},{8,10},{10,8},{9,1... | collective-permute-start | bytes 1179656 | tf_op jit(solution)/shard_map/ppermute | solution.py:577
  23.3 0.3 collective-permute-start
  23.6 15.2 %collective-permute-done.refs_0_ = s32[64]{0:T(128)S(1)} collective-permute-done((s32[64]{0:T(128)S(1)}, s32[64]{0:T(128)S(1)}, u32[]{:S(2)}, u32[]{:S(2)}) %collective-permute-start) | collective-permute-done | bytes 288 | tf_op jit(solution)/shard_map/ppermute | solution.py:578
  38.8 0.0 collective-permute-done.1.refs_2_
  38.8 0.6 copy-done.22
  39.4 0.2 copy-done.20
  39.6 11.3 %spread_other.1 = bf16[8,32,1536]{2,1,0:T(8,128)(2,1)} custom-call(s32[64]{0:T(128)} %copy-done.22, s32[1]{0:T(128)} %bitcast.3.refs_1_, bf16[6,64,512]{2,1,0:T(8,128)(2,1)} %copy-done.20, bf16[384,512]{1,0:T(8,128)(2,1)} %constant.96.clone.refs_3_, bf16[2,1024,1024]{2,1,0:T(8,128)(2,1)} %get-tuple-element.7.refs_4_), custom_call_target="tpu_custom_call" | custom-call | tf_op jit(solution)/shard_map/spread_other/pallas_call | solution.py:611
  50.9 0.0 all-to-all-done.own_force_ref
  50.9 0.0 copy-start.3
  50.9 6.9 %all-to-all-start.1 = ((bf16[8,32,1536]{2,1,0:T(8,128)(2,1)}), bf16[8,32,1536]{2,1,0:T(8,128)(2,1)}, u32[]{:S(2)}, u32[]{:S(2)}) async-start(bf16[8,32,1536]{2,1,0:T(8,128)(2,1)} %spread_other.1), calls=%async_computation.1 | async-start | bytes 1572864 | tf_op jit(solution)/shard_map/all_to_all | solution.py:619
  57.8 0.3 copy.26
  58.1 0.1 constant_dynamic-slice_fusion.1
  58.2 1.0 copy.27
  59.2 1.0 copy.28
  60.2 0.0 copy-start.8
  60.2 4.2 %reshape.79.state_ref = f32[512,1536]{1,0:T(8,128)S(1)} reshape(f32[512,3,1,2,256]{4,3,2,1,0:T(2,128)} %param.29) | data formatting | bytes 6291456 | tf_op jit(solution)/shard_map/reshape | solution.py:643
  64.4 1.4 fusion.2
  65.8 0.0 copy-start.21
  65.8 0.0 copy-start.15
  65.8 0.0 copy-start.18
  65.8 5.8 %project.1.state_ref = f32[512,1536]{1,0:T(8,128)S(1)} custom-call(bf16[512,512]{1,0:T(8,128)(2,1)S(1)} %get-tuple-element.11.high_ref, bf16[512,512]{1,0:T(8,128)(2,1)S(1)} %get-tuple-element.10.low_ref, bf16[256,256]{1,0:T(8,128)(2,1)S(1)} %copy-done.8, f32[512,1536]{1,0:T(8,128)S(1)} %reshape.79.state_ref), custom_call_target="tpu_custom_call" | custom-call | tf_op jit(solution)/shard_map/project/pallas_call | solution.py:646
  71.6 0.0 copy-start.1
  71.6 1.7 %copy-done.1 = f32[512,1536]{1,0:T(8,128)} copy-done((f32[512,1536]{1,0:T(8,128)}, f32[512,1536]{1,0:T(8,128)S(1)}, u32[]{:S(2)}) %copy-start.1) | copy-done | bytes 3145752
  73.3 1.2 add_divide_fusion.damping_ref
  74.5 1.6 %fusion = (bf16[512,512]{1,0:T(8,128)(2,1)}, bf16[512,512]{1,0:T(8,128)(2,1)}, bf16[512,512]{1,0:T(8,128)(2,1)}, bf16[512,512]{1,0:T(8,128)(2,1)}) fusion(f32[512,256]{1,0:T(8,128)S(1)} %copy-done.16, f32[512,256]{1,0:T(8,128)S(1)} %copy-done.15, f32[512,512]{1,0:T(8,128)S(1)} %copy-done.18), kind=kLoop, calls=%fused_computation.6 | loop fusion | flops 2359296 | bytes 4194304 | tf_op jit(solution)/shard_map/convert_element_type | solution.py:633
  76.0 0.0 all-to-all-done.1.other_force_ref
  76.0 8.8 %solve.1 = bf16[16,32,1536]{2,1,0:T(8,128)(2,1)} custom-call(bf16[512,512]{1,0:T(8,128)(2,1)} %get-tuple-element.15.inverse_high_ref, bf16[512,512]{1,0:T(8,128)(2,1)} %get-tuple-element.14.inverse_low_ref, bf16[512,512]{1,0:T(8,128)(2,1)} %get-tuple-element.18.basis_high_ref, bf16[512,512]{1,0:T(8,128)(2,1)} %get-tuple-element.19.basis_low_ref, ...), custom_call_target="tpu_custom_call" | custom-call | tf_op jit(solution)/shard_map/solve/pallas_call | solution.py:687
  84.9 0.0 copy-start.6
  84.9 0.0 copy-start.9
  84.9 0.0 copy-start.10
  84.9 0.0 copy-start.11
  84.9 0.0 copy-start.12
  84.9 6.7 %all-to-all-start.2 = ((bf16[16,32,1536]{2,1,0:T(8,128)(2,1)}), bf16[16,32,1536]{2,1,0:T(8,128)(2,1)S(1)}, u32[]{:S(2)}, u32[]{:S(2)}) async-start(bf16[16,32,1536]{2,1,0:T(8,128)(2,1)} %solve.1), calls=%async_computation.2 | async-start | bytes 3145728 | tf_op jit(solution)/shard_map/all_to_all | solution.py:710
  91.7 0.0 copy-start.5
  91.7 0.0 copy-start.7
  91.7 1.2 phases.1.phase_ref
  92.9 1.0 copy-done.2
  93.9 2.0 %waves.1.table_ref = bf16[2,1024,1024]{2,1,0:T(8,128)(2,1)S(1)} custom-call(f32[2,8,1024]{2,1,0:T(8,128)S(1)} %copy-done.9, f32[2,8,1024]{2,1,0:T(8,128)S(1)} %copy-done.10, f32[8,1024]{1,0:T(8,128)S(1)} %copy-done.11, f32[8,1024]{1,0:T(8,128)S(1)} %copy-done.12), custom_call_target="tpu_custom_call" | custom-call | tf_op jit(solution)/shard_map/waves/pallas_call | solution.py:677
  95.9 2.0 %copy-done = bf16[2,1024,1024]{2,1,0:T(8,128)(2,1)} copy-done((bf16[2,1024,1024]{2,1,0:T(8,128)(2,1)}, bf16[2,1024,1024]{2,1,0:T(8,128)(2,1)S(1)}, u32[]{:S(2)}) %copy-start) | copy-done | bytes 4194328
  97.8 31.9 %all-to-all-done.2.back_ref = bf16[16,32,1536]{2,1,0:T(8,128)(2,1)S(1)} async-done(((bf16[16,32,1536]{2,1,0:T(8,128)(2,1)}), bf16[16,32,1536]{2,1,0:T(8,128)(2,1)S(1)}, u32[]{:S(2)}, u32[]{:S(2)}) %all-to-all-start.2) | async-done | bytes 1572896 | tf_op jit(solution)/shard_map/all_to_all | solution.py:710
  129.7 10.3 %gather.1 = (bf16[32,3,4,2,2048]{4,3,2,1,0:T(2,128)(2,1)}, bf16[3,64,512]{2,1,0:T(8,128)(2,1)S(1)}) custom-call(s32[64]{0:T(128)S(1)} %copy-done.13, s32[64,512]{1,0:T(8,128)S(1)} %copy-done.5, bf16[512,256]{1,0:T(8,128)(2,1)S(1)} %copy-done.7, bf16[2,1024,1024]{2,1,0:T(8,128)(2,1)} %copy-done, bf16[16,32,1536]{2,1,0:T(8,128)(2,1)S(1)} %all-to-all-done.2.back_ref, ...), custom_call_target="tpu_custom_call" | custom-call | tf_op jit(solution)/shard_map/gather/pallas_call | solution.py:711
  140.1 1.5 %collective-permute-start.2 = (bf16[3,64,512]{2,1,0:T(8,128)(2,1)S(1)}, bf16[3,64,512]{2,1,0:T(8,128)(2,1)S(1)}, u32[]{:S(2)}, u32[]{:S(2)}) collective-permute-start(bf16[3,64,512]{2,1,0:T(8,128)(2,1)S(1)} %get-tuple-element.9), channel_id=1, source_target_pairs={{0,16},{16,0},{1,17},{17,1},{2,18},{18,2},{3,19},{19,3},{4,20},{20... | collective-permute-start | bytes 589832 | tf_op jit(solution)/shard_map/ppermute | solution.py:740
  141.6 5.1 %collective-permute-done.2 = bf16[3,64,512]{2,1,0:T(8,128)(2,1)S(1)} collective-permute-done((bf16[3,64,512]{2,1,0:T(8,128)(2,1)S(1)}, bf16[3,64,512]{2,1,0:T(8,128)(2,1)S(1)}, u32[]{:S(2)}, u32[]{:S(2)}) %collective-permute-start.2) | collective-permute-done | bytes 196640 | tf_op jit(solution)/shard_map/ppermute | solution.py:740
  146.7 0.9 add_subtract_fusion
  (32 shorter events, 0.1 us)
Async XLA Ops:
  0.6 22.7 %copy-start.13 = (s32[64]{0:T(128)S(1)}, s32[64]{0:T(128)}, u32[]{:S(2)}) copy-start(s32[64]{0:T(128)} %block_ref.1) | copy-start | bytes 772
  15.4 35.5 %all-to-all-start = ((bf16[8,32,1536]{2,1,0:T(8,128)(2,1)}), bf16[8,32,1536]{2,1,0:T(8,128)(2,1)S(1)}, u32[]{:S(2)}, u32[]{:S(2)}) async-start(bf16[8,32,1536]{2,1,0:T(8,128)(2,1)} %get-tuple-element.6), calls=%async_computation | async-start | bytes 1572864 | tf_op jit(solution)/shard_map/all_to_all | solution.py:610
  20.7 18.1 %collective-permute-start.1 = (bf16[6,64,512]{2,1,0:T(8,128)(2,1)}, bf16[6,64,512]{2,1,0:T(8,128)(2,1)S(1)}, u32[]{:S(2)}, u32[]{:S(2)}) collective-permute-start(bf16[6,64,512]{2,1,0:T(8,128)(2,1)} %pack.1.refs_2_), channel_id=1, source_target_pairs={{0,2},{2,0},{1,3},{3,1},{4,6},{6,4},{5,7},{7,5},{8,10},{10,8},{9,1... | collective-permute-start | bytes 1179656 | tf_op jit(solution)/shard_map/ppermute | solution.py:577
  23.3 15.5 %collective-permute-start = (s32[64]{0:T(128)S(1)}, s32[64]{0:T(128)S(1)}, u32[]{:S(2)}, u32[]{:S(2)}) collective-permute-start(s32[64]{0:T(128)S(1)} %copy-done.13), channel_id=1, source_target_pairs={{0,2},{2,0},{1,3},{3,1},{4,6},{6,4},{5,7},{7,5},{8,10},{10,8},{9,1... | collective-permute-start | bytes 776 | tf_op jit(solution)/shard_map/ppermute | solution.py:578
  38.8 0.6 copy-start.22
  38.8 0.7 copy-start.20
  39.6 18.2 %copy-start.14 = (f32[512,512]{1,0:T(8,128)S(1)}, f32[512,512]{1,0:T(8,128)}, u32[]{:S(2)}) copy-start(f32[512,512]{1,0:T(8,128)} %param.31) | copy-start | bytes 3145732
  50.9 8.3 %copy-start.3 = (bf16[8,32,1536]{2,1,0:T(8,128)(2,1)}, bf16[8,32,1536]{2,1,0:T(8,128)(2,1)S(1)}, u32[]{:S(2)}) copy-start(bf16[8,32,1536]{2,1,0:T(8,128)(2,1)S(1)} %all-to-all-done.own_force_ref) | copy-start | bytes 2359300
  50.9 25.1 %all-to-all-start.1 = ((bf16[8,32,1536]{2,1,0:T(8,128)(2,1)}), bf16[8,32,1536]{2,1,0:T(8,128)(2,1)}, u32[]{:S(2)}, u32[]{:S(2)}) async-start(bf16[8,32,1536]{2,1,0:T(8,128)(2,1)} %spread_other.1), calls=%async_computation.1 | async-start | bytes 1572864 | tf_op jit(solution)/shard_map/all_to_all | solution.py:619
  60.2 5.6 %copy-start.8 = (bf16[256,256]{1,0:T(8,128)(2,1)S(1)}, bf16[256,256]{1,0:T(8,128)(2,1)}, u32[]{:S(2)}) copy-start(bf16[256,256]{1,0:T(8,128)(2,1)} %constant.101.clone.order_ref) | copy-start | bytes 393220
  65.8 7.5 %copy-start.21 = (f32[512]{0:T(512)S(1)}, f32[512]{0:T(512)}, u32[]{:S(2)}) copy-start(f32[512]{0:T(512)} %param.32) | copy-start | bytes 6148
  65.8 8.7 %copy-start.15 = (f32[512,256]{1,0:T(8,128)S(1)}, f32[512,256]{1,0:T(8,128)}, u32[]{:S(2)}) copy-start(f32[512,256]{1,0:T(8,128)} %copy.27) | copy-start | bytes 1572868
  65.8 8.6 %copy-start.16 = (f32[512,256]{1,0:T(8,128)S(1)}, f32[512,256]{1,0:T(8,128)}, u32[]{:S(2)}) copy-start(f32[512,256]{1,0:T(8,128)} %copy.28) | copy-start | bytes 1572868
  65.8 8.6 %copy-start.18 = (f32[512,512]{1,0:T(8,128)S(1)}, f32[512,512]{1,0:T(8,128)}, u32[]{:S(2)}) copy-start(f32[512,512]{1,0:T(8,128)} %param.30) | copy-start | bytes 3145732
  71.6 1.7 %copy-start.1 = (f32[512,1536]{1,0:T(8,128)}, f32[512,1536]{1,0:T(8,128)S(1)}, u32[]{:S(2)}) copy-start(f32[512,1536]{1,0:T(8,128)S(1)} %project.1.state_ref) | copy-start | bytes 9437188
  73.3 2.8 %copy-start.4 = (bf16[8,32,1536]{2,1,0:T(8,128)(2,1)S(1)}, bf16[8,32,1536]{2,1,0:T(8,128)(2,1)}, u32[]{:S(2)}) copy-start(bf16[8,32,1536]{2,1,0:T(8,128)(2,1)} %copy-done.3) | copy-start | bytes 2359300
  84.9 6.8 %copy-start.6 = (f32[64,512]{1,0:T(8,128)S(1)}, f32[64,512]{1,0:T(8,128)}, u32[]{:S(2)}) copy-start(f32[64,512]{1,0:T(8,128)} %place_ref.3) | copy-start | bytes 393220
  84.9 9.0 %copy-start.9 = (f32[2,8,1024]{2,1,0:T(8,128)S(1)}, f32[2,8,1024]{2,1,0:T(8,128)}, u32[]{:S(2)}) copy-start(f32[2,8,1024]{2,1,0:T(8,128)} %constant.102.clone.base_cos_ref) | copy-start | bytes 196612
  84.9 9.0 %copy-start.10 = (f32[2,8,1024]{2,1,0:T(8,128)S(1)}, f32[2,8,1024]{2,1,0:T(8,128)}, u32[]{:S(2)}) copy-start(f32[2,8,1024]{2,1,0:T(8,128)} %constant.103.clone.base_sin_ref) | copy-start | bytes 196612
  84.9 9.0 %copy-start.11 = (f32[8,1024]{1,0:T(8,128)S(1)}, f32[8,1024]{1,0:T(8,128)}, u32[]{:S(2)}) copy-start(f32[8,1024]{1,0:T(8,128)} %constant.104.clone.step_cos_ref) | copy-start | bytes 98308
  84.9 9.0 %copy-start.12 = (f32[8,1024]{1,0:T(8,128)S(1)}, f32[8,1024]{1,0:T(8,128)}, u32[]{:S(2)}) copy-start(f32[8,1024]{1,0:T(8,128)} %constant.105.clone.step_sin_ref) | copy-start | bytes 98308
  84.9 44.8 %all-to-all-start.2 = ((bf16[16,32,1536]{2,1,0:T(8,128)(2,1)}), bf16[16,32,1536]{2,1,0:T(8,128)(2,1)S(1)}, u32[]{:S(2)}, u32[]{:S(2)}) async-start(bf16[16,32,1536]{2,1,0:T(8,128)(2,1)} %solve.1), calls=%async_computation.2 | async-start | bytes 3145728 | tf_op jit(solution)/shard_map/all_to_all | solution.py:710
  91.7 38.1 %copy-start.5 = (s32[64,512]{1,0:T(8,128)S(1)}, s32[64,512]{1,0:T(8,128)}, u32[]{:S(2)}) copy-start(s32[64,512]{1,0:T(8,128)} %cell_ref.3) | copy-start | bytes 393220
  91.7 38.1 %copy-start.7 = (bf16[512,256]{1,0:T(8,128)(2,1)S(1)}, bf16[512,256]{1,0:T(8,128)(2,1)}, u32[]{:S(2)}) copy-start(bf16[512,256]{1,0:T(8,128)(2,1)} %constant.106.clone.order_ref) | copy-start | bytes 786436
  92.9 1.0 copy-start.2
  95.8 2.0 %copy-start = (bf16[2,1024,1024]{2,1,0:T(8,128)(2,1)}, bf16[2,1024,1024]{2,1,0:T(8,128)(2,1)S(1)}, u32[]{:S(2)}) copy-start(bf16[2,1024,1024]{2,1,0:T(8,128)(2,1)S(1)} %waves.1.table_ref) | copy-start | bytes 12582916
  97.8 43.8 %copy-start.19 = (f32[64,512]{1,0:T(8,128)S(1)}, f32[64,512]{1,0:T(8,128)}, u32[]{:S(2)}) copy-start(f32[64,512]{1,0:T(8,128)} %rate_ref.1) | copy-start | bytes 393220
  97.8 48.9 %copy-start.17 = (f32[3,64,512]{2,1,0:T(8,128)S(1)}, f32[3,64,512]{2,1,0:T(8,128)}, u32[]{:S(2)}) copy-start(f32[3,64,512]{2,1,0:T(8,128)} %motion_ref.1) | copy-start | bytes 1179652
  140.1 6.7 %collective-permute-start.2 = (bf16[3,64,512]{2,1,0:T(8,128)(2,1)S(1)}, bf16[3,64,512]{2,1,0:T(8,128)(2,1)S(1)}, u32[]{:S(2)}, u32[]{:S(2)}) collective-permute-start(bf16[3,64,512]{2,1,0:T(8,128)(2,1)S(1)} %get-tuple-element.9), channel_id=1, source_target_pairs={{0,16},{16,0},{1,17},{17,1},{2,18},{18,2},{3,19},{19,3},{4,20},{20... | collective-permute-start | bytes 589832 | tf_op jit(solution)/shard_map/ppermute | solution.py:740

commit v3 on v1

--- a/solution.py
+++ b/solution.py
@@ -12,8 +12,9 @@
 NX = 2048
 KX = 1024
 CB = 256
-HALF = NX // 2
-PAIR = KX // 2
+SPLIT = 4
+POINTS = NX // SPLIT
+WAVES = KX // SPLIT
 TILE_GROUP = 8
 
 time_step = 0.5
@@ -28,7 +29,7 @@
 
 
 def forward_seeds():
-    waves = np.concatenate([2 * np.arange(PAIR) - KX // 2, 2 * np.arange(PAIR) + 1 - KX // 2])
+    waves = np.concatenate([SPLIT * np.arange(WAVES) + rest - KX // 2 for rest in range(SPLIT)])
     base = turns(np.arange(8), waves)
     steps = turns(8 * 2 ** np.arange(8), waves)
     scale = np.float32(1.0 / math.sqrt(NX))
@@ -36,9 +37,11 @@
 
 
 def inverse_seeds():
-    points = np.arange(HALF)
-    bases = [turns(2 * np.arange(8) + parity - KX // 2, points) for parity in range(2)]
-    steps = turns(16 * 2 ** np.arange(8), points)
+    points = np.arange(POINTS)
+    bases = [
+        turns(SPLIT * np.arange(8) + rest - KX // 2, points) for rest in range(SPLIT)
+    ]
+    steps = turns(8 * SPLIT * 2 ** np.arange(8), points)
     scale = np.float32(1.0 / math.sqrt(NX))
     cosines = np.stack([b[0] for b in bases]) * scale
     sines = np.stack([b[1] for b in bases]) * scale
@@ -48,8 +51,8 @@
 def order_matrix(waves):
     matrix = np.zeros((waves, waves), np.float32)
     lanes = np.arange(waves)
-    half = waves // 2
-    matrix[2 * (lanes % half) + lanes // half, lanes] = 1.0
+    span = waves // SPLIT
+    matrix[SPLIT * (lanes % span) + lanes // span, lanes] = 1.0
     return matrix
 
 
@@ -118,7 +121,6 @@
     step_sin_ref,
     order_ref,
     out_ref,
-    phase_out_ref,
     field,
     table_cos,
     table_sin,
@@ -126,9 +128,7 @@
     left,
     amounts,
     phases,
-    phases_out,
     packed,
-    phase_sem,
     out_sem,
     *,
     half_modes,
@@ -142,25 +142,13 @@
     component_rows = slab_rows * group_rows
     pz_count = half_modes // pencil_modes
 
-    place = place_ref[...]
     first = (group_ref[0] * half_modes + 1).astype(jnp.float32)
-    cos_one = jnp.cos(place)
-    sin_one = jnp.sin(place)
-    cos_now = jnp.cos(place * first)
-    sin_now = jnp.sin(place * first)
-    for mode in range(half_modes):
+    for mode, (cosine, sine) in enumerate(turn_modes(place_ref[...], first, half_modes)):
         for piece in range(size // 128):
             lanes = slice(piece * 128, (piece + 1) * 128)
-            for part, value in ((0, cos_now[:, lanes]), (1, -sin_now[:, lanes])):
-                phases[piece, pl.ds(part * half_modes + mode, tiles, stride=group_rows), :] = value
-                phases_out[piece, pl.ds(2 * mode + part, tiles, stride=group_rows), :] = value
-        if mode + 1 < half_modes:
-            cos_now, sin_now = (
-                cos_now * cos_one - sin_now * sin_one,
-                sin_now * cos_one + cos_now * sin_one,
-            )
-    phase_copy = pltpu.make_async_copy(phases_out, phase_out_ref, phase_sem)
-    phase_copy.start()
+            for part, value in ((0, cosine), (1, -sine)):
+                rows = pl.ds(part * half_modes + mode, tiles, stride=group_rows)
+                phases[piece, rows, :] = value[:, lanes]
 
     upper = cell_ref[...] >= 128
     volume = volume_ref[...]
@@ -177,12 +165,12 @@
         table_sin,
         (base_cos_ref[...], base_sin_ref[...]),
         (step_cos_ref, step_sin_ref),
-        HALF,
-    )
-    for parity in range(2):
-        lanes = slice(parity * PAIR, (parity + 1) * PAIR)
-        table[parity, :, 0:PAIR] = table_cos[:, lanes].astype(jnp.bfloat16)
-        table[parity, :, PAIR:KX] = table_sin[:, lanes].astype(jnp.bfloat16)
+        POINTS,
+    )
+    for rest in range(SPLIT):
+        lanes = slice(rest * WAVES, (rest + 1) * WAVES)
+        table[rest, :, 0:WAVES] = table_cos[:, lanes].astype(jnp.bfloat16)
+        table[rest, :, WAVES:] = table_sin[:, lanes].astype(jnp.bfloat16)
 
     def clear(index, carry):
         field[index] = jnp.zeros(field.shape[1:], jnp.float32)
@@ -228,42 +216,47 @@
     lax.fori_loop(0, tiles // TILE_GROUP, tile_group, 0)
 
     order = order_ref[...]
-    part_sign = jnp.where(
-        lax.broadcasted_iota(jnp.int32, (slab_rows, group_rows, PAIR), 1) < half_modes, 1.0, -1.0
-    )
-    half_waves = pencil_waves // 2
+    def times_minus_i(value):
+        lanes = value.shape[1]
+        value = value.reshape(slab_rows, group_rows, lanes)
+        part = lax.broadcasted_iota(jnp.int32, value.shape, 1) // half_modes
+        moved = pltpu.roll(value, half_modes, 1)
+        return jnp.where(part == 0, moved, -moved).reshape(component_rows, lanes)
+
+    rest_waves = pencil_waves // SPLIT
     copies = []
     for component in range(3):
         rows = slice(component * component_rows, (component + 1) * component_rows)
-        for strip in range(HALF // 128):
-            low = field[strip, rows, :]
-            high = field[strip + HALF // 128, rows, :]
+        for strip in range(POINTS // 128):
+            values = [field[strip + j * (POINTS // 128), rows, :] for j in range(SPLIT)]
             lanes = slice(strip * 128, (strip + 1) * 128)
-            left[0, :, lanes] = (low + high).astype(jnp.bfloat16)
-            left[1, :, lanes] = (low - high).astype(jnp.bfloat16)
-        for parity in range(2):
-            product = dot32(left[parity], table[parity])
-            turned = product[:, PAIR:].reshape(slab_rows, group_rows, PAIR)
-            turned = pltpu.roll(turned, half_modes, 1) * part_sign
-            spectrum = (product[:, :PAIR] + turned.reshape(component_rows, PAIR)).astype(
-                jnp.bfloat16
-            )
-            spectrum = dot32(order, spectrum).astype(jnp.bfloat16)
-            for owner_px in range(KX // pencil_waves):
-                for part in range(2):
-                    for mode in range(half_modes):
-                        column = (
-                            (component * pencil_modes + mode % pencil_modes) * 2 + part
-                        ) * pencil_waves + parity * half_waves
-                        row = (part * half_modes + mode) * slab_rows
-                        packed[
-                            owner_px * pz_count + mode // pencil_modes,
-                            :,
-                            column : column + half_waves,
-                        ] = spectrum[
-                            row : row + slab_rows,
-                            owner_px * half_waves : (owner_px + 1) * half_waves,
-                        ]
+            even_sum = values[0] + values[2]
+            odd_sum = values[1] + values[3]
+            even_gap = values[0] - values[2]
+            odd_gap = times_minus_i(values[1] - values[3])
+            left[0, :, lanes] = (even_sum + odd_sum).astype(jnp.bfloat16)
+            left[1, :, lanes] = (even_gap + odd_gap).astype(jnp.bfloat16)
+            left[2, :, lanes] = (even_sum - odd_sum).astype(jnp.bfloat16)
+            left[3, :, lanes] = (even_gap - odd_gap).astype(jnp.bfloat16)
+        spectra = []
+        for rest in range(SPLIT):
+            product = dot32(left[rest], table[rest])
+            spectrum = product[:, :WAVES] + times_minus_i(product[:, WAVES:])
+            spectra.append(dot32(order, spectrum.astype(jnp.bfloat16)).astype(jnp.bfloat16))
+        for owner_px in range(KX // pencil_waves):
+            own = slice(owner_px * rest_waves, (owner_px + 1) * rest_waves)
+            joined = jnp.concatenate([spectrum[:, own] for spectrum in spectra], axis=1)
+            for part in range(2):
+                for mode in range(half_modes):
+                    column = (
+                        (component * pencil_modes + mode % pencil_modes) * 2 + part
+                    ) * pencil_waves
+                    row = (part * half_modes + mode) * slab_rows
+                    packed[
+                        owner_px * pz_count + mode // pencil_modes,
+                        :,
+                        column : column + pencil_waves,
+                    ] = joined[row : row + slab_rows]
         span = 2 * pencil_modes * pencil_waves
         lanes = pl.ds(component * span, span)
         copy = pltpu.make_async_copy(
@@ -273,20 +266,45 @@
         copies.append(copy)
     for copy in copies:
         copy.wait()
-    phase_copy.wait()
 
 
 def table_kernel(base_cos_ref, base_sin_ref, step_cos_ref, step_sin_ref, out_ref, work_cos, work_sin):
-    for parity in range(2):
+    for rest in range(SPLIT):
         grow(
             work_cos,
             work_sin,
-            (base_cos_ref[parity], base_sin_ref[parity]),
+            (base_cos_ref[rest], base_sin_ref[rest]),
             (step_cos_ref, step_sin_ref),
-            PAIR,
+            WAVES,
         )
-        out_ref[parity, 0:PAIR, :] = work_cos[...].astype(jnp.bfloat16)
-        out_ref[parity, PAIR:KX, :] = work_sin[...].astype(jnp.bfloat16)
+        out_ref[rest, 0:WAVES, :] = work_cos[...].astype(jnp.bfloat16)
+        out_ref[rest, WAVES:, :] = work_sin[...].astype(jnp.bfloat16)
+
+
+def turn_modes(place, first, modes):
+    cos_one = jnp.cos(place)
+    sin_one = jnp.sin(place)
+    cos_now = jnp.cos(place * first)
+    sin_now = jnp.sin(place * first)
+    turned = [(cos_now, sin_now)]
+    for _ in range(modes - 1):
+        cos_now, sin_now = (
+            cos_now * cos_one - sin_now * sin_one,
+            sin_now * cos_one + cos_now * sin_one,
+        )
+        turned.append((cos_now, sin_now))
+    return turned
+
+
+def phase_kernel(group_ref, place_ref, out_ref, *, half_modes):
+    tiles, size = place_ref.shape
+    first = (group_ref[0] * half_modes + 1).astype(jnp.float32)
+    for mode, (cosine, sine) in enumerate(turn_modes(place_ref[...], first, half_modes)):
+        for piece in range(size // 128):
+            lanes = slice(piece * 128, (piece + 1) * 128)
+            for part, value in ((0, cosine), (1, -sine)):
+                rows = pl.ds(2 * mode + part, tiles, stride=2 * half_modes)
+                out_ref[piece, rows, :] = value[:, lanes]
 
 
 def split(value):
@@ -308,7 +326,6 @@
 
 def solve_kernel(
     inverse_high_ref,
-    inverse_low_ref,
     basis_high_ref,
     basis_low_ref,
     damping_ref,
@@ -318,7 +335,9 @@
     matrices,
     damping,
     state,
+    results,
     sems,
+    out_sems,
 ):
     rows, step = damping_ref.shape
     columns = force_ref.shape[-1]
@@ -327,11 +346,10 @@
     spans = [pl.ds(start, step) for start in range(0, columns, step)]
     loads = [
         (inverse_high_ref, matrices.at[0]),
-        (inverse_low_ref, matrices.at[1]),
         (state_ref.at[:, spans[0]], state.at[:, spans[0]]),
         (damping_ref, damping),
-        (basis_high_ref, matrices.at[2]),
-        (basis_low_ref, matrices.at[3]),
+        (basis_high_ref, matrices.at[1]),
+        (basis_low_ref, matrices.at[2]),
     ] + [(state_ref.at[:, span], state.at[:, span]) for span in spans[1:]]
     copies = [
         pltpu.make_async_copy(source, target, sems.at[index])
@@ -339,27 +357,33 @@
     ]
     for copy in copies:
         copy.start()
+    stores = []
     for index, start in enumerate(range(0, columns, step)):
         lanes = slice(start, start + step)
         force = force_rows[:, lanes]
         if index == 0:
             copies[0].wait()
-            copies[1].wait()
-        pushed = dot32(matrices[0], force) + dot32(matrices[1], force)
-        copies[2 if index == 0 else 5 + index].wait()
+        pushed = dot32(matrices[0], force)
+        copies[1 if index == 0 else 4 + index].wait()
+        if index == 0:
+            copies[2].wait()
+        modal_high, modal_low = split((state[:, lanes] + time_step * pushed) * damping[...])
         if index == 0:
             copies[3].wait()
-        modal = (state[:, lanes] + time_step * pushed) * damping[...]
-        modal_high, modal_low = split(modal)
-        if index == 0:
             copies[4].wait()
-            copies[5].wait()
         solved = (
-            dot32(matrices[2], modal_high)
-            + dot32(matrices[2], modal_low)
-            + dot32(matrices[3], modal_high)
+            dot32(matrices[1], modal_high)
+            + dot32(matrices[1], modal_low)
+            + dot32(matrices[2], modal_high)
         )
-        out_ref[:, :, lanes] = solved.astype(jnp.bfloat16).reshape(slab_shape + (step,))
+        results[:, :, lanes] = solved.astype(jnp.bfloat16).reshape(slab_shape + (step,))
+        copy = pltpu.make_async_copy(
+            results.at[:, :, spans[index]], out_ref.at[:, :, spans[index]], out_sems.at[index]
+        )
+        copy.start()
+        stores.append(copy)
+    for copy in stores:
+        copy.wait()
 
 
 def merge_rows(values):
@@ -411,16 +435,25 @@
     group_rows = 2 * half_modes
     slab_rows = back_ref.shape[1]
     pz_count = half_modes // pencil_modes
-    half_waves = pencil_waves // 2
     component_rows = group_rows * slab_rows
     table_copies = [
-        pltpu.make_async_copy(table_ref.at[parity], table.at[parity], table_sem.at[parity])
-        for parity in range(2)
+        pltpu.make_async_copy(table_ref.at[rest], table.at[rest], table_sem.at[rest])
+        for rest in range(SPLIT)
     ]
     for copy in table_copies:
         copy.start()
     phase_copy = pltpu.make_async_copy(phase_ref, phases, phase_sem)
     phase_copy.start()
+    rest_waves = pencil_waves // SPLIT
+
+    def times_i(value):
+        shape = value.shape
+        value = value.reshape(shape[0] // 8, 8, shape[1])
+        part = lax.broadcasted_iota(jnp.int32, value.shape, 1) % 2
+        return jnp.where(
+            part == 0, -pltpu.roll(value, 7, 1), pltpu.roll(value, 1, 1)
+        ).reshape(shape)
+
     copies = []
     for component in range(3):
         rows = []
@@ -429,38 +462,45 @@
                 column = (
                     (component * pencil_modes + mode % pencil_modes) * 2 + part
                 ) * pencil_waves
-                pieces = []
-                for parity in range(2):
-                    for px in range(KX // pencil_waves):
-                        first = column + parity * half_waves
-                        pieces.append(
-                            back_ref[
-                                px * pz_count + mode // pencil_modes,
-                                :,
-                                first : first + half_waves,
-                            ]
-                        )
-                rows.append(jnp.concatenate(pieces, axis=1))
+                sources = [
+                    back_ref[
+                        px * pz_count + mode // pencil_modes, :, column : column + pencil_waves
+                    ]
+                    for px in range(KX // pencil_waves)
+                ]
+                rows.append(
+                    jnp.concatenate(
+                        [
+                            source[:, rest * rest_waves : (rest + 1) * rest_waves]
+                            for rest in range(SPLIT)
+                            for source in sources
+                        ],
+                        axis=1,
+                    )
+                )
         turned = dot32(order_ref[...], jnp.concatenate(rows, axis=0)).astype(jnp.bfloat16)
-        for parity in range(2):
-            lanes = slice(parity * PAIR, (parity + 1) * PAIR)
-            left[parity, :, 0:PAIR] = turned[0:component_rows, lanes]
-            left[parity, :, PAIR:KX] = turned[component_rows:, lanes]
-        if component == 0:
-            table_copies[0].wait()
-        even = dot32(left[0], table[0])
-        if component == 0:
-            table_copies[1].wait()
-        odd = dot32(left[1], table[1])
-        for side in range(2):
-            plane = (even + odd if side == 0 else even - odd).astype(jnp.bfloat16)
+        results = []
+        for rest in range(SPLIT):
+            lanes = slice(rest * WAVES, (rest + 1) * WAVES)
+            left[rest, :, 0:WAVES] = turned[0:component_rows, lanes]
+            left[rest, :, WAVES:] = turned[component_rows:, lanes]
+            if component == 0:
+                table_copies[rest].wait()
+            results.append(dot32(left[rest], table[rest]))
+        even_sum = results[0] + results[2]
+        odd_sum = results[1] + results[3]
+        even_gap = results[0] - results[2]
+        odd_gap = times_i(results[1] - results[3])
+        quarters = [even_sum + odd_sum, even_gap + odd_gap, even_sum - odd_sum, even_gap - odd_gap]
+        for side, quarter in enumerate(quarters):
+            plane = quarter.astype(jnp.bfloat16)
             whole = plane.astype(jnp.float32)
-            planes[:, component, :, :, side * HALF : (side + 1) * HALF] = plane.reshape(
-                slab_rows, half_modes, 2, HALF
+            planes[:, component, :, :, side * POINTS : (side + 1) * POINTS] = plane.reshape(
+                slab_rows, half_modes, 2, POINTS
             )
-            for strip in range(HALF // 128):
+            for strip in range(POINTS // 128):
                 values[
-                    side * (HALF // 128) + strip,
+                    side * (POINTS // 128) + strip,
                     component * component_rows : (component + 1) * component_rows,
                     :,
                 ] = whole[:, strip * 128 : (strip + 1) * 128]
@@ -544,31 +584,27 @@
     in_hbm = functools.partial(pltpu.with_memory_space_constraint, memory_space=pltpu.HBM)
     phase_shape = (size // 128, tiles * 2 * half_modes, 128)
 
-    outgoing, phases = pl.pallas_call(
+    group = group_index.reshape(1).astype(jnp.int32)
+    outgoing = pl.pallas_call(
         functools.partial(spread_kernel, **sizes),
-        out_shape=(
-            jax.ShapeDtypeStruct((slabs, slab_rows, columns), jnp.bfloat16),
-            jax.ShapeDtypeStruct(phase_shape, jnp.float32),
-        ),
+        out_shape=jax.ShapeDtypeStruct((slabs, slab_rows, columns), jnp.bfloat16),
         in_specs=[smem, smem] + [vmem] * 11,
-        out_specs=(hbm, hbm),
+        out_specs=hbm,
         scratch_shapes=[
             pltpu.VMEM((NX // 128, slab_rows * width, 128), jnp.float32),
-            pltpu.VMEM((HALF, KX), jnp.float32),
-            pltpu.VMEM((HALF, KX), jnp.float32),
-            pltpu.VMEM((2, HALF, KX), jnp.bfloat16),
-            pltpu.VMEM((2, component_rows, HALF), jnp.bfloat16),
+            pltpu.VMEM((POINTS, KX), jnp.float32),
+            pltpu.VMEM((POINTS, KX), jnp.float32),
+            pltpu.VMEM((SPLIT, POINTS, 2 * WAVES), jnp.bfloat16),
+            pltpu.VMEM((SPLIT, component_rows, POINTS), jnp.bfloat16),
             pltpu.VMEM((6, tiles, size), jnp.float32),
             pltpu.VMEM(phase_shape, jnp.float32),
-            pltpu.VMEM(phase_shape, jnp.float32),
             pltpu.VMEM((slabs, slab_rows, columns), jnp.bfloat16),
-            pltpu.SemaphoreType.DMA,
             pltpu.SemaphoreType.DMA((3,)),
         ],
         name="spread",
     )(
         block_index,
-        group_index.reshape(1).astype(jnp.int32),
+        group,
         cell_index,
         volume,
         response_rate,
@@ -604,8 +640,8 @@
         name="project",
     )(inverse_high, inverse_low, jnp.asarray(order_matrix(pencil_waves), jnp.bfloat16), state)
     lane = jnp.arange(pencil_waves)
-    half_waves = pencil_waves // 2
-    wave = 2 * (lane % half_waves) + lane // half_waves
+    rest_waves = pencil_waves // SPLIT
+    wave = SPLIT * (lane % rest_waves) + lane // rest_waves
     stream_wave = (lax.axis_index("px") * pencil_waves + wave - KX // 2).astype(jnp.float32) * 0.5
     span_wave = (
         group_index * half_modes
@@ -622,30 +658,40 @@
     )
     table = pl.pallas_call(
         table_kernel,
-        out_shape=jax.ShapeDtypeStruct((2, KX, HALF), jnp.bfloat16),
+        out_shape=jax.ShapeDtypeStruct((SPLIT, 2 * WAVES, POINTS), jnp.bfloat16),
         in_specs=[vmem] * 4,
         out_specs=vmem,
-        scratch_shapes=[pltpu.VMEM((PAIR, HALF), jnp.float32)] * 2,
+        scratch_shapes=[pltpu.VMEM((WAVES, POINTS), jnp.float32)] * 2,
         compiler_params=pltpu.CompilerParams(vmem_limit_bytes=24 << 20),
         name="waves",
     )(*[jnp.asarray(seed) for seed in inverse_seeds()])
 
+    phases = pl.pallas_call(
+        functools.partial(phase_kernel, half_modes=half_modes),
+        out_shape=jax.ShapeDtypeStruct(phase_shape, jnp.float32),
+        in_specs=[smem, vmem],
+        out_specs=vmem,
+        compiler_params=pltpu.CompilerParams(vmem_limit_bytes=24 << 20),
+        name="phases",
+    )(group, spanwise_position)
+
     solved = pl.pallas_call(
         solve_kernel,
         out_shape=jax.ShapeDtypeStruct((slabs, slab_rows, columns), jnp.bfloat16),
-        in_specs=[hbm] * 6 + [vmem],
-        out_specs=vmem,
+        in_specs=[hbm] * 5 + [vmem],
+        out_specs=hbm,
         scratch_shapes=[
-            pltpu.VMEM((4, rows, rows), jnp.bfloat16),
+            pltpu.VMEM((3, rows, rows), jnp.bfloat16),
             pltpu.VMEM((rows, 2 * pencil), jnp.float32),
             pltpu.VMEM((rows, columns), jnp.float32),
-            pltpu.SemaphoreType.DMA((8,)),
+            pltpu.VMEM((slabs, slab_rows, columns), jnp.bfloat16),
+            pltpu.SemaphoreType.DMA((7,)),
+            pltpu.SemaphoreType.DMA((3,)),
         ],
         compiler_params=pltpu.CompilerParams(vmem_limit_bytes=32 << 20),
         name="solve",
     )(
         in_hbm(inverse_high),
-        in_hbm(inverse_low),
         in_hbm(basis_high),
         in_hbm(basis_low),
         in_hbm(damping),
@@ -662,13 +708,13 @@
         in_specs=[smem, vmem, vmem, hbm, vmem, hbm],
         out_specs=(hbm, vmem),
         scratch_shapes=[
-            pltpu.VMEM((2, component_rows, KX), jnp.bfloat16),
+            pltpu.VMEM((SPLIT, component_rows, 2 * WAVES), jnp.bfloat16),
             pltpu.VMEM((NX // 128, slab_rows * width, 128), jnp.float32),
             pltpu.VMEM((slab_rows, 3, half_modes, 2, NX), jnp.bfloat16),
             pltpu.VMEM((3, tiles, size), jnp.float32),
             pltpu.VMEM(phase_shape, jnp.float32),
-            pltpu.VMEM((2, KX, HALF), jnp.bfloat16),
-            pltpu.SemaphoreType.DMA((2,)),
+            pltpu.VMEM((SPLIT, 2 * WAVES, POINTS), jnp.bfloat16),
+            pltpu.SemaphoreType.DMA((SPLIT,)),
             pltpu.SemaphoreType.DMA,
             pltpu.SemaphoreType.DMA((3,)),
         ],

time: 131 us -> 127 us (0.969)
  Pallas kernels: 42.2 us -> 39.2 us
    pallas_call x2 -> x3, Pallas kernels: 17.1 us -> 16.3 us  [the longest x1 13.9 us: on_device(): pl.pallas_call(functools.partial(spread_kernel, **sizes), out_shape=jax.S...]
    unnamed x32 -> x34, local copies, waits for them, and re-layouts: 3.74 us -> 4.01 us
  transfers between devices with their start and end apart: 3 -> 3, of which waited for: 3 -> 3; matrix products, arithmetic and copies ran while one was open for 6% -> 7% of each run, Pallas kernels for 6% -> 6%
where the time goes in v3:
time: 127 us
  waiting for transfers between devices  60.5 us (48%)
  Pallas kernels  39.2 us (31%)
  starting transfers between devices  13.1 us (10%)
  local copies, waits for them, and re-layouts  8.14 us (6%)
  other arithmetic  4.99 us (4%)
    all_to_all x1, waiting for transfers between devices, on_device(): lax.all_to_all(solved, ('px', 'pz'), split_axis=0, concat_axis=0, tiled=T...  33.1 us
    all_to_all x1, waiting for transfers between devices, on_device(): lax.all_to_all(outgoing, ('px', 'pz'), split_axis=0, concat_axis=0, tiled...  22.4 us
    pallas_call x1, Pallas kernels, on_device(): pl.pallas_call(functools.partial(spread_kernel, **sizes), out_shape=jax.S...  13.9 us
    pallas_call x1, Pallas kernels, on_device(): pl.pallas_call(functools.partial(gather_kernel, **sizes), out_shape=(jax....  9.09 us
    pallas_call x1, Pallas kernels, on_device(): pl.pallas_call(solve_kernel, out_shape=jax.ShapeDtypeStruct((slabs, slab_...  8.03 us
    all_to_all x1, starting transfers between devices, on_device(): lax.all_to_all(outgoing, ('px', 'pz'), split_axis=0, concat_axis=0, tiled...  7.48 us
    pallas_call x1, Pallas kernels, on_device(): pl.pallas_call(project_kernel, grid=(columns // pencil_waves,), out_shape...  5.7 us
    ppermute x1, waiting for transfers between devices, on_device(): other_part = lax.ppermute(mode_part, 'grp', [(0, 1), (1, 0)])  5.01 us
  transfers between devices with their start and end apart: 3, of which 3 were waited for; matrix products, arithmetic and copies ran while one was open for 7% of the time, Pallas kernels for 6%

profile of v3, /device:TPU:0, one launch (start us, length us, event | category | flops | bytes accessed | tf_op | source)
XLA Modules:
  0.0 126.8 jit_solution(16748715091194715278)
XLA Ops:
  0.6 13.9 %spread.1 = bf16[16,32,1536]{2,1,0:T(8,128)(2,1)} custom-call(s32[64]{0:T(128)} %block_ref.3, s32[1]{0:T(128)} %bitcast.group_ref, s32[64,512]{1,0:T(8,128)} %cell_ref.3, f32[64,512]{1,0:T(8,128)} %volume_ref.1, f32[64,512]{1,0:T(8,128)} %rate_ref.1, f32[64,512]{1,0:T(8,128)} %place_ref.3, f32[3,64,512]{2,1,0:T(8,128)} %motion_ref.1, ...), custom_call_target="tpu_custom_call" | custom-call | tf_op jit(solution)/shard_map/spread/pallas_call | solution.py:588
  14.6 7.5 %all-to-all-start = ((bf16[16,32,1536]{2,1,0:T(8,128)(2,1)}), bf16[16,32,1536]{2,1,0:T(8,128)(2,1)}, u32[]{:S(2)}, u32[]{:S(2)}) async-start(bf16[16,32,1536]{2,1,0:T(8,128)(2,1)} %spread.1), calls=%async_computation | async-start | bytes 3145728 | tf_op jit(solution)/shard_map/all_to_all | solution.py:617
  22.1 4.1 %reshape.64.state_ref = f32[512,1536]{1,0:T(8,128)S(1)} reshape(f32[512,3,1,2,256]{4,3,2,1,0:T(2,128)} %param.29) | data formatting | bytes 6291456 | tf_op jit(solution)/shard_map/reshape | solution.py:625
  26.3 0.0 copy-start.7
  26.3 2.9 %fusion = (bf16[512,512]{1,0:T(8,128)(2,1)S(1)}, bf16[512,512]{1,0:T(8,128)(2,1)S(1)}, bf16[512,512]{1,0:T(8,128)(2,1)}, bf16[512,512]{1,0:T(8,128)(2,1)}) fusion(f32[512,512]{1,0:T(8,128)} %param.31, f32[512,512]{1,0:T(8,128)} %param.30), kind=kLoop, calls=%fused_computation.4 | loop fusion | flops 2097152 | bytes 4194304 | tf_op jit(solution)/shard_map/convert_element_type | solution.py:621
  29.2 0.0 copy-start.2
  29.2 0.0 copy-done.7
  29.2 0.0 copy-start.15
  29.2 5.7 %project.1.state_ref = f32[512,1536]{1,0:T(8,128)S(1)} custom-call(bf16[512,512]{1,0:T(8,128)(2,1)S(1)} %get-tuple-element.7.high_ref.inverse_high_ref, bf16[512,512]{1,0:T(8,128)(2,1)S(1)} %get-tuple-element.6.low_ref, bf16[256,256]{1,0:T(8,128)(2,1)S(1)} %copy-done.7, f32[512,1536]{1,0:T(8,128)S(1)} %reshape.64.state_ref), custom_call_target="tpu_custom_call" | custom-call | tf_op jit(solution)/shard_map/project/pallas_call | solution.py:628
  34.9 0.0 copy-done.2
  34.9 0.0 copy-start
  34.9 1.7 %copy-done = f32[512,1536]{1,0:T(8,128)} copy-done((f32[512,1536]{1,0:T(8,128)}, f32[512,1536]{1,0:T(8,128)S(1)}, u32[]{:S(2)}) %copy-start) | copy-done | bytes 3145752
  36.6 0.0 copy-done.15
  36.6 1.2 add_divide_fusion.damping_ref
  37.8 22.4 %all-to-all-done.force_ref = bf16[16,32,1536]{2,1,0:T(8,128)(2,1)} async-done(((bf16[16,32,1536]{2,1,0:T(8,128)(2,1)}), bf16[16,32,1536]{2,1,0:T(8,128)(2,1)}, u32[]{:S(2)}, u32[]{:S(2)}) %all-to-all-start) | async-done | bytes 1572896 | tf_op jit(solution)/shard_map/all_to_all | solution.py:617
  60.2 8.0 %solve.1 = bf16[16,32,1536]{2,1,0:T(8,128)(2,1)} custom-call(bf16[512,512]{1,0:T(8,128)(2,1)} %copy-done.2, bf16[512,512]{1,0:T(8,128)(2,1)} %get-tuple-element.10.basis_high_ref, bf16[512,512]{1,0:T(8,128)(2,1)} %get-tuple-element.11.basis_low_ref, f32[512,512]{1,0:T(8,128)} %add_divide_fusion.damping_ref, f32[512,1536]{1,0:T(8,128)} %copy-done, ...), custom_call_target="tpu_custom_call" | custom-call | tf_op jit(solution)/shard_map/solve/pallas_call | solution.py:678
  68.2 0.0 copy-start.4
  68.2 0.0 copy-start.8
  68.2 0.0 copy-start.9
  68.3 0.0 copy-start.10
  68.3 0.0 copy-start.11
  68.3 4.1 %all-to-all-start.1 = ((bf16[16,32,1536]{2,1,0:T(8,128)(2,1)}), bf16[16,32,1536]{2,1,0:T(8,128)(2,1)S(1)}, u32[]{:S(2)}, u32[]{:S(2)}) async-start(bf16[16,32,1536]{2,1,0:T(8,128)(2,1)} %solve.1), calls=%async_computation.1 | async-start | bytes 3145728 | tf_op jit(solution)/shard_map/all_to_all | solution.py:701
  72.4 0.0 copy-done.4
  72.4 0.0 copy-start.5
  72.4 0.0 copy-start.6
  72.4 0.0 copy-start.12
  72.4 1.2 phases.1.phase_ref
  73.6 0.0 copy-start.3
  73.6 1.0 copy-done.3
  74.6 0.0 copy-done.8
  74.6 0.0 copy-done.9
  74.6 0.0 copy-done.10
  74.6 0.0 copy-done.11
  74.6 1.2 waves.1.table_ref
  75.8 0.0 copy-start.1
  75.8 1.3 %copy-done.1 = bf16[4,512,512]{2,1,0:T(8,128)(2,1)} copy-done((bf16[4,512,512]{2,1,0:T(8,128)(2,1)}, bf16[4,512,512]{2,1,0:T(8,128)(2,1)S(1)}, u32[]{:S(2)}) %copy-start.1) | copy-done | bytes 2097176
  77.1 0.0 copy-start.14
  77.1 0.0 copy-start.13
  77.1 33.1 %all-to-all-done.1.back_ref = bf16[16,32,1536]{2,1,0:T(8,128)(2,1)S(1)} async-done(((bf16[16,32,1536]{2,1,0:T(8,128)(2,1)}), bf16[16,32,1536]{2,1,0:T(8,128)(2,1)S(1)}, u32[]{:S(2)}, u32[]{:S(2)}) %all-to-all-start.1) | async-done | bytes 1572896 | tf_op jit(solution)/shard_map/all_to_all | solution.py:701
  110.2 0.0 copy-done.5
  110.2 0.0 copy-done.6
  110.2 0.0 copy-done.12
  110.2 9.1 %gather.1 = (bf16[32,3,4,2,2048]{4,3,2,1,0:T(2,128)(2,1)}, bf16[3,64,512]{2,1,0:T(8,128)(2,1)S(1)}) custom-call(s32[64]{0:T(128)S(1)} %copy-done.12, s32[64,512]{1,0:T(8,128)S(1)} %copy-done.5, bf16[512,256]{1,0:T(8,128)(2,1)S(1)} %copy-done.6, bf16[4,512,512]{2,1,0:T(8,128)(2,1)} %copy-done.1, bf16[16,32,1536]{2,1,0:T(8,128)(2,1)S(1)} %all-to-all-done.1.back_ref, ...), custom_call_target="tpu_custom_call" | custom-call | tf_op jit(solution)/shard_map/gather/pallas_call | solution.py:702
  119.3 1.6 %collective-permute-start = (bf16[3,64,512]{2,1,0:T(8,128)(2,1)S(1)}, bf16[3,64,512]{2,1,0:T(8,128)(2,1)S(1)}, u32[]{:S(2)}, u32[]{:S(2)}) collective-permute-start(bf16[3,64,512]{2,1,0:T(8,128)(2,1)S(1)} %get-tuple-element.5), channel_id=1, source_target_pairs={{0,16},{16,0},{1,17},{17,1},{2,18},{18,2},{3,19},{19,3},{4,20},{20... | collective-permute-start | bytes 589832 | tf_op jit(solution)/shard_map/ppermute | solution.py:731
  120.9 0.0 copy-done.14
  120.9 5.0 %collective-permute-done = bf16[3,64,512]{2,1,0:T(8,128)(2,1)S(1)} collective-permute-done((bf16[3,64,512]{2,1,0:T(8,128)(2,1)S(1)}, bf16[3,64,512]{2,1,0:T(8,128)(2,1)S(1)}, u32[]{:S(2)}, u32[]{:S(2)}) %collective-permute-start) | collective-permute-done | bytes 196640 | tf_op jit(solution)/shard_map/ppermute | solution.py:731
  125.9 0.0 copy-done.13
  125.9 0.9 add_subtract_fusion
  (5 shorter events, 0.0 us)
Async XLA Ops:
  14.6 45.6 %all-to-all-start = ((bf16[16,32,1536]{2,1,0:T(8,128)(2,1)}), bf16[16,32,1536]{2,1,0:T(8,128)(2,1)}, u32[]{:S(2)}, u32[]{:S(2)}) async-start(bf16[16,32,1536]{2,1,0:T(8,128)(2,1)} %spread.1), calls=%async_computation | async-start | bytes 3145728 | tf_op jit(solution)/shard_map/all_to_all | solution.py:617
  26.3 2.9 %copy-start.7 = (bf16[256,256]{1,0:T(8,128)(2,1)S(1)}, bf16[256,256]{1,0:T(8,128)(2,1)}, u32[]{:S(2)}) copy-start(bf16[256,256]{1,0:T(8,128)(2,1)} %constant.93.clone.order_ref) | copy-start | bytes 393220
  29.2 5.7 %copy-start.2 = (bf16[512,512]{1,0:T(8,128)(2,1)}, bf16[512,512]{1,0:T(8,128)(2,1)S(1)}, u32[]{:S(2)}) copy-start(bf16[512,512]{1,0:T(8,128)(2,1)S(1)} %get-tuple-element.7.high_ref.inverse_high_ref) | copy-start | bytes 1572868
  29.2 7.4 %copy-start.15 = (f32[512]{0:T(512)S(1)}, f32[512]{0:T(512)}, u32[]{:S(2)}) copy-start(f32[512]{0:T(512)} %param.32) | copy-start | bytes 6148
  34.9 1.7 %copy-start = (f32[512,1536]{1,0:T(8,128)}, f32[512,1536]{1,0:T(8,128)S(1)}, u32[]{:S(2)}) copy-start(f32[512,1536]{1,0:T(8,128)S(1)} %project.1.state_ref) | copy-start | bytes 9437188
  68.2 4.1 %copy-start.4 = (f32[64,512]{1,0:T(8,128)S(1)}, f32[64,512]{1,0:T(8,128)}, u32[]{:S(2)}) copy-start(f32[64,512]{1,0:T(8,128)} %place_ref.3) | copy-start | bytes 393220
  68.2 6.3 %copy-start.8 = (f32[4,8,512]{2,1,0:T(8,128)S(1)}, f32[4,8,512]{2,1,0:T(8,128)}, u32[]{:S(2)}) copy-start(f32[4,8,512]{2,1,0:T(8,128)} %constant.94.clone.base_cos_ref) | copy-start | bytes 196612
  68.2 6.3 %copy-start.9 = (f32[4,8,512]{2,1,0:T(8,128)S(1)}, f32[4,8,512]{2,1,0:T(8,128)}, u32[]{:S(2)}) copy-start(f32[4,8,512]{2,1,0:T(8,128)} %constant.95.clone.base_sin_ref) | copy-start | bytes 196612
  68.3 6.3 %copy-start.10 = (f32[8,512]{1,0:T(8,128)S(1)}, f32[8,512]{1,0:T(8,128)}, u32[]{:S(2)}) copy-start(f32[8,512]{1,0:T(8,128)} %constant.96.clone.step_cos_ref) | copy-start | bytes 49156
  68.3 6.3 %copy-start.11 = (f32[8,512]{1,0:T(8,128)S(1)}, f32[8,512]{1,0:T(8,128)}, u32[]{:S(2)}) copy-start(f32[8,512]{1,0:T(8,128)} %constant.97.clone.step_sin_ref) | copy-start | bytes 49156
  68.3 41.9 %all-to-all-start.1 = ((bf16[16,32,1536]{2,1,0:T(8,128)(2,1)}), bf16[16,32,1536]{2,1,0:T(8,128)(2,1)S(1)}, u32[]{:S(2)}, u32[]{:S(2)}) async-start(bf16[16,32,1536]{2,1,0:T(8,128)(2,1)} %solve.1), calls=%async_computation.1 | async-start | bytes 3145728 | tf_op jit(solution)/shard_map/all_to_all | solution.py:701
  72.4 37.8 %copy-start.5 = (s32[64,512]{1,0:T(8,128)S(1)}, s32[64,512]{1,0:T(8,128)}, u32[]{:S(2)}) copy-start(s32[64,512]{1,0:T(8,128)} %cell_ref.3) | copy-start | bytes 393220
  72.4 37.8 %copy-start.6 = (bf16[512,256]{1,0:T(8,128)(2,1)S(1)}, bf16[512,256]{1,0:T(8,128)(2,1)}, u32[]{:S(2)}) copy-start(bf16[512,256]{1,0:T(8,128)(2,1)} %constant.98.clone.order_ref) | copy-start | bytes 786436
  72.4 37.8 %copy-start.12 = (s32[64]{0:T(128)S(1)}, s32[64]{0:T(128)}, u32[]{:S(2)}) copy-start(s32[64]{0:T(128)} %block_ref.3) | copy-start | bytes 772
  73.6 1.0 copy-start.3
  75.8 1.3 %copy-start.1 = (bf16[4,512,512]{2,1,0:T(8,128)(2,1)}, bf16[4,512,512]{2,1,0:T(8,128)(2,1)S(1)}, u32[]{:S(2)}) copy-start(bf16[4,512,512]{2,1,0:T(8,128)(2,1)S(1)} %waves.1.table_ref) | copy-start | bytes 6291460
  77.1 43.8 %copy-start.14 = (f32[64,512]{1,0:T(8,128)S(1)}, f32[64,512]{1,0:T(8,128)}, u32[]{:S(2)}) copy-start(f32[64,512]{1,0:T(8,128)} %rate_ref.1) | copy-start | bytes 393220
  77.1 48.8 %copy-start.13 = (f32[3,64,512]{2,1,0:T(8,128)S(1)}, f32[3,64,512]{2,1,0:T(8,128)}, u32[]{:S(2)}) copy-start(f32[3,64,512]{2,1,0:T(8,128)} %motion_ref.1) | copy-start | bytes 1179652
  119.3 6.6 %collective-permute-start = (bf16[3,64,512]{2,1,0:T(8,128)(2,1)S(1)}, bf16[3,64,512]{2,1,0:T(8,128)(2,1)S(1)}, u32[]{:S(2)}, u32[]{:S(2)}) collective-permute-start(bf16[3,64,512]{2,1,0:T(8,128)(2,1)S(1)} %get-tuple-element.5), channel_id=1, source_target_pairs={{0,16},{16,0},{1,17},{17,1},{2,18},{18,2},{3,19},{19,3},{4,20},{20... | collective-permute-start | bytes 589832 | tf_op jit(solution)/shard_map/ppermute | solution.py:731

commit v4 on v3

--- a/solution.py
+++ b/solution.py
@@ -109,12 +109,12 @@
 def spread_kernel(
     block_ref,
     group_ref,
-    cell_ref,
-    volume_ref,
-    rate_ref,
-    place_ref,
-    motion_ref,
-    seen_ref,
+    cell_in,
+    volume_in,
+    rate_in,
+    place_in,
+    motion_in,
+    seen_in,
     base_cos_ref,
     base_sin_ref,
     step_cos_ref,
@@ -129,6 +129,13 @@
     amounts,
     phases,
     packed,
+    cell_ref,
+    volume_ref,
+    rate_ref,
+    place_ref,
+    motion_ref,
+    seen_ref,
+    in_sem,
     out_sem,
     *,
     half_modes,
@@ -142,6 +149,40 @@
     component_rows = slab_rows * group_rows
     pz_count = half_modes // pencil_modes
 
+    loads = [
+        (place_in, place_ref),
+        (cell_in, cell_ref),
+        (volume_in, volume_ref),
+        (rate_in, rate_ref),
+        (motion_in, motion_ref),
+        (seen_in, seen_ref),
+    ]
+    loads = [
+        pltpu.make_async_copy(source, target, in_sem.at[index])
+        for index, (source, target) in enumerate(loads)
+    ]
+    for load in loads:
+        load.start()
+
+    grow(
+        table_cos,
+        table_sin,
+        (base_cos_ref[...], base_sin_ref[...]),
+        (step_cos_ref, step_sin_ref),
+        POINTS,
+    )
+    for rest in range(SPLIT):
+        lanes = slice(rest * WAVES, (rest + 1) * WAVES)
+        table[rest, :, 0:WAVES] = table_cos[:, lanes].astype(jnp.bfloat16)
+        table[rest, :, WAVES:] = table_sin[:, lanes].astype(jnp.bfloat16)
+
+    def clear(index, carry):
+        field[index] = jnp.zeros(field.shape[1:], jnp.float32)
+        return carry
+
+    lax.fori_loop(0, field.shape[0], clear, 0)
+
+    loads[0].wait()
     first = (group_ref[0] * half_modes + 1).astype(jnp.float32)
     for mode, (cosine, sine) in enumerate(turn_modes(place_ref[...], first, half_modes)):
         for piece in range(size // 128):
@@ -150,6 +191,8 @@
                 rows = pl.ds(part * half_modes + mode, tiles, stride=group_rows)
                 phases[piece, rows, :] = value[:, lanes]
 
+    for load in loads[1:]:
+        load.wait()
     upper = cell_ref[...] >= 128
     volume = volume_ref[...]
     pull = volume * rate_ref[...]
@@ -159,24 +202,6 @@
             amount = amount - gravity * volume
         amounts[component] = jnp.where(upper, 0.0, amount)
         amounts[3 + component] = jnp.where(upper, amount, 0.0)
-
-    grow(
-        table_cos,
-        table_sin,
-        (base_cos_ref[...], base_sin_ref[...]),
-        (step_cos_ref, step_sin_ref),
-        POINTS,
-    )
-    for rest in range(SPLIT):
-        lanes = slice(rest * WAVES, (rest + 1) * WAVES)
-        table[rest, :, 0:WAVES] = table_cos[:, lanes].astype(jnp.bfloat16)
-        table[rest, :, WAVES:] = table_sin[:, lanes].astype(jnp.bfloat16)
-
-    def clear(index, carry):
-        field[index] = jnp.zeros(field.shape[1:], jnp.float32)
-        return carry
-
-    lax.fori_loop(0, field.shape[0], clear, 0)
 
     cells = lax.broadcasted_iota(jnp.int32, (128, size), 0)
 
@@ -325,57 +350,67 @@
 
 
 def solve_kernel(
-    inverse_high_ref,
+    inverse_ref,
     basis_high_ref,
     basis_low_ref,
     damping_ref,
     state_ref,
     force_ref,
     out_ref,
-    matrices,
+    inverse,
+    basis,
     damping,
     state,
+    pushed,
+    modal,
     results,
     sems,
     out_sems,
+    *,
+    pencil_waves,
 ):
-    rows, step = damping_ref.shape
+    rows = inverse.shape[0]
     columns = force_ref.shape[-1]
-    force_rows = force_ref[...].reshape(rows, columns)
+    step = columns // 3
     slab_shape = out_ref.shape[:2]
     spans = [pl.ds(start, step) for start in range(0, columns, step)]
     loads = [
-        (inverse_high_ref, matrices.at[0]),
+        (inverse_ref, inverse),
         (state_ref.at[:, spans[0]], state.at[:, spans[0]]),
         (damping_ref, damping),
-        (basis_high_ref, matrices.at[1]),
-        (basis_low_ref, matrices.at[2]),
-    ] + [(state_ref.at[:, span], state.at[:, span]) for span in spans[1:]]
+        (basis_high_ref, basis.at[:, pl.ds(0, rows)]),
+        (basis_high_ref, basis.at[:, pl.ds(rows, rows)]),
+        (basis_low_ref, basis.at[:, pl.ds(2 * rows, rows)]),
+        (state_ref.at[:, spans[1]], state.at[:, spans[1]]),
+        (state_ref.at[:, spans[2]], state.at[:, spans[2]]),
+    ]
     copies = [
         pltpu.make_async_copy(source, target, sems.at[index])
         for index, (source, target) in enumerate(loads)
     ]
     for copy in copies:
         copy.start()
+    copies[0].wait()
+    pushed[...] = dot32(inverse[...], force_ref[...].reshape(rows, columns))
     stores = []
-    for index, start in enumerate(range(0, columns, step)):
-        lanes = slice(start, start + step)
-        force = force_rows[:, lanes]
-        if index == 0:
-            copies[0].wait()
-        pushed = dot32(matrices[0], force)
-        copies[1 if index == 0 else 4 + index].wait()
+    for index in range(3):
+        lanes = slice(index * step, (index + 1) * step)
+        copies[1 if index == 0 else 5 + index].wait()
         if index == 0:
             copies[2].wait()
-        modal_high, modal_low = split((state[:, lanes] + time_step * pushed) * damping[...])
+        for block in range(step // pencil_waves):
+            own = slice(block * pencil_waves, (block + 1) * pencil_waves)
+            column = slice(index * step + own.start, index * step + own.stop)
+            mode = slice((block // 2) * pencil_waves, (block // 2 + 1) * pencil_waves)
+            damped = (state[:, column] + time_step * pushed[:, column]) * damping[:, mode]
+            high, low = split(damped)
+            modal[0:rows, own] = high
+            modal[rows : 2 * rows, own] = low
+            modal[2 * rows : 3 * rows, own] = high
         if index == 0:
-            copies[3].wait()
-            copies[4].wait()
-        solved = (
-            dot32(matrices[1], modal_high)
-            + dot32(matrices[1], modal_low)
-            + dot32(matrices[2], modal_high)
-        )
+            for copy in copies[3:6]:
+                copy.wait()
+        solved = dot32(basis[...], modal[...])
         results[:, :, lanes] = solved.astype(jnp.bfloat16).reshape(slab_shape + (step,))
         copy = pltpu.make_async_copy(
             results.at[:, :, spans[index]], out_ref.at[:, :, spans[index]], out_sems.at[index]
@@ -588,7 +623,7 @@
     outgoing = pl.pallas_call(
         functools.partial(spread_kernel, **sizes),
         out_shape=jax.ShapeDtypeStruct((slabs, slab_rows, columns), jnp.bfloat16),
-        in_specs=[smem, smem] + [vmem] * 11,
+        in_specs=[smem, smem] + [hbm] * 6 + [vmem] * 5,
         out_specs=hbm,
         scratch_shapes=[
             pltpu.VMEM((NX // 128, slab_rows * width, 128), jnp.float32),
@@ -599,8 +634,11 @@
             pltpu.VMEM((6, tiles, size), jnp.float32),
             pltpu.VMEM(phase_shape, jnp.float32),
             pltpu.VMEM((slabs, slab_rows, columns), jnp.bfloat16),
-            pltpu.SemaphoreType.DMA((3,)),
-        ],
+            pltpu.VMEM((tiles, size), jnp.int32),
+        ]
+        + [pltpu.VMEM((tiles, size), jnp.float32)] * 3
+        + [pltpu.VMEM((3, tiles, size), jnp.float32)] * 2
+        + [pltpu.SemaphoreType.DMA((6,)), pltpu.SemaphoreType.DMA((3,))],
         name="spread",
     )(
         block_index,
@@ -652,10 +690,10 @@
     wave_square = (
         stream_wave[None, :] * stream_wave[None, :] + span_wave[:, None] * span_wave[:, None]
     )
-    wave_square = jnp.broadcast_to(wave_square[:, None, :], (pencil_modes, 2, pencil_waves))
-    damping = 1.0 / (
-        1.0 + viscosity * (eigenvalues[:, None] + wave_square.reshape(1, 2 * pencil))
-    )
+    wave_square = jnp.broadcast_to(
+        wave_square[None, :, None, :], (3, pencil_modes, 2, pencil_waves)
+    ).reshape(1, columns)
+    damping = 1.0 / (1.0 + viscosity * (eigenvalues[:, None] + wave_square))
     table = pl.pallas_call(
         table_kernel,
         out_shape=jax.ShapeDtypeStruct((SPLIT, 2 * WAVES, POINTS), jnp.bfloat16),
@@ -675,29 +713,12 @@
         name="phases",
     )(group, spanwise_position)
 
-    solved = pl.pallas_call(
-        solve_kernel,
-        out_shape=jax.ShapeDtypeStruct((slabs, slab_rows, columns), jnp.bfloat16),
-        in_specs=[hbm] * 5 + [vmem],
-        out_specs=hbm,
-        scratch_shapes=[
-            pltpu.VMEM((3, rows, rows), jnp.bfloat16),
-            pltpu.VMEM((rows, 2 * pencil), jnp.float32),
-            pltpu.VMEM((rows, columns), jnp.float32),
-            pltpu.VMEM((slabs, slab_rows, columns), jnp.bfloat16),
-            pltpu.SemaphoreType.DMA((7,)),
-            pltpu.SemaphoreType.DMA((3,)),
-        ],
-        compiler_params=pltpu.CompilerParams(vmem_limit_bytes=32 << 20),
-        name="solve",
-    )(
-        in_hbm(inverse_high),
-        in_hbm(basis_high),
-        in_hbm(basis_low),
-        in_hbm(damping),
-        in_hbm(projected),
-        force,
-    )
+    pushed = jnp.dot(
+        inverse_high, force.reshape(rows, columns), preferred_element_type=jnp.float32
+    )
+    modal = (projected + time_step * pushed) * damping
+    solved = jnp.dot(eigen_basis, modal, precision=lax.Precision.HIGH).astype(jnp.bfloat16)
+    solved = solved.reshape(slabs, slab_rows, columns)
     returned = lax.all_to_all(solved, ("px", "pz"), split_axis=0, concat_axis=0, tiled=True)
     velocity_planes, mode_part = pl.pallas_call(
         functools.partial(gather_kernel, **sizes),

time: 127 us -> 125 us (0.984)
  Pallas kernels: 39.2 us -> 30.7 us
  matrix products: 0 us -> 6.75 us
  local copies, waits for them, and re-layouts: 8.14 us -> 11.4 us
  other arithmetic: 4.99 us -> 2.3 us
    pallas_call x1 -> x0, Pallas kernels: 8.03 us -> none  [on_device(): pl.pallas_call(solve_kernel, out_shape=jax.ShapeDtypeStruct((slabs, slab_...]
    dot_general x0 -> x2, matrix products: none -> 6.75 us  [the longest x1 3.81 us: on_device(): jnp.dot(eigen_basis, modal, precision=lax.Precision.HIGH)]
    unnamed x34, local copies, waits for them, and re-layouts: 4.01 us -> 5.91 us
    convert_element_type x1, other arithmetic: 2.9 us -> 1.38 us  [halves(): return (high.astype(jnp.bfloat16), (matrix - high).astype(jnp.bfloat16))]
    reshape x1, local copies, waits for them, and re-layouts: 4.14 us -> 5.5 us  [on_device(): state = fluid_velocity.transpose(0, 1, 2, 3, 4).reshape(rows, columns)]
  transfers between devices with their start and end apart: 3 -> 3, of which waited for: 3 -> 3; matrix products, arithmetic and copies ran while one was open for 7% -> 6% of each run, Pallas kernels for 6% -> 6%
where the time goes in v4:
time: 125 us
  waiting for transfers between devices  60 us (48%)
  Pallas kernels  30.7 us (25%)
  starting transfers between devices  13 us (10%)
  local copies, waits for them, and re-layouts  11.4 us (9%)
  matrix products  6.75 us (5%)
  other arithmetic  2.3 us (2%)
    all_to_all x1, waiting for transfers between devices, on_device(): lax.all_to_all(solved, ('px', 'pz'), split_axis=0, concat_axis=0, tiled=T...  33.1 us
    all_to_all x1, waiting for transfers between devices, on_device(): lax.all_to_all(outgoing, ('px', 'pz'), split_axis=0, concat_axis=0, tiled...  21.9 us
    pallas_call x1, Pallas kernels, on_device(): pl.pallas_call(functools.partial(spread_kernel, **sizes), out_shape=jax.S...  13.4 us
    pallas_call x1, Pallas kernels, on_device(): pl.pallas_call(functools.partial(gather_kernel, **sizes), out_shape=(jax....  9.14 us
    all_to_all x1, starting transfers between devices, on_device(): lax.all_to_all(outgoing, ('px', 'pz'), split_axis=0, concat_axis=0, tiled...  7.43 us
    unnamed x34, local copies, waits for them, and re-layouts  5.91 us
    pallas_call x1, Pallas kernels, on_device(): pl.pallas_call(project_kernel, grid=(columns // pencil_waves,), out_shape...  5.69 us
    reshape x1, local copies, waits for them, and re-layouts, on_device(): state = fluid_velocity.transpose(0, 1, 2, 3, 4).reshape(rows, columns)  5.5 us
  transfers between devices with their start and end apart: 3, of which 3 were waited for; matrix products, arithmetic and copies ran while one was open for 6% of the time, Pallas kernels for 6%

profile of v4, /device:TPU:0, one launch (start us, length us, event | category | flops | bytes accessed | tf_op | source)
XLA Modules:
  0.0 125.0 jit_solution(15964513429939972280)
XLA Ops:
  0.6 0.0 copy-start
  0.7 13.4 %spread.1 = bf16[16,32,1536]{2,1,0:T(8,128)(2,1)} custom-call(s32[64]{0:T(128)} %block_ref.3, s32[1]{0:T(128)} %bitcast.group_ref, s32[64,512]{1,0:T(8,128)} %cell_ref.1, f32[64,512]{1,0:T(8,128)} %volume_in.1, f32[64,512]{1,0:T(8,128)} %rate_in.1, f32[64,512]{1,0:T(8,128)} %place_ref.1, f32[3,64,512]{2,1,0:T(8,128)} %motion_in.1, f32[3,64,512]{2,1,0:T(8,128)} %seen_in.1, ...), custom_call_target="tpu_custom_call" | custom-call | tf_op jit(solution)/shard_map/spread/pallas_call | solution.py:623
  14.1 7.4 %all-to-all-start = ((bf16[16,32,1536]{2,1,0:T(8,128)(2,1)}), bf16[16,32,1536]{2,1,0:T(8,128)(2,1)S(1)}, u32[]{:S(2)}, u32[]{:S(2)}) async-start(bf16[16,32,1536]{2,1,0:T(8,128)(2,1)} %spread.1), calls=%async_computation | async-start | bytes 3145728 | tf_op jit(solution)/shard_map/all_to_all | solution.py:655
  21.6 0.0 copy-start.8
  21.6 5.5 %reshape.68.state_ref = f32[512,1536]{1,0:T(8,128)} reshape(f32[512,3,1,2,256]{4,3,2,1,0:T(2,128)} %param.29) | data formatting | bytes 6291456 | tf_op jit(solution)/shard_map/reshape | solution.py:663
  27.1 1.4 %fusion.3 = (bf16[512,512]{1,0:T(8,128)(2,1)S(1)}, bf16[512,512]{1,0:T(8,128)(2,1)S(1)}) fusion(f32[512,512]{1,0:T(8,128)} %param.31), kind=kLoop, calls=%fused_computation.7 | loop fusion | flops 1048576 | bytes 2097152 | tf_op jit(solution)/shard_map/convert_element_type | solution.py:659
  28.5 0.0 copy-done.8
  28.5 0.0 copy-start.1
  28.5 1.9 %copy-done.1 = f32[512,1536]{1,0:T(8,128)S(1)} copy-done((f32[512,1536]{1,0:T(8,128)S(1)}, f32[512,1536]{1,0:T(8,128)}, u32[]{:S(2)}) %copy-start.1) | copy-done | bytes 3145752
  30.4 0.0 copy-start.16
  30.4 5.7 %project.1 = f32[512,1536]{1,0:T(8,128)S(1)} custom-call(bf16[512,512]{1,0:T(8,128)(2,1)S(1)} %get-tuple-element.7.high_ref, bf16[512,512]{1,0:T(8,128)(2,1)S(1)} %get-tuple-element.6.low_ref, bf16[256,256]{1,0:T(8,128)(2,1)S(1)} %copy-done.8, f32[512,1536]{1,0:T(8,128)S(1)} %copy-done.1), custom_call_target="tpu_custom_call" | custom-call | tf_op jit(solution)/shard_map/project/pallas_call | solution.py:666
  36.1 0.0 copy-start.4
  36.1 1.7 %copy-done.4 = f32[512,1536]{1,0:T(8,128)} copy-done((f32[512,1536]{1,0:T(8,128)}, f32[512,1536]{1,0:T(8,128)S(1)}, u32[]{:S(2)}) %copy-start.4) | copy-done | bytes 3145752
  37.8 21.9 %all-to-all-done = bf16[16,32,1536]{2,1,0:T(8,128)(2,1)S(1)} async-done(((bf16[16,32,1536]{2,1,0:T(8,128)(2,1)}), bf16[16,32,1536]{2,1,0:T(8,128)(2,1)S(1)}, u32[]{:S(2)}, u32[]{:S(2)}) %all-to-all-start) | async-done | bytes 1572896 | tf_op jit(solution)/shard_map/all_to_all | solution.py:655
  59.6 0.0 copy-done.16
  59.6 2.9 %fusion.2 = f32[512,1536]{1,0:T(8,128)S(1)} fusion(f32[512,1536]{1,0:T(8,128)} %copy-done.4, bf16[512,512]{1,0:T(8,128)(2,1)S(1)} %get-tuple-element.7.high_ref, bf16[512,1536]{1,0:T(8,128)(2,1)S(1)} %bitcast.18, f32[1536]{0:T(1024)S(1)} %add.101, f32[512]{0:T(512)S(1)} %copy-done.16), kind=kOutput, calls=%fused_computation.3 | convolution fusion | flops 810811392 | bytes 8396800 | tf_op jit(solution)/shard_map/dot_general | solution.py:716
  62.6 0.0 copy-done
  62.6 0.0 copy-start.5
  62.6 3.8 %convolution_convert_fusion = bf16[1536,512]{0,1:T(8,128)(2,1)} fusion(f32[512,1536]{1,0:T(8,128)S(1)} %fusion.2, f32[512,512]{1,0:T(8,128)S(1)} %copy-done), kind=kOutput, calls=%fused_computation.4 | convolution fusion | flops 2416705536 | bytes 5767168 | tf_op jit(solution)/shard_map/dot_general | solution.py:720
  66.4 0.0 copy-start.9
  66.4 0.0 copy-start.10
  66.4 0.0 copy-start.11
  66.4 0.0 copy-start.6
  66.4 0.0 copy-start.7
  66.4 0.0 copy-start.13
  66.4 4.0 %all-to-all-start.1 = ((bf16[16,32,1536]{2,1,0:T(8,128)(2,1)}), bf16[16,32,1536]{2,1,0:T(8,128)(2,1)S(1)}, u32[]{:S(2)}, u32[]{:S(2)}) async-start(bf16[16,32,1536]{2,1,0:T(8,128)(2,1)} %bitcast.17), calls=%async_computation.1 | async-start | bytes 3145728 | tf_op jit(solution)/shard_map/all_to_all | solution.py:722
  70.5 0.0 copy-done.5
  70.5 1.2 phases.1.phase_ref
  71.7 0.0 copy-start.3
  71.7 1.0 copy-done.3
  72.6 0.0 copy-done.9
  72.6 0.0 copy-done.10
  72.7 0.0 copy-done.11
  72.7 0.0 copy-done.12
  72.7 0.0 copy-start.15
  72.7 1.2 waves.1.table_ref
  73.9 0.0 copy-start.2
  73.9 1.3 %copy-done.2 = bf16[4,512,512]{2,1,0:T(8,128)(2,1)} copy-done((bf16[4,512,512]{2,1,0:T(8,128)(2,1)}, bf16[4,512,512]{2,1,0:T(8,128)(2,1)S(1)}, u32[]{:S(2)}) %copy-start.2) | copy-done | bytes 2097176
  75.2 33.1 %all-to-all-done.1.back_ref = bf16[16,32,1536]{2,1,0:T(8,128)(2,1)S(1)} async-done(((bf16[16,32,1536]{2,1,0:T(8,128)(2,1)}), bf16[16,32,1536]{2,1,0:T(8,128)(2,1)S(1)}, u32[]{:S(2)}, u32[]{:S(2)}) %all-to-all-start.1) | async-done | bytes 1572896 | tf_op jit(solution)/shard_map/all_to_all | solution.py:722
  108.4 0.0 copy-done.6
  108.4 0.0 copy-done.7
  108.4 0.0 copy-done.13
  108.4 9.1 %gather.1 = (bf16[32,3,4,2,2048]{4,3,2,1,0:T(2,128)(2,1)}, bf16[3,64,512]{2,1,0:T(8,128)(2,1)S(1)}) custom-call(s32[64]{0:T(128)S(1)} %copy-done.13, s32[64,512]{1,0:T(8,128)S(1)} %copy-done.6, bf16[512,256]{1,0:T(8,128)(2,1)S(1)} %copy-done.7, bf16[4,512,512]{2,1,0:T(8,128)(2,1)} %copy-done.2, bf16[16,32,1536]{2,1,0:T(8,128)(2,1)S(1)} %all-to-all-done.1.back_ref, ...), custom_call_target="tpu_custom_call" | custom-call | tf_op jit(solution)/shard_map/gather/pallas_call | solution.py:723
  117.5 1.6 %collective-permute-start = (bf16[3,64,512]{2,1,0:T(8,128)(2,1)S(1)}, bf16[3,64,512]{2,1,0:T(8,128)(2,1)S(1)}, u32[]{:S(2)}, u32[]{:S(2)}) collective-permute-start(bf16[3,64,512]{2,1,0:T(8,128)(2,1)S(1)} %get-tuple-element.5), channel_id=1, source_target_pairs={{0,16},{16,0},{1,17},{17,1},{2,18},{18,2},{3,19},{19,3},{4,20},{20... | collective-permute-start | bytes 589832 | tf_op jit(solution)/shard_map/ppermute | solution.py:752
  119.1 0.0 copy-done.15
  119.1 5.0 %collective-permute-done = bf16[3,64,512]{2,1,0:T(8,128)(2,1)S(1)} collective-permute-done((bf16[3,64,512]{2,1,0:T(8,128)(2,1)S(1)}, bf16[3,64,512]{2,1,0:T(8,128)(2,1)S(1)}, u32[]{:S(2)}, u32[]{:S(2)}) %collective-permute-start) | collective-permute-done | bytes 196640 | tf_op jit(solution)/shard_map/ppermute | solution.py:752
  124.1 0.0 copy-done.14
  124.1 0.9 add_subtract_fusion
  (7 shorter events, 0.0 us)
Async XLA Ops:
  0.6 61.9 %copy-start = (f32[512,512]{1,0:T(8,128)S(1)}, f32[512,512]{1,0:T(8,128)}, u32[]{:S(2)}) copy-start(f32[512,512]{1,0:T(8,128)} %param.30) | copy-start | bytes 3145732
  14.1 45.5 %all-to-all-start = ((bf16[16,32,1536]{2,1,0:T(8,128)(2,1)}), bf16[16,32,1536]{2,1,0:T(8,128)(2,1)S(1)}, u32[]{:S(2)}, u32[]{:S(2)}) async-start(bf16[16,32,1536]{2,1,0:T(8,128)(2,1)} %spread.1), calls=%async_computation | async-start | bytes 3145728 | tf_op jit(solution)/shard_map/all_to_all | solution.py:655
  21.6 6.9 %copy-start.8 = (bf16[256,256]{1,0:T(8,128)(2,1)S(1)}, bf16[256,256]{1,0:T(8,128)(2,1)}, u32[]{:S(2)}) copy-start(bf16[256,256]{1,0:T(8,128)(2,1)} %constant.94.clone.order_ref) | copy-start | bytes 393220
  28.5 1.9 %copy-start.1 = (f32[512,1536]{1,0:T(8,128)S(1)}, f32[512,1536]{1,0:T(8,128)}, u32[]{:S(2)}) copy-start(f32[512,1536]{1,0:T(8,128)} %reshape.68.state_ref) | copy-start | bytes 9437188
  30.4 29.2 %copy-start.16 = (f32[512]{0:T(512)S(1)}, f32[512]{0:T(512)}, u32[]{:S(2)}) copy-start(f32[512]{0:T(512)} %param.32) | copy-start | bytes 6148
  36.1 1.7 %copy-start.4 = (f32[512,1536]{1,0:T(8,128)}, f32[512,1536]{1,0:T(8,128)S(1)}, u32[]{:S(2)}) copy-start(f32[512,1536]{1,0:T(8,128)S(1)} %project.1) | copy-start | bytes 9437188
  62.6 7.9 %copy-start.5 = (f32[64,512]{1,0:T(8,128)S(1)}, f32[64,512]{1,0:T(8,128)}, u32[]{:S(2)}) copy-start(f32[64,512]{1,0:T(8,128)} %place_ref.1) | copy-start | bytes 393220
  66.4 6.2 %copy-start.9 = (f32[4,8,512]{2,1,0:T(8,128)S(1)}, f32[4,8,512]{2,1,0:T(8,128)}, u32[]{:S(2)}) copy-start(f32[4,8,512]{2,1,0:T(8,128)} %constant.95.clone.base_cos_ref) | copy-start | bytes 196612
  66.4 6.2 %copy-start.10 = (f32[4,8,512]{2,1,0:T(8,128)S(1)}, f32[4,8,512]{2,1,0:T(8,128)}, u32[]{:S(2)}) copy-start(f32[4,8,512]{2,1,0:T(8,128)} %constant.96.clone.base_sin_ref) | copy-start | bytes 196612
  66.4 6.3 %copy-start.11 = (f32[8,512]{1,0:T(8,128)S(1)}, f32[8,512]{1,0:T(8,128)}, u32[]{:S(2)}) copy-start(f32[8,512]{1,0:T(8,128)} %constant.97.clone.step_cos_ref) | copy-start | bytes 49156
  66.4 6.3 %copy-start.12 = (f32[8,512]{1,0:T(8,128)S(1)}, f32[8,512]{1,0:T(8,128)}, u32[]{:S(2)}) copy-start(f32[8,512]{1,0:T(8,128)} %constant.98.clone.step_sin_ref) | copy-start | bytes 49156
  66.4 42.0 %copy-start.6 = (s32[64,512]{1,0:T(8,128)S(1)}, s32[64,512]{1,0:T(8,128)}, u32[]{:S(2)}) copy-start(s32[64,512]{1,0:T(8,128)} %cell_ref.1) | copy-start | bytes 393220
  66.4 42.0 %copy-start.7 = (bf16[512,256]{1,0:T(8,128)(2,1)S(1)}, bf16[512,256]{1,0:T(8,128)(2,1)}, u32[]{:S(2)}) copy-start(bf16[512,256]{1,0:T(8,128)(2,1)} %constant.99.clone.order_ref) | copy-start | bytes 786436
  66.4 41.9 %copy-start.13 = (s32[64]{0:T(128)S(1)}, s32[64]{0:T(128)}, u32[]{:S(2)}) copy-start(s32[64]{0:T(128)} %block_ref.3) | copy-start | bytes 772
  66.4 41.9 %all-to-all-start.1 = ((bf16[16,32,1536]{2,1,0:T(8,128)(2,1)}), bf16[16,32,1536]{2,1,0:T(8,128)(2,1)S(1)}, u32[]{:S(2)}, u32[]{:S(2)}) async-start(bf16[16,32,1536]{2,1,0:T(8,128)(2,1)} %bitcast.17), calls=%async_computation.1 | async-start | bytes 3145728 | tf_op jit(solution)/shard_map/all_to_all | solution.py:722
  71.7 1.0 copy-start.3
  72.7 46.4 %copy-start.15 = (f32[64,512]{1,0:T(8,128)S(1)}, f32[64,512]{1,0:T(8,128)}, u32[]{:S(2)}) copy-start(f32[64,512]{1,0:T(8,128)} %rate_in.1) | copy-start | bytes 393220
  73.9 1.3 %copy-start.2 = (bf16[4,512,512]{2,1,0:T(8,128)(2,1)}, bf16[4,512,512]{2,1,0:T(8,128)(2,1)S(1)}, u32[]{:S(2)}) copy-start(bf16[4,512,512]{2,1,0:T(8,128)(2,1)S(1)} %waves.1.table_ref) | copy-start | bytes 6291460
  75.2 48.9 %copy-start.14 = (f32[3,64,512]{2,1,0:T(8,128)S(1)}, f32[3,64,512]{2,1,0:T(8,128)}, u32[]{:S(2)}) copy-start(f32[3,64,512]{2,1,0:T(8,128)} %motion_in.1) | copy-start | bytes 1179652
  117.5 6.6 %collective-permute-start = (bf16[3,64,512]{2,1,0:T(8,128)(2,1)S(1)}, bf16[3,64,512]{2,1,0:T(8,128)(2,1)S(1)}, u32[]{:S(2)}, u32[]{:S(2)}) collective-permute-start(bf16[3,64,512]{2,1,0:T(8,128)(2,1)S(1)} %get-tuple-element.5), channel_id=1, source_target_pairs={{0,16},{16,0},{1,17},{17,1},{2,18},{18,2},{3,19},{19,3},{4,20},{20... | collective-permute-start | bytes 589832 | tf_op jit(solution)/shard_map/ppermute | solution.py:752

commit v5 on v4

--- a/solution.py
+++ b/solution.py
@@ -243,31 +243,35 @@
     order = order_ref[...]
     def times_minus_i(value):
         lanes = value.shape[1]
-        value = value.reshape(slab_rows, group_rows, lanes)
+        rows = value.shape[0]
+        value = value.reshape(rows // group_rows, group_rows, lanes)
         part = lax.broadcasted_iota(jnp.int32, value.shape, 1) // half_modes
         moved = pltpu.roll(value, half_modes, 1)
-        return jnp.where(part == 0, moved, -moved).reshape(component_rows, lanes)
+        return jnp.where(part == 0, moved, -moved).reshape(rows, lanes)
 
     rest_waves = pencil_waves // SPLIT
+    for strip in range(POINTS // 128):
+        values = [field[strip + j * (POINTS // 128)] for j in range(SPLIT)]
+        lanes = slice(strip * 128, (strip + 1) * 128)
+        even_sum = values[0] + values[2]
+        odd_sum = values[1] + values[3]
+        even_gap = values[0] - values[2]
+        odd_gap = times_minus_i(values[1] - values[3])
+        left[0, :, lanes] = (even_sum + odd_sum).astype(jnp.bfloat16)
+        left[1, :, lanes] = (even_gap + odd_gap).astype(jnp.bfloat16)
+        left[2, :, lanes] = (even_sum - odd_sum).astype(jnp.bfloat16)
+        left[3, :, lanes] = (even_gap - odd_gap).astype(jnp.bfloat16)
+    all_spectra = []
+    for rest in range(SPLIT):
+        product = dot32(left[rest], table[rest])
+        spectrum = product[:, :WAVES] + times_minus_i(product[:, WAVES:])
+        all_spectra.append(spectrum.astype(jnp.bfloat16))
     copies = []
     for component in range(3):
         rows = slice(component * component_rows, (component + 1) * component_rows)
-        for strip in range(POINTS // 128):
-            values = [field[strip + j * (POINTS // 128), rows, :] for j in range(SPLIT)]
-            lanes = slice(strip * 128, (strip + 1) * 128)
-            even_sum = values[0] + values[2]
-            odd_sum = values[1] + values[3]
-            even_gap = values[0] - values[2]
-            odd_gap = times_minus_i(values[1] - values[3])
-            left[0, :, lanes] = (even_sum + odd_sum).astype(jnp.bfloat16)
-            left[1, :, lanes] = (even_gap + odd_gap).astype(jnp.bfloat16)
-            left[2, :, lanes] = (even_sum - odd_sum).astype(jnp.bfloat16)
-            left[3, :, lanes] = (even_gap - odd_gap).astype(jnp.bfloat16)
-        spectra = []
-        for rest in range(SPLIT):
-            product = dot32(left[rest], table[rest])
-            spectrum = product[:, :WAVES] + times_minus_i(product[:, WAVES:])
-            spectra.append(dot32(order, spectrum.astype(jnp.bfloat16)).astype(jnp.bfloat16))
+        spectra = [
+            dot32(order, spectrum[rows]).astype(jnp.bfloat16) for spectrum in all_spectra
+        ]
         for owner_px in range(KX // pencil_waves):
             own = slice(owner_px * rest_waves, (owner_px + 1) * rest_waves)
             joined = jnp.concatenate([spectrum[:, own] for spectrum in spectra], axis=1)
@@ -630,7 +634,7 @@
             pltpu.VMEM((POINTS, KX), jnp.float32),
             pltpu.VMEM((POINTS, KX), jnp.float32),
             pltpu.VMEM((SPLIT, POINTS, 2 * WAVES), jnp.bfloat16),
-            pltpu.VMEM((SPLIT, component_rows, POINTS), jnp.bfloat16),
+            pltpu.VMEM((SPLIT, 3 * component_rows, POINTS), jnp.bfloat16),
             pltpu.VMEM((6, tiles, size), jnp.float32),
             pltpu.VMEM(phase_shape, jnp.float32),
             pltpu.VMEM((slabs, slab_rows, columns), jnp.bfloat16),

time: 125 us -> 123 us (0.984)
  Pallas kernels: 30.7 us -> 28.7 us
    pallas_call x1, Pallas kernels: 13.4 us -> 11.5 us  [on_device(): pl.pallas_call(functools.partial(spread_kernel, **sizes), out_shape=jax.S...]
  transfers between devices with their start and end apart: 3 -> 3, of which waited for: 3 -> 3; matrix products, arithmetic and copies ran while one was open for 6% -> 6% of each run, Pallas kernels for 6% -> 7%
where the time goes in v5:
time: 123 us
  waiting for transfers between devices  60 us (49%)
  Pallas kernels  28.7 us (23%)
  starting transfers between devices  13 us (11%)
  local copies, waits for them, and re-layouts  11.4 us (9%)
  matrix products  6.75 us (5%)
  other arithmetic  2.3 us (2%)
    all_to_all x1, waiting for transfers between devices, on_device(): lax.all_to_all(solved, ('px', 'pz'), split_axis=0, concat_axis=0, tiled=T...  33.1 us
    all_to_all x1, waiting for transfers between devices, on_device(): lax.all_to_all(outgoing, ('px', 'pz'), split_axis=0, concat_axis=0, tiled...  21.9 us
    pallas_call x1, Pallas kernels, on_device(): pl.pallas_call(functools.partial(spread_kernel, **sizes), out_shape=jax.S...  11.5 us
    pallas_call x1, Pallas kernels, on_device(): pl.pallas_call(functools.partial(gather_kernel, **sizes), out_shape=(jax....  9.14 us
    all_to_all x1, starting transfers between devices, on_device(): lax.all_to_all(outgoing, ('px', 'pz'), split_axis=0, concat_axis=0, tiled...  7.43 us
    unnamed x34, local copies, waits for them, and re-layouts  5.91 us
    pallas_call x1, Pallas kernels, on_device(): pl.pallas_call(project_kernel, grid=(columns // pencil_waves,), out_shape...  5.69 us
    reshape x1, local copies, waits for them, and re-layouts, on_device(): state = fluid_velocity.transpose(0, 1, 2, 3, 4).reshape(rows, columns)  5.5 us
  transfers between devices with their start and end apart: 3, of which 3 were waited for; matrix products, arithmetic and copies ran while one was open for 6% of the time, Pallas kernels for 7%

profile of v5, /device:TPU:0, one launch (start us, length us, event | category | flops | bytes accessed | tf_op | source)
XLA Modules:
  0.0 123.0 jit_solution(12151702901980059437)
XLA Ops:
  0.6 0.0 copy-start
  0.7 11.5 %spread.1 = bf16[16,32,1536]{2,1,0:T(8,128)(2,1)} custom-call(s32[64]{0:T(128)} %block_ref.3, s32[1]{0:T(128)} %bitcast.group_ref, s32[64,512]{1,0:T(8,128)} %cell_ref.1, f32[64,512]{1,0:T(8,128)} %volume_in.1, f32[64,512]{1,0:T(8,128)} %rate_in.1, f32[64,512]{1,0:T(8,128)} %place_ref.1, f32[3,64,512]{2,1,0:T(8,128)} %motion_in.1, f32[3,64,512]{2,1,0:T(8,128)} %seen_in.1, ...), custom_call_target="tpu_custom_call" | custom-call | tf_op jit(solution)/shard_map/spread/pallas_call | solution.py:627
  12.1 7.4 %all-to-all-start = ((bf16[16,32,1536]{2,1,0:T(8,128)(2,1)}), bf16[16,32,1536]{2,1,0:T(8,128)(2,1)S(1)}, u32[]{:S(2)}, u32[]{:S(2)}) async-start(bf16[16,32,1536]{2,1,0:T(8,128)(2,1)} %spread.1), calls=%async_computation | async-start | bytes 3145728 | tf_op jit(solution)/shard_map/all_to_all | solution.py:659
  19.6 0.0 copy-start.8
  19.6 5.5 %reshape.68.state_ref = f32[512,1536]{1,0:T(8,128)} reshape(f32[512,3,1,2,256]{4,3,2,1,0:T(2,128)} %param.29) | data formatting | bytes 6291456 | tf_op jit(solution)/shard_map/reshape | solution.py:667
  25.1 1.4 %fusion.3 = (bf16[512,512]{1,0:T(8,128)(2,1)S(1)}, bf16[512,512]{1,0:T(8,128)(2,1)S(1)}) fusion(f32[512,512]{1,0:T(8,128)} %param.31), kind=kLoop, calls=%fused_computation.7 | loop fusion | flops 1048576 | bytes 2097152 | tf_op jit(solution)/shard_map/convert_element_type | solution.py:663
  26.5 0.0 copy-done.8
  26.5 0.0 copy-start.1
  26.5 1.9 %copy-done.1 = f32[512,1536]{1,0:T(8,128)S(1)} copy-done((f32[512,1536]{1,0:T(8,128)S(1)}, f32[512,1536]{1,0:T(8,128)}, u32[]{:S(2)}) %copy-start.1) | copy-done | bytes 3145752
  28.4 0.0 copy-start.16
  28.4 5.7 %project.1 = f32[512,1536]{1,0:T(8,128)S(1)} custom-call(bf16[512,512]{1,0:T(8,128)(2,1)S(1)} %get-tuple-element.7.high_ref, bf16[512,512]{1,0:T(8,128)(2,1)S(1)} %get-tuple-element.6.low_ref, bf16[256,256]{1,0:T(8,128)(2,1)S(1)} %copy-done.8, f32[512,1536]{1,0:T(8,128)S(1)} %copy-done.1), custom_call_target="tpu_custom_call" | custom-call | tf_op jit(solution)/shard_map/project/pallas_call | solution.py:670
  34.1 0.0 copy-start.4
  34.1 1.7 %copy-done.4 = f32[512,1536]{1,0:T(8,128)} copy-done((f32[512,1536]{1,0:T(8,128)}, f32[512,1536]{1,0:T(8,128)S(1)}, u32[]{:S(2)}) %copy-start.4) | copy-done | bytes 3145752
  35.8 21.9 %all-to-all-done = bf16[16,32,1536]{2,1,0:T(8,128)(2,1)S(1)} async-done(((bf16[16,32,1536]{2,1,0:T(8,128)(2,1)}), bf16[16,32,1536]{2,1,0:T(8,128)(2,1)S(1)}, u32[]{:S(2)}, u32[]{:S(2)}) %all-to-all-start) | async-done | bytes 1572896 | tf_op jit(solution)/shard_map/all_to_all | solution.py:659
  57.6 0.0 copy-done.16
  57.6 2.9 %fusion.2 = f32[512,1536]{1,0:T(8,128)S(1)} fusion(f32[512,1536]{1,0:T(8,128)} %copy-done.4, bf16[512,512]{1,0:T(8,128)(2,1)S(1)} %get-tuple-element.7.high_ref, bf16[512,1536]{1,0:T(8,128)(2,1)S(1)} %bitcast.18, f32[1536]{0:T(1024)S(1)} %add.101, f32[512]{0:T(512)S(1)} %copy-done.16), kind=kOutput, calls=%fused_computation.3 | convolution fusion | flops 810811392 | bytes 8396800 | tf_op jit(solution)/shard_map/dot_general | solution.py:720
  60.6 0.0 copy-done
  60.6 0.0 copy-start.5
  60.6 3.8 %convolution_convert_fusion = bf16[1536,512]{0,1:T(8,128)(2,1)} fusion(f32[512,1536]{1,0:T(8,128)S(1)} %fusion.2, f32[512,512]{1,0:T(8,128)S(1)} %copy-done), kind=kOutput, calls=%fused_computation.4 | convolution fusion | flops 2416705536 | bytes 5767168 | tf_op jit(solution)/shard_map/dot_general | solution.py:724
  64.4 0.0 copy-start.9
  64.4 0.0 copy-start.10
  64.4 0.0 copy-start.11
  64.4 0.0 copy-start.6
  64.4 0.0 copy-start.7
  64.4 0.0 copy-start.13
  64.5 4.0 %all-to-all-start.1 = ((bf16[16,32,1536]{2,1,0:T(8,128)(2,1)}), bf16[16,32,1536]{2,1,0:T(8,128)(2,1)S(1)}, u32[]{:S(2)}, u32[]{:S(2)}) async-start(bf16[16,32,1536]{2,1,0:T(8,128)(2,1)} %bitcast.17), calls=%async_computation.1 | async-start | bytes 3145728 | tf_op jit(solution)/shard_map/all_to_all | solution.py:726
  68.5 0.0 copy-done.5
  68.5 1.2 phases.1.phase_ref
  69.7 0.0 copy-start.3
  69.7 1.0 copy-done.3
  70.7 0.0 copy-done.9
  70.7 0.0 copy-done.10
  70.7 0.0 copy-done.11
  70.7 0.0 copy-done.12
  70.7 0.0 copy-start.15
  70.7 1.2 %waves.1.table_ref = bf16[4,512,512]{2,1,0:T(8,128)(2,1)S(1)} custom-call(f32[4,8,512]{2,1,0:T(8,128)S(1)} %copy-done.9, f32[4,8,512]{2,1,0:T(8,128)S(1)} %copy-done.10, f32[8,512]{1,0:T(8,128)S(1)} %copy-done.11, f32[8,512]{1,0:T(8,128)S(1)} %copy-done.12), custom_call_target="tpu_custom_call" | custom-call | tf_op jit(solution)/shard_map/waves/pallas_call | solution.py:701
  71.9 0.0 copy-start.2
  71.9 1.3 %copy-done.2 = bf16[4,512,512]{2,1,0:T(8,128)(2,1)} copy-done((bf16[4,512,512]{2,1,0:T(8,128)(2,1)}, bf16[4,512,512]{2,1,0:T(8,128)(2,1)S(1)}, u32[]{:S(2)}) %copy-start.2) | copy-done | bytes 2097176
  73.3 33.1 %all-to-all-done.1.back_ref = bf16[16,32,1536]{2,1,0:T(8,128)(2,1)S(1)} async-done(((bf16[16,32,1536]{2,1,0:T(8,128)(2,1)}), bf16[16,32,1536]{2,1,0:T(8,128)(2,1)S(1)}, u32[]{:S(2)}, u32[]{:S(2)}) %all-to-all-start.1) | async-done | bytes 1572896 | tf_op jit(solution)/shard_map/all_to_all | solution.py:726
  106.4 0.0 copy-done.6
  106.4 0.0 copy-done.7
  106.4 0.0 copy-done.13
  106.4 9.1 %gather.1 = (bf16[32,3,4,2,2048]{4,3,2,1,0:T(2,128)(2,1)}, bf16[3,64,512]{2,1,0:T(8,128)(2,1)S(1)}) custom-call(s32[64]{0:T(128)S(1)} %copy-done.13, s32[64,512]{1,0:T(8,128)S(1)} %copy-done.6, bf16[512,256]{1,0:T(8,128)(2,1)S(1)} %copy-done.7, bf16[4,512,512]{2,1,0:T(8,128)(2,1)} %copy-done.2, bf16[16,32,1536]{2,1,0:T(8,128)(2,1)S(1)} %all-to-all-done.1.back_ref, ...), custom_call_target="tpu_custom_call" | custom-call | tf_op jit(solution)/shard_map/gather/pallas_call | solution.py:727
  115.5 1.6 %collective-permute-start = (bf16[3,64,512]{2,1,0:T(8,128)(2,1)S(1)}, bf16[3,64,512]{2,1,0:T(8,128)(2,1)S(1)}, u32[]{:S(2)}, u32[]{:S(2)}) collective-permute-start(bf16[3,64,512]{2,1,0:T(8,128)(2,1)S(1)} %get-tuple-element.5), channel_id=1, source_target_pairs={{0,16},{16,0},{1,17},{17,1},{2,18},{18,2},{3,19},{19,3},{4,20},{20... | collective-permute-start | bytes 589832 | tf_op jit(solution)/shard_map/ppermute | solution.py:756
  117.1 0.0 copy-done.15
  117.1 5.0 %collective-permute-done = bf16[3,64,512]{2,1,0:T(8,128)(2,1)S(1)} collective-permute-done((bf16[3,64,512]{2,1,0:T(8,128)(2,1)S(1)}, bf16[3,64,512]{2,1,0:T(8,128)(2,1)S(1)}, u32[]{:S(2)}, u32[]{:S(2)}) %collective-permute-start) | collective-permute-done | bytes 196640 | tf_op jit(solution)/shard_map/ppermute | solution.py:756
  122.1 0.0 copy-done.14
  122.1 0.9 add_subtract_fusion
  (7 shorter events, 0.0 us)
Async XLA Ops:
  0.6 59.9 %copy-start = (f32[512,512]{1,0:T(8,128)S(1)}, f32[512,512]{1,0:T(8,128)}, u32[]{:S(2)}) copy-start(f32[512,512]{1,0:T(8,128)} %param.30) | copy-start | bytes 3145732
  12.1 45.5 %all-to-all-start = ((bf16[16,32,1536]{2,1,0:T(8,128)(2,1)}), bf16[16,32,1536]{2,1,0:T(8,128)(2,1)S(1)}, u32[]{:S(2)}, u32[]{:S(2)}) async-start(bf16[16,32,1536]{2,1,0:T(8,128)(2,1)} %spread.1), calls=%async_computation | async-start | bytes 3145728 | tf_op jit(solution)/shard_map/all_to_all | solution.py:659
  19.6 6.9 %copy-start.8 = (bf16[256,256]{1,0:T(8,128)(2,1)S(1)}, bf16[256,256]{1,0:T(8,128)(2,1)}, u32[]{:S(2)}) copy-start(bf16[256,256]{1,0:T(8,128)(2,1)} %constant.94.clone.order_ref) | copy-start | bytes 393220
  26.5 1.9 %copy-start.1 = (f32[512,1536]{1,0:T(8,128)S(1)}, f32[512,1536]{1,0:T(8,128)}, u32[]{:S(2)}) copy-start(f32[512,1536]{1,0:T(8,128)} %reshape.68.state_ref) | copy-start | bytes 9437188
  28.4 29.2 %copy-start.16 = (f32[512]{0:T(512)S(1)}, f32[512]{0:T(512)}, u32[]{:S(2)}) copy-start(f32[512]{0:T(512)} %param.32) | copy-start | bytes 6148
  34.1 1.7 %copy-start.4 = (f32[512,1536]{1,0:T(8,128)}, f32[512,1536]{1,0:T(8,128)S(1)}, u32[]{:S(2)}) copy-start(f32[512,1536]{1,0:T(8,128)S(1)} %project.1) | copy-start | bytes 9437188
  60.6 7.9 %copy-start.5 = (f32[64,512]{1,0:T(8,128)S(1)}, f32[64,512]{1,0:T(8,128)}, u32[]{:S(2)}) copy-start(f32[64,512]{1,0:T(8,128)} %place_ref.1) | copy-start | bytes 393220
  64.4 6.2 %copy-start.9 = (f32[4,8,512]{2,1,0:T(8,128)S(1)}, f32[4,8,512]{2,1,0:T(8,128)}, u32[]{:S(2)}) copy-start(f32[4,8,512]{2,1,0:T(8,128)} %constant.95.clone.base_cos_ref) | copy-start | bytes 196612
  64.4 6.2 %copy-start.10 = (f32[4,8,512]{2,1,0:T(8,128)S(1)}, f32[4,8,512]{2,1,0:T(8,128)}, u32[]{:S(2)}) copy-start(f32[4,8,512]{2,1,0:T(8,128)} %constant.96.clone.base_sin_ref) | copy-start | bytes 196612
  64.4 6.3 %copy-start.11 = (f32[8,512]{1,0:T(8,128)S(1)}, f32[8,512]{1,0:T(8,128)}, u32[]{:S(2)}) copy-start(f32[8,512]{1,0:T(8,128)} %constant.97.clone.step_cos_ref) | copy-start | bytes 49156
  64.4 6.3 %copy-start.12 = (f32[8,512]{1,0:T(8,128)S(1)}, f32[8,512]{1,0:T(8,128)}, u32[]{:S(2)}) copy-start(f32[8,512]{1,0:T(8,128)} %constant.98.clone.step_sin_ref) | copy-start | bytes 49156
  64.4 42.0 %copy-start.6 = (s32[64,512]{1,0:T(8,128)S(1)}, s32[64,512]{1,0:T(8,128)}, u32[]{:S(2)}) copy-start(s32[64,512]{1,0:T(8,128)} %cell_ref.1) | copy-start | bytes 393220
  64.4 42.0 %copy-start.7 = (bf16[512,256]{1,0:T(8,128)(2,1)S(1)}, bf16[512,256]{1,0:T(8,128)(2,1)}, u32[]{:S(2)}) copy-start(bf16[512,256]{1,0:T(8,128)(2,1)} %constant.99.clone.order_ref) | copy-start | bytes 786436
  64.4 41.9 %copy-start.13 = (s32[64]{0:T(128)S(1)}, s32[64]{0:T(128)}, u32[]{:S(2)}) copy-start(s32[64]{0:T(128)} %block_ref.3) | copy-start | bytes 772
  64.5 41.9 %all-to-all-start.1 = ((bf16[16,32,1536]{2,1,0:T(8,128)(2,1)}), bf16[16,32,1536]{2,1,0:T(8,128)(2,1)S(1)}, u32[]{:S(2)}, u32[]{:S(2)}) async-start(bf16[16,32,1536]{2,1,0:T(8,128)(2,1)} %bitcast.17), calls=%async_computation.1 | async-start | bytes 3145728 | tf_op jit(solution)/shard_map/all_to_all | solution.py:726
  69.7 1.0 copy-start.3
  70.7 46.4 %copy-start.15 = (f32[64,512]{1,0:T(8,128)S(1)}, f32[64,512]{1,0:T(8,128)}, u32[]{:S(2)}) copy-start(f32[64,512]{1,0:T(8,128)} %rate_in.1) | copy-start | bytes 393220
  71.9 1.3 %copy-start.2 = (bf16[4,512,512]{2,1,0:T(8,128)(2,1)}, bf16[4,512,512]{2,1,0:T(8,128)(2,1)S(1)}, u32[]{:S(2)}) copy-start(bf16[4,512,512]{2,1,0:T(8,128)(2,1)S(1)} %waves.1.table_ref) | copy-start | bytes 6291460
  73.2 48.9 %copy-start.14 = (f32[3,64,512]{2,1,0:T(8,128)S(1)}, f32[3,64,512]{2,1,0:T(8,128)}, u32[]{:S(2)}) copy-start(f32[3,64,512]{2,1,0:T(8,128)} %motion_in.1) | copy-start | bytes 1179652
  115.5 6.6 %collective-permute-start = (bf16[3,64,512]{2,1,0:T(8,128)(2,1)S(1)}, bf16[3,64,512]{2,1,0:T(8,128)(2,1)S(1)}, u32[]{:S(2)}, u32[]{:S(2)}) collective-permute-start(bf16[3,64,512]{2,1,0:T(8,128)(2,1)S(1)} %get-tuple-element.5), channel_id=1, source_target_pairs={{0,16},{16,0},{1,17},{17,1},{2,18},{18,2},{3,19},{19,3},{4,20},{20... | collective-permute-start | bytes 589832 | tf_op jit(solution)/shard_map/ppermute | solution.py:756

commit v6 on v5

--- a/solution.py
+++ b/solution.py
@@ -15,7 +15,7 @@
 SPLIT = 4
 POINTS = NX // SPLIT
 WAVES = KX // SPLIT
-TILE_GROUP = 8
+TILE_GROUP = 16
 
 time_step = 0.5
 gravity = 0.8

time: 123 us -> 123 us (level)
  no operation moved by 1% of the time
where the time goes in v6:
time: 123 us
  waiting for transfers between devices  60 us (49%)
  Pallas kernels  28.2 us (23%)
  starting transfers between devices  13 us (11%)
  local copies, waits for them, and re-layouts  11.4 us (9%)
  matrix products  6.75 us (5%)
  other arithmetic  2.3 us (2%)
    all_to_all x1, waiting for transfers between devices, on_device(): lax.all_to_all(solved, ('px', 'pz'), split_axis=0, concat_axis=0, tiled=T...  33.1 us
    all_to_all x1, waiting for transfers between devices, on_device(): lax.all_to_all(outgoing, ('px', 'pz'), split_axis=0, concat_axis=0, tiled...  21.9 us
    pallas_call x1, Pallas kernels, on_device(): pl.pallas_call(functools.partial(spread_kernel, **sizes), out_shape=jax.S...  10.9 us
    pallas_call x1, Pallas kernels, on_device(): pl.pallas_call(functools.partial(gather_kernel, **sizes), out_shape=(jax....  9.14 us
    all_to_all x1, starting transfers between devices, on_device(): lax.all_to_all(outgoing, ('px', 'pz'), split_axis=0, concat_axis=0, tiled...  7.43 us
    unnamed x34, local copies, waits for them, and re-layouts  5.91 us
    pallas_call x1, Pallas kernels, on_device(): pl.pallas_call(project_kernel, grid=(columns // pencil_waves,), out_shape...  5.69 us
    reshape x1, local copies, waits for them, and re-layouts, on_device(): state = fluid_velocity.transpose(0, 1, 2, 3, 4).reshape(rows, columns)  5.5 us
  transfers between devices with their start and end apart: 3, of which 3 were waited for; matrix products, arithmetic and copies ran while one was open for 6% of the time, Pallas kernels for 7%

profile of v6, /device:TPU:0, one launch (start us, length us, event | category | flops | bytes accessed | tf_op | source)
XLA Modules:
  0.0 122.5 jit_solution(10055100381651569344)
XLA Ops:
  0.6 0.0 copy-start
  0.7 10.9 %spread.1 = bf16[16,32,1536]{2,1,0:T(8,128)(2,1)} custom-call(s32[64]{0:T(128)} %block_ref.3, s32[1]{0:T(128)} %bitcast.group_ref, s32[64,512]{1,0:T(8,128)} %cell_ref.1, f32[64,512]{1,0:T(8,128)} %volume_in.1, f32[64,512]{1,0:T(8,128)} %rate_in.1, f32[64,512]{1,0:T(8,128)} %place_ref.1, f32[3,64,512]{2,1,0:T(8,128)} %motion_in.1, f32[3,64,512]{2,1,0:T(8,128)} %seen_in.1, ...), custom_call_target="tpu_custom_call" | custom-call | tf_op jit(solution)/shard_map/spread/pallas_call | solution.py:627
  11.6 7.4 %all-to-all-start = ((bf16[16,32,1536]{2,1,0:T(8,128)(2,1)}), bf16[16,32,1536]{2,1,0:T(8,128)(2,1)S(1)}, u32[]{:S(2)}, u32[]{:S(2)}) async-start(bf16[16,32,1536]{2,1,0:T(8,128)(2,1)} %spread.1), calls=%async_computation | async-start | bytes 3145728 | tf_op jit(solution)/shard_map/all_to_all | solution.py:659
  19.1 0.0 copy-start.8
  19.1 5.5 %reshape.68.state_ref = f32[512,1536]{1,0:T(8,128)} reshape(f32[512,3,1,2,256]{4,3,2,1,0:T(2,128)} %param.29) | data formatting | bytes 6291456 | tf_op jit(solution)/shard_map/reshape | solution.py:667
  24.6 1.4 %fusion.3 = (bf16[512,512]{1,0:T(8,128)(2,1)S(1)}, bf16[512,512]{1,0:T(8,128)(2,1)S(1)}) fusion(f32[512,512]{1,0:T(8,128)} %param.31), kind=kLoop, calls=%fused_computation.7 | loop fusion | flops 1048576 | bytes 2097152 | tf_op jit(solution)/shard_map/convert_element_type | solution.py:663
  26.0 0.0 copy-done.8
  26.0 0.0 copy-start.1
  26.0 1.9 %copy-done.1 = f32[512,1536]{1,0:T(8,128)S(1)} copy-done((f32[512,1536]{1,0:T(8,128)S(1)}, f32[512,1536]{1,0:T(8,128)}, u32[]{:S(2)}) %copy-start.1) | copy-done | bytes 3145752
  27.9 0.0 copy-start.16
  27.9 5.7 %project.1 = f32[512,1536]{1,0:T(8,128)S(1)} custom-call(bf16[512,512]{1,0:T(8,128)(2,1)S(1)} %get-tuple-element.7.high_ref, bf16[512,512]{1,0:T(8,128)(2,1)S(1)} %get-tuple-element.6.low_ref, bf16[256,256]{1,0:T(8,128)(2,1)S(1)} %copy-done.8, f32[512,1536]{1,0:T(8,128)S(1)} %copy-done.1), custom_call_target="tpu_custom_call" | custom-call | tf_op jit(solution)/shard_map/project/pallas_call | solution.py:670
  33.6 0.0 copy-start.4
  33.6 1.7 %copy-done.4 = f32[512,1536]{1,0:T(8,128)} copy-done((f32[512,1536]{1,0:T(8,128)}, f32[512,1536]{1,0:T(8,128)S(1)}, u32[]{:S(2)}) %copy-start.4) | copy-done | bytes 3145752
  35.3 21.9 %all-to-all-done = bf16[16,32,1536]{2,1,0:T(8,128)(2,1)S(1)} async-done(((bf16[16,32,1536]{2,1,0:T(8,128)(2,1)}), bf16[16,32,1536]{2,1,0:T(8,128)(2,1)S(1)}, u32[]{:S(2)}, u32[]{:S(2)}) %all-to-all-start) | async-done | bytes 1572896 | tf_op jit(solution)/shard_map/all_to_all | solution.py:659
  57.1 0.0 copy-done.16
  57.1 2.9 %fusion.2 = f32[512,1536]{1,0:T(8,128)S(1)} fusion(f32[512,1536]{1,0:T(8,128)} %copy-done.4, bf16[512,512]{1,0:T(8,128)(2,1)S(1)} %get-tuple-element.7.high_ref, bf16[512,1536]{1,0:T(8,128)(2,1)S(1)} %bitcast.18, f32[1536]{0:T(1024)S(1)} %add.101, f32[512]{0:T(512)S(1)} %copy-done.16), kind=kOutput, calls=%fused_computation.3 | convolution fusion | flops 810811392 | bytes 8396800 | tf_op jit(solution)/shard_map/dot_general | solution.py:720
  60.1 0.0 copy-done
  60.1 0.0 copy-start.5
  60.1 3.8 %convolution_convert_fusion = bf16[1536,512]{0,1:T(8,128)(2,1)} fusion(f32[512,1536]{1,0:T(8,128)S(1)} %fusion.2, f32[512,512]{1,0:T(8,128)S(1)} %copy-done), kind=kOutput, calls=%fused_computation.4 | convolution fusion | flops 2416705536 | bytes 5767168 | tf_op jit(solution)/shard_map/dot_general | solution.py:724
  63.9 0.0 copy-start.9
  63.9 0.0 copy-start.10
  63.9 0.0 copy-start.11
  63.9 0.0 copy-start.6
  63.9 0.0 copy-start.7
  63.9 0.0 copy-start.13
  63.9 4.0 %all-to-all-start.1 = ((bf16[16,32,1536]{2,1,0:T(8,128)(2,1)}), bf16[16,32,1536]{2,1,0:T(8,128)(2,1)S(1)}, u32[]{:S(2)}, u32[]{:S(2)}) async-start(bf16[16,32,1536]{2,1,0:T(8,128)(2,1)} %bitcast.17), calls=%async_computation.1 | async-start | bytes 3145728 | tf_op jit(solution)/shard_map/all_to_all | solution.py:726
  68.0 0.0 copy-done.5
  68.0 1.2 phases.1.phase_ref
  69.2 0.0 copy-start.3
  69.2 1.0 copy-done.3
  70.1 0.0 copy-done.9
  70.1 0.0 copy-done.10
  70.2 0.0 copy-done.11
  70.2 0.0 copy-done.12
  70.2 0.0 copy-start.15
  70.2 1.2 %waves.1.table_ref = bf16[4,512,512]{2,1,0:T(8,128)(2,1)S(1)} custom-call(f32[4,8,512]{2,1,0:T(8,128)S(1)} %copy-done.9, f32[4,8,512]{2,1,0:T(8,128)S(1)} %copy-done.10, f32[8,512]{1,0:T(8,128)S(1)} %copy-done.11, f32[8,512]{1,0:T(8,128)S(1)} %copy-done.12), custom_call_target="tpu_custom_call" | custom-call | tf_op jit(solution)/shard_map/waves/pallas_call | solution.py:701
  71.4 0.0 copy-start.2
  71.4 1.3 %copy-done.2 = bf16[4,512,512]{2,1,0:T(8,128)(2,1)} copy-done((bf16[4,512,512]{2,1,0:T(8,128)(2,1)}, bf16[4,512,512]{2,1,0:T(8,128)(2,1)S(1)}, u32[]{:S(2)}) %copy-start.2) | copy-done | bytes 2097176
  72.8 33.1 %all-to-all-done.1.back_ref = bf16[16,32,1536]{2,1,0:T(8,128)(2,1)S(1)} async-done(((bf16[16,32,1536]{2,1,0:T(8,128)(2,1)}), bf16[16,32,1536]{2,1,0:T(8,128)(2,1)S(1)}, u32[]{:S(2)}, u32[]{:S(2)}) %all-to-all-start.1) | async-done | bytes 1572896 | tf_op jit(solution)/shard_map/all_to_all | solution.py:726
  105.9 0.0 copy-done.6
  105.9 0.0 copy-done.7
  105.9 0.0 copy-done.13
  105.9 9.1 %gather.1 = (bf16[32,3,4,2,2048]{4,3,2,1,0:T(2,128)(2,1)}, bf16[3,64,512]{2,1,0:T(8,128)(2,1)S(1)}) custom-call(s32[64]{0:T(128)S(1)} %copy-done.13, s32[64,512]{1,0:T(8,128)S(1)} %copy-done.6, bf16[512,256]{1,0:T(8,128)(2,1)S(1)} %copy-done.7, bf16[4,512,512]{2,1,0:T(8,128)(2,1)} %copy-done.2, bf16[16,32,1536]{2,1,0:T(8,128)(2,1)S(1)} %all-to-all-done.1.back_ref, ...), custom_call_target="tpu_custom_call" | custom-call | tf_op jit(solution)/shard_map/gather/pallas_call | solution.py:727
  115.0 1.6 %collective-permute-start = (bf16[3,64,512]{2,1,0:T(8,128)(2,1)S(1)}, bf16[3,64,512]{2,1,0:T(8,128)(2,1)S(1)}, u32[]{:S(2)}, u32[]{:S(2)}) collective-permute-start(bf16[3,64,512]{2,1,0:T(8,128)(2,1)S(1)} %get-tuple-element.5), channel_id=1, source_target_pairs={{0,16},{16,0},{1,17},{17,1},{2,18},{18,2},{3,19},{19,3},{4,20},{20... | collective-permute-start | bytes 589832 | tf_op jit(solution)/shard_map/ppermute | solution.py:756
  116.6 0.0 copy-done.15
  116.6 5.0 %collective-permute-done = bf16[3,64,512]{2,1,0:T(8,128)(2,1)S(1)} collective-permute-done((bf16[3,64,512]{2,1,0:T(8,128)(2,1)S(1)}, bf16[3,64,512]{2,1,0:T(8,128)(2,1)S(1)}, u32[]{:S(2)}, u32[]{:S(2)}) %collective-permute-start) | collective-permute-done | bytes 196640 | tf_op jit(solution)/shard_map/ppermute | solution.py:756
  121.6 0.0 copy-done.14
  121.6 0.9 add_subtract_fusion
  (7 shorter events, 0.0 us)
Async XLA Ops:
  0.6 59.4 %copy-start = (f32[512,512]{1,0:T(8,128)S(1)}, f32[512,512]{1,0:T(8,128)}, u32[]{:S(2)}) copy-start(f32[512,512]{1,0:T(8,128)} %param.30) | copy-start | bytes 3145732
  11.6 45.5 %all-to-all-start = ((bf16[16,32,1536]{2,1,0:T(8,128)(2,1)}), bf16[16,32,1536]{2,1,0:T(8,128)(2,1)S(1)}, u32[]{:S(2)}, u32[]{:S(2)}) async-start(bf16[16,32,1536]{2,1,0:T(8,128)(2,1)} %spread.1), calls=%async_computation | async-start | bytes 3145728 | tf_op jit(solution)/shard_map/all_to_all | solution.py:659
  19.1 6.9 %copy-start.8 = (bf16[256,256]{1,0:T(8,128)(2,1)S(1)}, bf16[256,256]{1,0:T(8,128)(2,1)}, u32[]{:S(2)}) copy-start(bf16[256,256]{1,0:T(8,128)(2,1)} %constant.94.clone.order_ref) | copy-start | bytes 393220
  26.0 1.9 %copy-start.1 = (f32[512,1536]{1,0:T(8,128)S(1)}, f32[512,1536]{1,0:T(8,128)}, u32[]{:S(2)}) copy-start(f32[512,1536]{1,0:T(8,128)} %reshape.68.state_ref) | copy-start | bytes 9437188
  27.9 29.2 %copy-start.16 = (f32[512]{0:T(512)S(1)}, f32[512]{0:T(512)}, u32[]{:S(2)}) copy-start(f32[512]{0:T(512)} %param.32) | copy-start | bytes 6148
  33.6 1.7 %copy-start.4 = (f32[512,1536]{1,0:T(8,128)}, f32[512,1536]{1,0:T(8,128)S(1)}, u32[]{:S(2)}) copy-start(f32[512,1536]{1,0:T(8,128)S(1)} %project.1) | copy-start | bytes 9437188
  60.1 7.9 %copy-start.5 = (f32[64,512]{1,0:T(8,128)S(1)}, f32[64,512]{1,0:T(8,128)}, u32[]{:S(2)}) copy-start(f32[64,512]{1,0:T(8,128)} %place_ref.1) | copy-start | bytes 393220
  63.9 6.2 %copy-start.9 = (f32[4,8,512]{2,1,0:T(8,128)S(1)}, f32[4,8,512]{2,1,0:T(8,128)}, u32[]{:S(2)}) copy-start(f32[4,8,512]{2,1,0:T(8,128)} %constant.95.clone.base_cos_ref) | copy-start | bytes 196612
  63.9 6.2 %copy-start.10 = (f32[4,8,512]{2,1,0:T(8,128)S(1)}, f32[4,8,512]{2,1,0:T(8,128)}, u32[]{:S(2)}) copy-start(f32[4,8,512]{2,1,0:T(8,128)} %constant.96.clone.base_sin_ref) | copy-start | bytes 196612
  63.9 6.3 %copy-start.11 = (f32[8,512]{1,0:T(8,128)S(1)}, f32[8,512]{1,0:T(8,128)}, u32[]{:S(2)}) copy-start(f32[8,512]{1,0:T(8,128)} %constant.97.clone.step_cos_ref) | copy-start | bytes 49156
  63.9 6.3 %copy-start.12 = (f32[8,512]{1,0:T(8,128)S(1)}, f32[8,512]{1,0:T(8,128)}, u32[]{:S(2)}) copy-start(f32[8,512]{1,0:T(8,128)} %constant.98.clone.step_sin_ref) | copy-start | bytes 49156
  63.9 42.0 %copy-start.6 = (s32[64,512]{1,0:T(8,128)S(1)}, s32[64,512]{1,0:T(8,128)}, u32[]{:S(2)}) copy-start(s32[64,512]{1,0:T(8,128)} %cell_ref.1) | copy-start | bytes 393220
  63.9 42.0 %copy-start.7 = (bf16[512,256]{1,0:T(8,128)(2,1)S(1)}, bf16[512,256]{1,0:T(8,128)(2,1)}, u32[]{:S(2)}) copy-start(bf16[512,256]{1,0:T(8,128)(2,1)} %constant.99.clone.order_ref) | copy-start | bytes 786436
  63.9 41.9 %copy-start.13 = (s32[64]{0:T(128)S(1)}, s32[64]{0:T(128)}, u32[]{:S(2)}) copy-start(s32[64]{0:T(128)} %block_ref.3) | copy-start | bytes 772
  63.9 41.9 %all-to-all-start.1 = ((bf16[16,32,1536]{2,1,0:T(8,128)(2,1)}), bf16[16,32,1536]{2,1,0:T(8,128)(2,1)S(1)}, u32[]{:S(2)}, u32[]{:S(2)}) async-start(bf16[16,32,1536]{2,1,0:T(8,128)(2,1)} %bitcast.17), calls=%async_computation.1 | async-start | bytes 3145728 | tf_op jit(solution)/shard_map/all_to_all | solution.py:726
  69.2 1.0 copy-start.3
  70.2 46.4 %copy-start.15 = (f32[64,512]{1,0:T(8,128)S(1)}, f32[64,512]{1,0:T(8,128)}, u32[]{:S(2)}) copy-start(f32[64,512]{1,0:T(8,128)} %rate_in.1) | copy-start | bytes 393220
  71.4 1.3 %copy-start.2 = (bf16[4,512,512]{2,1,0:T(8,128)(2,1)}, bf16[4,512,512]{2,1,0:T(8,128)(2,1)S(1)}, u32[]{:S(2)}) copy-start(bf16[4,512,512]{2,1,0:T(8,128)(2,1)S(1)} %waves.1.table_ref) | copy-start | bytes 6291460
  72.7 48.9 %copy-start.14 = (f32[3,64,512]{2,1,0:T(8,128)S(1)}, f32[3,64,512]{2,1,0:T(8,128)}, u32[]{:S(2)}) copy-start(f32[3,64,512]{2,1,0:T(8,128)} %motion_in.1) | copy-start | bytes 1179652
  115.0 6.6 %collective-permute-start = (bf16[3,64,512]{2,1,0:T(8,128)(2,1)S(1)}, bf16[3,64,512]{2,1,0:T(8,128)(2,1)S(1)}, u32[]{:S(2)}, u32[]{:S(2)}) collective-permute-start(bf16[3,64,512]{2,1,0:T(8,128)(2,1)S(1)} %get-tuple-element.5), channel_id=1, source_target_pairs={{0,16},{16,0},{1,17},{17,1},{2,18},{18,2},{3,19},{19,3},{4,20},{20... | collective-permute-start | bytes 589832 | tf_op jit(solution)/shard_map/ppermute | solution.py:756
